TPU v7x, 128 devices: a whole 4x4x4 slice. The times are simulated.
128 devices in a mesh: seq: 8 (over y, core), exp: 16 (over z, x).
Axes of the slice: x: 4, y: 4, z: 4, core: 2. Of those that a mesh axis runs over, the one named last changes fastest.
Arguments:
- frames: bfloat16 [16, 1024, 1024], P('exp', 'seq'), may hold values from -6 to 6
- conv_kernel: float32 [31, 1024], replicated, may hold values from -1 to 1
- routes: int32 [16, 1024, 2], P('exp', 'seq'), may hold values from 0 to 63, all different within a row; in each aligned block of 128 rows (0 to 127, 128 to 255, ..., all dimensions but the last counted through in order) at most 8 rows name the same one
- gates: float32 [16, 1024, 2], P('exp', 'seq'), may hold values from 0.25 to 1
- w_in: bfloat16 [64, 1024, 2048], P('exp', None, 'seq'), may hold values from -0.1875 to 0.1875
- w_out: bfloat16 [64, 2048, 1024], P('exp', 'seq'), may hold values from -0.125 to 0.125
- cotangent: bfloat16 [16, 1024, 1024], P('exp', 'seq'), may hold values from -1.5 to 1.5
Outputs:
- mixed: bfloat16 [16, 1024, 1024], P('exp', 'seq')
- frames_grad: bfloat16 [16, 1024, 1024], P('exp', 'seq')
- w_in_grad: float32 [64, 1024, 2048], P('exp', None, 'seq')
- w_out_grad: float32 [64, 2048, 1024], P('exp', 'seq')
Inputs may be any that keep to these rules, and one draw needn't show every extreme that they name: `routes`: each frame names two different experts. Within each aligned block of 128 frames of a recording no expert is named more than 8 times, and in every draw some expert is named exactly 8 times within some block.
All inputs are finite; a program needn't handle non-finite values.
Results may differ from a plain program's by a relative error of at most 0.012.
Values may be sent and summed in bfloat16 or wider, within the bound.
No kernel may reach another device: no remote copies, remote signals or barrier semaphores. Data moves between devices by JAX's collectives and lax.ppermute only.
A program may use at most 192 MiB of HBM per device.

v0:
```python
import jax
import jax.numpy as jnp
from jax import lax
from jax.sharding import PartitionSpec as P

KERNEL = 31
CAP = 8


def extended(block, sides, width):
    for axis, dim in sides:
        count = lax.axis_size(axis)
        forward = [(i, i + 1) for i in range(count - 1)]
        backward = [(target, source) for source, target in forward]
        low = lax.ppermute(
            lax.slice_in_dim(block, block.shape[dim] - width, None, axis=dim), axis, forward
        )
        high = lax.ppermute(lax.slice_in_dim(block, 0, width, axis=dim), axis, backward)
        block = jnp.concatenate([low, block, high], axis=dim)
    return block


def silu_slope(values):
    logistic = jax.nn.sigmoid(values)
    return logistic * (1.0 + values * (1.0 - logistic))


def edge_rows(field):
    return extended(field, (("seq", 1),), (KERNEL - 1) // 2)


def local_conv(padded, kernel, reverse, length):
    margin = (KERNEL - 1) // 2
    summed = jnp.zeros((padded.shape[0], length, padded.shape[2]), jnp.float32)
    for tap_index in range(KERNEL):
        offset = 2 * margin - tap_index if reverse else tap_index
        summed = summed + kernel[tap_index] * padded[:, offset : offset + length, :]
    return summed


def to_sources(term_fn, groups, n_seq, n_exp, per_dest, model_width):
    whole_term = term_fn(0, groups).astype(jnp.bfloat16).reshape(groups, per_dest, model_width)
    arrived = lax.all_to_all(whole_term, ("seq", "exp"), split_axis=0, concat_axis=0, tiled=True)
    summed = jnp.sum(
        arrived.reshape(n_seq, n_exp, per_dest, model_width).astype(jnp.float32), axis=0
    ).astype(jnp.bfloat16)
    return summed.reshape(n_exp * per_dest, model_width)


def per_device(frames, conv_kernel, routes, gates, w_in, w_out, cotangent):
    n_seq = lax.axis_size("seq")
    n_exp = lax.axis_size("exp")
    local_experts = w_in.shape[0]
    all_experts = local_experts * n_exp
    length = frames.shape[1]
    model_width = frames.shape[2]
    groups = n_seq * n_exp
    per_dest = local_experts * CAP
    mixing = local_conv(edge_rows(frames).astype(jnp.float32), conv_kernel, False, length)
    hidden = (frames.astype(jnp.float32) + jax.nn.silu(mixing)).astype(jnp.bfloat16)
    flat_hidden = hidden[0]
    expert_ids = routes[0].reshape(2 * length)
    onehot = (expert_ids[:, None] == jnp.arange(all_experts, dtype=jnp.int32)[None, :]).astype(
        jnp.int32
    )
    slot_rank = jnp.sum((jnp.cumsum(onehot, axis=0) - onehot) * onehot, axis=1)
    places = expert_ids * CAP + slot_rank
    gate_pair = gates[0]
    up_rows = jnp.repeat(flat_hidden, 2, axis=0)
    down_rows = (
        gate_pair.reshape(2 * length, 1) * jnp.repeat(cotangent[0].astype(jnp.float32), 2, axis=0)
    ).astype(jnp.bfloat16)
    blank_slots = jnp.zeros((all_experts * CAP, model_width), jnp.bfloat16)
    send_up = blank_slots.at[places].set(up_rows).reshape(n_exp, per_dest, model_width)
    send_down = blank_slots.at[places].set(down_rows).reshape(n_exp, per_dest, model_width)
    wide_up = jnp.broadcast_to(send_up[None], (n_seq, n_exp, per_dest, model_width)).reshape(
        groups, per_dest, model_width
    )
    wide_down = jnp.broadcast_to(send_down[None], (n_seq, n_exp, per_dest, model_width)).reshape(
        groups, per_dest, model_width
    )
    got_up, got_down = (
        lax.all_to_all(wide_up, ("seq", "exp"), split_axis=0, concat_axis=0, tiled=True),
        lax.all_to_all(wide_down, ("seq", "exp"), split_axis=0, concat_axis=0, tiled=True),
    )
    routed_up = got_up.reshape(groups, local_experts, CAP, model_width)
    routed_down = got_down.reshape(groups, local_experts, CAP, model_width)
    pre_act = jnp.einsum("gecd,edh->gech", routed_up, w_in, preferred_element_type=jnp.float32)
    activation = jax.nn.silu(pre_act).astype(jnp.bfloat16)

    def forward_term(offset, row_count):
        return jnp.einsum("gech,ehd->gecd", activation, w_out, preferred_element_type=jnp.float32)

    expert_out = to_sources(forward_term, groups, n_seq, n_exp, per_dest, model_width)
    picked = expert_out[places].reshape(length, 2, model_width).astype(jnp.float32)
    mixed = (
        flat_hidden.astype(jnp.float32) + jnp.sum(gate_pair[:, :, None] * picked, axis=1)
    ).astype(jnp.bfloat16)
    act_grad = jnp.einsum("gecd,ehd->gech", routed_down, w_out, preferred_element_type=jnp.float32)
    pre_grad = (act_grad * silu_slope(pre_act)).astype(jnp.bfloat16)
    w_out_grad = jnp.einsum(
        "gech,gecd->ehd", activation, routed_down, preferred_element_type=jnp.float32
    )
    w_in_grad = jnp.einsum(
        "gecd,gech->edh", routed_up, pre_grad, preferred_element_type=jnp.float32
    )

    def backward_term(offset, row_count):
        return jnp.einsum("gech,edh->gecd", pre_grad, w_in, preferred_element_type=jnp.float32)

    input_grad = to_sources(backward_term, groups, n_seq, n_exp, per_dest, model_width)
    back_rows = input_grad[places].reshape(length, 2, model_width).astype(jnp.float32)
    hidden_grad = cotangent[0].astype(jnp.float32) + jnp.sum(back_rows, axis=1)
    conv_back = (hidden_grad * silu_slope(mixing[0])).astype(jnp.bfloat16)
    spread = local_conv(edge_rows(conv_back[None]).astype(jnp.float32), conv_kernel, True, length)
    frames_grad = (hidden_grad + spread[0]).astype(jnp.bfloat16)
    return (mixed[None], frames_grad[None], w_in_grad, w_out_grad)


def solution(mesh):
    in_specs = (
        P("exp", "seq", None),
        P(),
        P("exp", "seq", None),
        P("exp", "seq", None),
        P("exp", None, "seq"),
        P("exp", "seq", None),
        P("exp", "seq", None),
    )
    out_specs = (
        P("exp", "seq", None),
        P("exp", "seq", None),
        P("exp", None, "seq"),
        P("exp", "seq", None),
    )
    return jax.shard_map(
        per_device, mesh=mesh, in_specs=in_specs, out_specs=out_specs, check_vma=False
    )
```

profile of v0, /device:TPU:5, one launch (start us, length us, event | category | flops | bytes accessed | tf_op | source)
XLA Modules:
  0.0 533.2 jit_solution(14637964337151677861)
XLA Ops:
  1.6 3.8 collective-permute-start
  5.4 1.9 collective-permute-start.1
  14.1 3.8 add_convert_fusion
  19.4 2.6 scatter_custom_fusion
  22.0 5.5 %broadcast_in_dim.34 = bf16[8,16,32,1024]{3,2,1,0:T(8,128)(2,1)} broadcast(bf16[16,32,1024]{2,1,0:T(8,128)(2,1)} %bitcast.148), dimensions={1,2,3} | broadcast | bytes 9437184 | tf_op jit(solution)/shard_map/broadcast_in_dim | solution.py:76
  27.6 11.2 %all-to-all-start = ((bf16[128,32,1024]{2,1,0:T(8,128)(2,1)}), bf16[128,32,1024]{2,1,0:T(8,128)(2,1)}, u32[]{:S(2)}, u32[]{:S(2)}) async-start(bf16[128,32,1024]{2,1,0:T(8,128)(2,1)} %bitcast.139), calls=%async_computation | async-start | bytes 16777216 | tf_op jit(solution)/shard_map/all_to_all | solution.py:83
  40.4 2.9 reshape.284
  43.3 3.4 scatter_custom_fusion.1
  46.7 100.5 %all-to-all-done = bf16[128,32,1024]{2,1,0:T(8,128)(2,1)} async-done(((bf16[128,32,1024]{2,1,0:T(8,128)(2,1)}), bf16[128,32,1024]{2,1,0:T(8,128)(2,1)}, u32[]{:S(2)}, u32[]{:S(2)}) %all-to-all-start) | async-done | bytes 8388640 | tf_op jit(solution)/shard_map/all_to_all | solution.py:83
  147.2 5.5 %broadcast_in_dim.37 = bf16[8,16,32,1024]{3,2,1,0:T(8,128)(2,1)} broadcast(bf16[16,32,1024]{2,1,0:T(8,128)(2,1)} %bitcast.147), dimensions={1,2,3} | broadcast | bytes 9437184 | tf_op jit(solution)/shard_map/broadcast_in_dim | solution.py:79
  152.7 10.7 %all-to-all-start.2 = ((bf16[128,32,1024]{2,1,0:T(8,128)(2,1)}), bf16[128,32,1024]{2,1,0:T(8,128)(2,1)}, u32[]{:S(2)}, u32[]{:S(2)}) async-start(bf16[128,32,1024]{2,1,0:T(8,128)(2,1)} %bitcast.140), calls=%async_computation.2 | async-start | bytes 16777216 | tf_op jit(solution)/shard_map/all_to_all | solution.py:84
  163.5 11.5 %copy.29 = bf16[128,32,1024]{2,0,1:T(8,128)(2,1)} copy(bf16[128,32,1024]{2,1,0:T(8,128)(2,1)} %all-to-all-done) | data formatting | bytes 16777216 | tf_op jit(solution)/shard_map/all_to_all | solution.py:83
  175.0 5.7 %fusion.13 = f32[4,128,8,256]{3,1,2,0:T(8,128)S(1)} fusion(bf16[128,4,8,1024]{3,0,2,1:T(8,128)(2,1)} %bitcast.138, bf16[4,1024,256]{2,1,0:T(8,128)(2,1)S(1)} %copy-done.2), kind=kOutput, calls=%fused_computation.22 | convolution fusion | flops 2147483648 | bytes 14680064 | tf_op jit(solution)/shard_map/gecd,edh->gech/dot_general | solution.py:88
  180.7 5.7 %convolution_convert_fusion.1 = bf16[4,128,8,1024]{3,1,2,0:T(8,128)(2,1)} fusion(bf16[4,256,1024]{2,1,0:T(8,128)(2,1)S(1)} %copy-done, f32[4,128,8,256]{3,1,2,0:T(8,128)S(1)} %fusion.13), kind=kOutput, calls=%fused_computation.7 | convolution fusion | flops 2156920832 | bytes 14680064 | tf_op jit(solution)/shard_map/gech,ehd->gecd/dot_general | solution.py:92
  186.4 11.5 %copy.30 = bf16[128,32,1024]{2,1,0:T(8,128)(2,1)} copy(bf16[128,32,1024]{2,0,1:T(8,128)(2,1)} %bitcast.146) | data formatting | bytes 16777216 | tf_op jit(solution)/shard_map/reshape | solution.py:42
  197.9 73.6 %all-to-all-done.2 = bf16[128,32,1024]{2,1,0:T(8,128)(2,1)} async-done(((bf16[128,32,1024]{2,1,0:T(8,128)(2,1)}), bf16[128,32,1024]{2,1,0:T(8,128)(2,1)}, u32[]{:S(2)}, u32[]{:S(2)}) %all-to-all-start.2) | async-done | bytes 8388640 | tf_op jit(solution)/shard_map/all_to_all | solution.py:84
  271.5 10.3 %all-to-all-start.1 = ((bf16[128,32,1024]{2,1,0:T(8,128)(2,1)}), bf16[128,32,1024]{2,1,0:T(8,128)(2,1)}, u32[]{:S(2)}, u32[]{:S(2)}) async-start(bf16[128,32,1024]{2,1,0:T(8,128)(2,1)} %copy.30), calls=%async_computation.1 | async-start | bytes 16777216 | tf_op jit(solution)/shard_map/all_to_all | solution.py:43
  281.8 11.3 %copy.34 = bf16[128,32,1024]{2,0,1:T(8,128)(2,1)} copy(bf16[128,32,1024]{2,1,0:T(8,128)(2,1)} %all-to-all-done.2) | data formatting | bytes 16777216 | tf_op jit(solution)/shard_map/all_to_all | solution.py:84
  293.1 8.0 %fusion.2 = bf16[128,4,8,256]{3,0,2,1:T(8,128)(2,1)S(1)} fusion(f32[4,128,8,256]{3,1,2,0:T(8,128)} %copy-done.4, bf16[128,4,8,1024]{3,0,2,1:T(8,128)(2,1)} %bitcast.144, bf16[4,256,1024]{2,1,0:T(8,128)(2,1)S(1)} %copy-done), kind=kOutput, calls=%fused_computation.9 | convolution fusion | flops 2156920832 | bytes 16777216 | tf_op jit(solution)/shard_map/gecd,ehd->gech/dot_general | solution.py:99
  301.2 5.6 %convolution_convert_fusion = bf16[4,128,8,1024]{3,1,2,0:T(8,128)(2,1)} fusion(bf16[128,4,8,256]{3,0,2,1:T(8,128)(2,1)S(1)} %fusion.2, bf16[4,1024,256]{2,1,0:T(8,128)(2,1)S(1)} %copy-done.3), kind=kOutput, calls=%fused_computation.6 | convolution fusion | flops 2151677952 | bytes 12582912 | tf_op jit(solution)/shard_map/gech,edh->gecd/dot_general | solution.py:109
  306.8 11.8 %copy.35 = bf16[128,32,1024]{2,1,0:T(8,128)(2,1)} copy(bf16[128,32,1024]{2,0,1:T(8,128)(2,1)} %bitcast.141) | data formatting | bytes 16777216 | tf_op jit(solution)/shard_map/reshape | solution.py:42
  318.5 71.7 %all-to-all-done.1 = bf16[128,32,1024]{2,1,0:T(8,128)(2,1)} async-done(((bf16[128,32,1024]{2,1,0:T(8,128)(2,1)}), bf16[128,32,1024]{2,1,0:T(8,128)(2,1)}, u32[]{:S(2)}, u32[]{:S(2)}) %all-to-all-start.1) | async-done | bytes 8388640 | tf_op jit(solution)/shard_map/all_to_all | solution.py:43
  390.3 10.3 %all-to-all-start.3 = ((bf16[128,32,1024]{2,1,0:T(8,128)(2,1)}), bf16[128,32,1024]{2,1,0:T(8,128)(2,1)}, u32[]{:S(2)}, u32[]{:S(2)}) async-start(bf16[128,32,1024]{2,1,0:T(8,128)(2,1)} %copy.35), calls=%async_computation.3 | async-start | bytes 16777216 | tf_op jit(solution)/shard_map/all_to_all | solution.py:43
  400.7 15.1 %fusion.9 = f32[4,1024,256]{2,1,0:T(8,128)} fusion(bf16[128,4,8,256]{3,0,2,1:T(8,128)(2,1)S(1)} %copy-done.10, bf16[128,4,8,1024]{3,2,1,0:T(8,128)(2,1)} %bitcast.61), kind=kOutput, calls=%fused_computation.19 | convolution fusion | flops 2147483648 | bytes 14680064 | tf_op jit(solution)/shard_map/gecd,gech->edh/dot_general | solution.py:104
  415.8 8.2 %convolution_bitcast_fusion = f32[4,256,1024]{2,1,0:T(8,128)} fusion(bf16[128,4,8,1024]{3,0,2,1:T(8,128)(2,1)} %bitcast.145, f32[4,128,8,256]{3,1,2,0:T(8,128)S(1)} %copy-done.5), kind=kOutput, calls=%fused_computation.20 | convolution fusion | flops 2152726528 | bytes 16777216 | tf_op jit(solution)/shard_map/gech,gecd->ehd/dot_general | solution.py:101
  423.9 5.5 %reduce_sum.59 = bf16[16,32,1024]{2,1,0:T(8,128)(2,1)S(1)} reduce(bf16[8,16,32,1024]{3,2,1,0:T(8,128)(2,1)} %bitcast.46, bf16[]{:T(256)} %constant.8.clone.1), dimensions={0}, to_apply=%region_4.5 | reduce | flops 3670016 | bytes 9437186 | tf_op jit(solution)/shard_map/reduce_sum | solution.py:44
  431.3 77.7 %all-to-all-done.3 = bf16[128,32,1024]{2,1,0:T(8,128)(2,1)} async-done(((bf16[128,32,1024]{2,1,0:T(8,128)(2,1)}), bf16[128,32,1024]{2,1,0:T(8,128)(2,1)}, u32[]{:S(2)}, u32[]{:S(2)}) %all-to-all-start.3) | async-done | bytes 8388640 | tf_op jit(solution)/shard_map/all_to_all | solution.py:43
  509.0 5.5 %reduce_sum.62 = bf16[16,32,1024]{2,1,0:T(8,128)(2,1)S(1)} reduce(bf16[8,16,32,1024]{3,2,1,0:T(8,128)(2,1)} %bitcast.58, bf16[]{:T(256)} %constant.8.clone.1), dimensions={0}, to_apply=%region_7.8 | reduce | flops 3670016 | bytes 9437186 | tf_op jit(solution)/shard_map/reduce_sum | solution.py:44
  518.9 5.0 collective-permute-start.2
  523.9 1.9 collective-permute-start.3
  525.9 1.3 multiply_reduce_fusion
  529.3 3.8 fusion.20
  (120 shorter events, 18.7 us)
Async XLA Ops:
  0.6 180.1 %copy-start = (bf16[4,256,1024]{2,1,0:T(8,128)(2,1)S(1)}, bf16[4,256,1024]{2,1,0:T(8,128)(2,1)}, u32[]{:S(2)}) copy-start(bf16[4,256,1024]{2,1,0:T(8,128)(2,1)} %param.12) | copy-start | bytes 6291460
  1.6 11.5 %collective-permute-start = (bf16[1,15,1024]{2,1,0:T(8,128)(2,1)S(1)}, bf16[1,15,1024]{2,1,0:T(8,128)(2,1)S(1)}, u32[]{:S(2)}, u32[]{:S(2)}) collective-permute-start(bf16[1,15,1024]{2,1,0:T(8,128)(2,1)S(1)} %get-tuple-element.8), channel_id=1, source_target_pairs={{0,16},{16,32},{32,48},{48,64},{64,80},{80,96},{96,112},{1,17},{17... | collective-permute-start | bytes 92168 | tf_op jit(solution)/shard_map/ppermute | solution.py:15
  5.4 7.7 %collective-permute-start.1 = (bf16[1,15,1024]{2,1,0:T(8,128)(2,1)S(1)}, bf16[1,15,1024]{2,1,0:T(8,128)(2,1)S(1)}, u32[]{:S(2)}, u32[]{:S(2)}) collective-permute-start(bf16[1,15,1024]{2,1,0:T(8,128)(2,1)S(1)} %get-tuple-element.9), channel_id=1, source_target_pairs={{16,0},{32,16},{48,32},{64,48},{80,64},{96,80},{112,96},{17,1},{33... | collective-permute-start | bytes 92168 | tf_op jit(solution)/shard_map/ppermute | solution.py:18
  10.2 7.7 %copy-start.11 = (f32[1,1024]{1,0:T(1,128)}, f32[1,1024]{1,0:T(1,128)S(1)}, u32[]{:S(2)}) copy-start(f32[1,1024]{1,0:T(1,128)S(1)} %get-tuple-element.33) | copy-start | bytes 12292
  10.2 7.7 %copy-start.12 = (f32[1,1024]{1,0:T(1,128)}, f32[1,1024]{1,0:T(1,128)S(1)}, u32[]{:S(2)}) copy-start(f32[1,1024]{1,0:T(1,128)S(1)} %get-tuple-element.34) | copy-start | bytes 12292
  10.2 7.7 %copy-start.13 = (f32[1,1024]{1,0:T(1,128)}, f32[1,1024]{1,0:T(1,128)S(1)}, u32[]{:S(2)}) copy-start(f32[1,1024]{1,0:T(1,128)S(1)} %get-tuple-element.35) | copy-start | bytes 12292
  10.2 7.7 %copy-start.14 = (f32[1,1024]{1,0:T(1,128)}, f32[1,1024]{1,0:T(1,128)S(1)}, u32[]{:S(2)}) copy-start(f32[1,1024]{1,0:T(1,128)S(1)} %get-tuple-element.36) | copy-start | bytes 12292
  10.3 7.7 %copy-start.15 = (f32[1,1024]{1,0:T(1,128)}, f32[1,1024]{1,0:T(1,128)S(1)}, u32[]{:S(2)}) copy-start(f32[1,1024]{1,0:T(1,128)S(1)} %get-tuple-element.37) | copy-start | bytes 12292
  10.3 7.7 %copy-start.16 = (f32[1,1024]{1,0:T(1,128)}, f32[1,1024]{1,0:T(1,128)S(1)}, u32[]{:S(2)}) copy-start(f32[1,1024]{1,0:T(1,128)S(1)} %get-tuple-element.38) | copy-start | bytes 12292
  10.3 7.7 %copy-start.17 = (f32[1,1024]{1,0:T(1,128)}, f32[1,1024]{1,0:T(1,128)S(1)}, u32[]{:S(2)}) copy-start(f32[1,1024]{1,0:T(1,128)S(1)} %get-tuple-element.39) | copy-start | bytes 12292
  10.3 7.7 %copy-start.18 = (f32[1,1024]{1,0:T(1,128)}, f32[1,1024]{1,0:T(1,128)S(1)}, u32[]{:S(2)}) copy-start(f32[1,1024]{1,0:T(1,128)S(1)} %get-tuple-element.40) | copy-start | bytes 12292
  11.6 6.4 %copy-start.19 = (f32[1,1024]{1,0:T(1,128)}, f32[1,1024]{1,0:T(1,128)S(1)}, u32[]{:S(2)}) copy-start(f32[1,1024]{1,0:T(1,128)S(1)} %get-tuple-element.10) | copy-start | bytes 12292
  11.6 6.4 %copy-start.20 = (f32[1,1024]{1,0:T(1,128)}, f32[1,1024]{1,0:T(1,128)S(1)}, u32[]{:S(2)}) copy-start(f32[1,1024]{1,0:T(1,128)S(1)} %get-tuple-element.11) | copy-start | bytes 12292
  11.6 6.4 %copy-start.21 = (f32[1,1024]{1,0:T(1,128)}, f32[1,1024]{1,0:T(1,128)S(1)}, u32[]{:S(2)}) copy-start(f32[1,1024]{1,0:T(1,128)S(1)} %get-tuple-element.12) | copy-start | bytes 12292
  11.7 6.4 %copy-start.22 = (f32[1,1024]{1,0:T(1,128)}, f32[1,1024]{1,0:T(1,128)S(1)}, u32[]{:S(2)}) copy-start(f32[1,1024]{1,0:T(1,128)S(1)} %get-tuple-element.13) | copy-start | bytes 12292
  11.7 6.4 %copy-start.23 = (f32[1,1024]{1,0:T(1,128)}, f32[1,1024]{1,0:T(1,128)S(1)}, u32[]{:S(2)}) copy-start(f32[1,1024]{1,0:T(1,128)S(1)} %get-tuple-element.14) | copy-start | bytes 12292
  11.7 6.4 %copy-start.24 = (f32[1,1024]{1,0:T(1,128)}, f32[1,1024]{1,0:T(1,128)S(1)}, u32[]{:S(2)}) copy-start(f32[1,1024]{1,0:T(1,128)S(1)} %get-tuple-element.15) | copy-start | bytes 12292
  11.7 6.4 %copy-start.25 = (f32[1,1024]{1,0:T(1,128)}, f32[1,1024]{1,0:T(1,128)S(1)}, u32[]{:S(2)}) copy-start(f32[1,1024]{1,0:T(1,128)S(1)} %get-tuple-element.16) | copy-start | bytes 12292
  11.7 6.4 %copy-start.26 = (f32[1,1024]{1,0:T(1,128)}, f32[1,1024]{1,0:T(1,128)S(1)}, u32[]{:S(2)}) copy-start(f32[1,1024]{1,0:T(1,128)S(1)} %get-tuple-element.17) | copy-start | bytes 12292
  27.6 11.2 %copy-start.38 = (f32[1,128,2]{1,2,0:T(2,128)S(1)}, f32[1,128,2]{1,2,0:T(2,128)}, u32[]{:S(2)}) copy-start(f32[1,128,2]{1,2,0:T(2,128)} %param.10) | copy-start | bytes 3076
  27.6 11.4 %copy-start.6 = (bf16[1,128,1024]{2,1,0:T(8,128)(2,1)S(1)}, bf16[1,128,1024]{2,1,0:T(8,128)(2,1)}, u32[]{:S(2)}) copy-start(bf16[1,128,1024]{2,1,0:T(8,128)(2,1)} %param.13) | copy-start | bytes 786436
  27.6 119.6 %all-to-all-start = ((bf16[128,32,1024]{2,1,0:T(8,128)(2,1)}), bf16[128,32,1024]{2,1,0:T(8,128)(2,1)}, u32[]{:S(2)}, u32[]{:S(2)}) async-start(bf16[128,32,1024]{2,1,0:T(8,128)(2,1)} %bitcast.139), calls=%async_computation | async-start | bytes 16777216 | tf_op jit(solution)/shard_map/all_to_all | solution.py:83
  152.7 118.8 %all-to-all-start.2 = ((bf16[128,32,1024]{2,1,0:T(8,128)(2,1)}), bf16[128,32,1024]{2,1,0:T(8,128)(2,1)}, u32[]{:S(2)}, u32[]{:S(2)}) async-start(bf16[128,32,1024]{2,1,0:T(8,128)(2,1)} %bitcast.140), calls=%async_computation.2 | async-start | bytes 16777216 | tf_op jit(solution)/shard_map/all_to_all | solution.py:84
  163.5 11.5 %copy-start.2 = (bf16[4,1024,256]{2,1,0:T(8,128)(2,1)S(1)}, bf16[4,1024,256]{2,1,0:T(8,128)(2,1)}, u32[]{:S(2)}) copy-start(bf16[4,1024,256]{2,1,0:T(8,128)(2,1)} %param.11) | copy-start | bytes 6291460
  271.5 118.8 %all-to-all-start.1 = ((bf16[128,32,1024]{2,1,0:T(8,128)(2,1)}), bf16[128,32,1024]{2,1,0:T(8,128)(2,1)}, u32[]{:S(2)}, u32[]{:S(2)}) async-start(bf16[128,32,1024]{2,1,0:T(8,128)(2,1)} %copy.30), calls=%async_computation.1 | async-start | bytes 16777216 | tf_op jit(solution)/shard_map/all_to_all | solution.py:43
  293.1 8.0 %copy-start.3 = (bf16[4,1024,256]{2,1,0:T(8,128)(2,1)S(1)}, bf16[4,1024,256]{2,1,0:T(8,128)(2,1)}, u32[]{:S(2)}) copy-start(bf16[4,1024,256]{2,1,0:T(8,128)(2,1)} %param.11) | copy-start | bytes 6291460
  318.5 82.1 %copy-start.10 = (bf16[128,4,8,256]{3,0,2,1:T(8,128)(2,1)S(1)}, bf16[128,4,8,256]{3,0,2,1:T(8,128)(2,1)}, u32[]{:S(2)}) copy-start(bf16[128,4,8,256]{3,0,2,1:T(8,128)(2,1)} %copy-done.9) | copy-start | bytes 6291460
  390.3 118.8 %all-to-all-start.3 = ((bf16[128,32,1024]{2,1,0:T(8,128)(2,1)}), bf16[128,32,1024]{2,1,0:T(8,128)(2,1)}, u32[]{:S(2)}, u32[]{:S(2)}) async-start(bf16[128,32,1024]{2,1,0:T(8,128)(2,1)} %copy.35), calls=%async_computation.3 | async-start | bytes 16777216 | tf_op jit(solution)/shard_map/all_to_all | solution.py:43
  400.7 15.1 %copy-start.5 = (f32[4,128,8,256]{3,1,2,0:T(8,128)S(1)}, f32[4,128,8,256]{3,1,2,0:T(8,128)}, u32[]{:S(2)}) copy-start(f32[4,128,8,256]{3,1,2,0:T(8,128)} %copy-done.4) | copy-start | bytes 12582916
  515.7 11.5 %copy-start.8 = (bf16[1,128,1024]{2,1,0:T(8,128)(2,1)S(1)}, bf16[1,128,1024]{2,1,0:T(8,128)(2,1)}, u32[]{:S(2)}) copy-start(bf16[1,128,1024]{2,1,0:T(8,128)(2,1)} %copy-done.7) | copy-start | bytes 786436
  518.9 9.0 %collective-permute-start.2 = (bf16[1,15,1024]{2,1,0:T(8,128)(2,1)S(1)}, bf16[1,15,1024]{2,1,0:T(8,128)(2,1)S(1)}, u32[]{:S(2)}, u32[]{:S(2)}) collective-permute-start(bf16[1,15,1024]{2,1,0:T(8,128)(2,1)S(1)} %get-tuple-element.6), channel_id=1, source_target_pairs={{0,16},{16,32},{32,48},{48,64},{64,80},{80,96},{96,112},{1,17},{17... | collective-permute-start | bytes 92168 | tf_op jit(solution)/shard_map/ppermute | solution.py:15
  523.9 5.2 collective-permute-start.3
  (17 other events, 97.0 us)
where the time goes:
time: 542 us; the launch traced here: 533 us
  waiting for transfers between devices  325 us (60%)
  local copies, waits for them, and re-layouts  74.3 us (14%)
  starting transfers between devices  55 us (10%)
  matrix products  48.3 us (9%)
  other arithmetic  29.3 us (5%)
    all_to_all x2, waiting for transfers between devices, to_sources(): lax.all_to_all(whole_term, ('seq', 'exp'), split_axis=0, concat_axis=0, t...  149 us
    all_to_all x1, waiting for transfers between devices, per_device(): lax.all_to_all(wide_up, ('seq', 'exp'), split_axis=0, concat_axis=0, tile...  101 us
    all_to_all x1, waiting for transfers between devices, per_device(): lax.all_to_all(wide_down, ('seq', 'exp'), split_axis=0, concat_axis=0, ti...  73.6 us
    reshape x2, local copies, waits for them, and re-layouts, to_sources(): term_fn(0, groups).astype(jnp.bfloat16)  23.3 us
    all_to_all x2, starting transfers between devices, to_sources(): lax.all_to_all(whole_term, ('seq', 'exp'), split_axis=0, concat_axis=0, t...  20.5 us
    dot_general x1, matrix products, per_device(): jnp.einsum('gecd,gech->edh', routed_up, pre_grad, preferred_element_type=...  15.1 us
    all_to_all x1, local copies, waits for them, and re-layouts, per_device(): lax.all_to_all(wide_up, ('seq', 'exp'), split_axis=0, concat_axis=0, tile...  11.5 us
    all_to_all x1, local copies, waits for them, and re-layouts, per_device(): lax.all_to_all(wide_down, ('seq', 'exp'), split_axis=0, concat_axis=0, ti...  11.3 us
  transfers between devices with their start and end apart: 8, of which 5 were waited for; matrix products, arithmetic and copies ran while one was open for 22% of the time, Pallas kernels for 0%

commit v1 on v0

v1 whole, which is shorter than its diff:
```python
import jax
import jax.numpy as jnp
from jax import lax
from jax.experimental import pallas as pl
from jax.experimental.pallas import tpu as pltpu
from jax.sharding import Mesh, PartitionSpec as P

KERNEL = 31
MARGIN = (KERNEL - 1) // 2
CAP = 8
EDGE = 16
BF16 = jnp.bfloat16
F32 = jnp.float32


def shape_of(dims, dtype):
    return jax.ShapeDtypeStruct(dims, dtype)


def params(mib):
    return pltpu.CompilerParams(vmem_limit_bytes=mib << 20)


def cost(flops, nbytes):
    return pl.CostEstimate(flops=flops, bytes_accessed=nbytes, transcendentals=0)


def silu_slope(values):
    logistic = jax.nn.sigmoid(values)
    return logistic * (1.0 + values * (1.0 - logistic))


def dot(left, right, dims):
    return lax.dot_general(left, right, ((dims[:1], dims[1:]), ((), ())), preferred_element_type=F32)


def slot_masks(routes_ref, experts, n_y):
    length = routes_ref.shape[0]
    n_exp = experts // n_y
    slots = experts * CAP
    routes = routes_ref[...]
    lane = lax.broadcasted_iota(jnp.int32, (length, experts), 1)
    before = (
        lax.broadcasted_iota(jnp.int32, (length, length), 1)
        < lax.broadcasted_iota(jnp.int32, (length, length), 0)
    ).astype(F32).astype(BF16)
    place = lax.broadcasted_iota(jnp.int32, (length, slots), 1)
    base = jnp.zeros((1, experts), F32)
    masks = []
    for choice in range(2):
        expert = routes[:, choice : choice + 1]
        named = (lane == expert).astype(F32)
        earlier = dot(before, named.astype(BF16), (1, 0)) + base
        rank = jnp.sum(named * earlier, axis=1, keepdims=True).astype(jnp.int32)
        base = base + jnp.sum(named, axis=0, keepdims=True)
        start = (expert % n_y) * n_exp + expert // n_y
        masks.append((place == start * CAP + rank).astype(F32).astype(BF16))
    return masks


def down_slots(routes, gates, cotangent, experts, n_y):
    length, width = cotangent.shape

    def body(routes_ref, gates_ref, cot_ref, out_ref):
        masks = slot_masks(routes_ref, experts, n_y)
        cot = cot_ref[...].astype(F32)
        gate = gates_ref[...]
        total = None
        for choice in range(2):
            rows = (gate[:, choice : choice + 1] * cot).astype(BF16)
            part = dot(masks[choice], rows, (0, 0))
            total = part if total is None else total + part
        out_ref[...] = total.astype(BF16)

    return pl.pallas_call(
        body,
        out_shape=shape_of((experts * CAP, width), BF16),
        compiler_params=params(32),
        cost_estimate=cost(1 << 28, 2 << 20),
        name="down_slots",
    )(routes, gates, cotangent)


def tap_sum(pad_ref, kernel_ref, columns, length, reverse):
    padded = pad_ref[:, columns]
    taps = kernel_ref[:, columns]
    total = jnp.zeros((length, padded.shape[1]), F32)
    for residue in range(8):
        offsets = [
            tap for tap in range(KERNEL) if (EDGE - MARGIN + tap) % 8 == residue
        ]
        shifted = padded[residue : residue + length + 24, :]
        for tap in offsets:
            start = EDGE - MARGIN + tap - residue
            weight = KERNEL - 1 - tap if reverse else tap
            total = total + taps[weight : weight + 1, :] * shifted[start : start + length, :]
    return total


COLUMNS = 128


def conv_up(low, frames, high, kernel, routes, experts, n_y):
    length, width = frames.shape

    def body(low_ref, frames_ref, high_ref, kernel_ref, routes_ref, mix_ref, hid_ref, out_ref, pad):
        pad[:EDGE] = low_ref[...].astype(F32)
        pad[EDGE : EDGE + length] = frames_ref[...].astype(F32)
        pad[EDGE + length :] = high_ref[...].astype(F32)

        def step(index, carry):
            columns = pl.ds(pl.multiple_of(index * COLUMNS, COLUMNS), COLUMNS)
            mixing = tap_sum(pad, kernel_ref, columns, length, False)
            mix_ref[:, columns] = mixing
            own = pad[EDGE : EDGE + length, columns]
            hid_ref[:, columns] = (own + mixing * jax.nn.sigmoid(mixing)).astype(BF16)
            return carry

        lax.fori_loop(0, width // COLUMNS, step, 0)
        first, second = slot_masks(routes_ref, experts, n_y)
        out_ref[...] = dot(first + second, hid_ref[...], (0, 0)).astype(BF16)

    return pl.pallas_call(
        body,
        out_shape=(
            shape_of((length, width), F32),
            shape_of((length, width), BF16),
            shape_of((experts * CAP, width), BF16),
        ),
        scratch_shapes=[pltpu.VMEM((length + 2 * EDGE, width), F32)],
        compiler_params=params(32),
        cost_estimate=cost(1 << 28, 3 << 20),
        name="conv_up",
    )(low, frames, high, kernel, routes)


TILE = 256


def block_step(up, down, w_in, w_out, grad_type):
    rows, width = up[0].shape
    hidden = w_in.shape[1]

    def body(ua, ub, da, db, wi, wo, act_ref, pre_ref, gi_ref, go_ref):
        for half, (u_ref, d_ref) in enumerate(((ua, da), (ub, db))):
            for start in range(0, rows, TILE):
                part = slice(start, start + TILE)
                held = slice(half * rows + start, half * rows + start + TILE)
                pre = dot(u_ref[part, :], wi[...], (1, 0))
                logistic = jax.nn.sigmoid(pre)
                act_ref[held, :] = (pre * logistic).astype(BF16)
                back = dot(d_ref[part, :], wo[...], (1, 1))
                slope = logistic * (1.0 + pre * (1.0 - logistic))
                pre_ref[held, :] = (back * slope).astype(BF16)
        for start in range(0, width, TILE):
            part = slice(start, start + TILE)
            out = dot(act_ref[:rows, :], da[:, part], (0, 0))
            out = out + dot(act_ref[rows:, :], db[:, part], (0, 0))
            go_ref[:, part] = out.astype(grad_type)
            out = dot(ua[:, part], pre_ref[:rows, :], (0, 0))
            out = out + dot(ub[:, part], pre_ref[rows:, :], (0, 0))
            gi_ref[part, :] = out.astype(grad_type)

    return pl.pallas_call(
        body,
        out_shape=(
            shape_of((2 * rows, hidden), BF16),
            shape_of((2 * rows, hidden), BF16),
            shape_of((width, hidden), grad_type),
            shape_of((hidden, width), grad_type),
        ),
        compiler_params=params(48),
        cost_estimate=cost(16 * rows * width * hidden, 8 << 20),
        name="block_step",
    )(up[0], up[1], down[0], down[1], w_in, w_out)


def back_to_width(parts, weights, contract, rows):
    width = weights[0].shape[1 - contract]

    def body(*refs):
        part_refs, weight_refs = refs[:4], refs[4:8]
        own_ref, other_ref = refs[8:]
        for half, out_ref in enumerate((own_ref, other_ref)):
            for start in range(0, rows, TILE):
                held = slice(half * rows + start, half * rows + start + TILE)
                total = None
                for part_ref, weight_ref in zip(part_refs, weight_refs):
                    part = dot(part_ref[held, :], weight_ref[...], (1, contract))
                    total = part if total is None else total + part
                out_ref[start : start + TILE, :] = total.astype(BF16)

    return pl.pallas_call(
        body,
        out_shape=(shape_of((rows, width), BF16), shape_of((rows, width), BF16)),
        compiler_params=params(48),
        cost_estimate=cost(16 * rows * width * 256, 8 << 20),
        name="back_to_width",
    )(*parts, *weights)


def mix_out(routes, gates, hidden, expert_out, experts, n_y):
    def body(routes_ref, gates_ref, hid_ref, out_ref, mixed_ref):
        masks = slot_masks(routes_ref, experts, n_y)
        gate = gates_ref[...]
        total = hid_ref[...].astype(F32)
        for choice in range(2):
            total = total + gate[:, choice : choice + 1] * dot(masks[choice], out_ref[...], (1, 0))
        mixed_ref[...] = total.astype(BF16)

    return pl.pallas_call(
        body,
        out_shape=shape_of(hidden.shape, BF16),
        compiler_params=params(32),
        cost_estimate=cost(1 << 28, 2 << 20),
        name="mix_out",
    )(routes, gates, hidden, expert_out)


def grad_rows(routes, cotangent, mixing, input_grad, experts, n_y):
    def body(routes_ref, cot_ref, mix_ref, grad_ref, hidden_ref, back_ref):
        first, second = slot_masks(routes_ref, experts, n_y)
        grad = cot_ref[...].astype(F32) + dot(first + second, grad_ref[...], (1, 0))
        hidden_ref[...] = grad
        back_ref[...] = (grad * silu_slope(mix_ref[...])).astype(BF16)

    return pl.pallas_call(
        body,
        out_shape=(shape_of(cotangent.shape, F32), shape_of(cotangent.shape, BF16)),
        compiler_params=params(32),
        cost_estimate=cost(1 << 28, 3 << 20),
        name="grad_rows",
    )(routes, cotangent, mixing, input_grad)


def conv_down(low, back, high, kernel, hidden_grad):
    length, width = back.shape

    def body(low_ref, back_ref, high_ref, kernel_ref, grad_ref, out_ref, pad):
        pad[:EDGE] = low_ref[...].astype(F32)
        pad[EDGE : EDGE + length] = back_ref[...].astype(F32)
        pad[EDGE + length :] = high_ref[...].astype(F32)

        def step(index, carry):
            columns = pl.ds(pl.multiple_of(index * COLUMNS, COLUMNS), COLUMNS)
            spread = tap_sum(pad, kernel_ref, columns, length, True)
            out_ref[:, columns] = (grad_ref[:, columns] + spread).astype(BF16)
            return carry

        lax.fori_loop(0, width // COLUMNS, step, 0)

    return pl.pallas_call(
        body,
        out_shape=shape_of((length, width), BF16),
        scratch_shapes=[pltpu.VMEM((length + 2 * EDGE, width), F32)],
        compiler_params=params(32),
        cost_estimate=cost(1 << 27, 2 << 20),
        name="conv_down",
    )(low, back, high, kernel, hidden_grad)


def place_grads(spots, parts):
    rows, columns = parts[0].shape
    count = len(parts)

    def body(spots_ref, *refs):
        part_refs, out_ref = refs[:count], refs[count]
        for index in range(count):

            @pl.when(pl.program_id(0) == index)
            def _():
                out_ref[0] = part_refs[index][...].astype(F32)

    return pl.pallas_call(
        body,
        grid_spec=pltpu.PrefetchScalarGridSpec(
            num_scalar_prefetch=1,
            grid=(count,),
            in_specs=[
                pl.BlockSpec((rows, columns), lambda i, spots: (0, 0)) for _ in range(count)
            ],
            out_specs=pl.BlockSpec((1, rows, columns), lambda i, spots: (spots[i], 0, 0)),
        ),
        out_shape=shape_of((count, rows, columns), F32),
        compiler_params=params(32),
        cost_estimate=cost(1 << 20, 7 << 20),
        name="place_grads",
    )(spots, *parts)


def edges(block):
    count = lax.axis_size("y") * lax.axis_size("core")
    forward = [(i, i + 1) for i in range(count - 1)]
    backward = [(target, source) for source, target in forward]
    low = lax.ppermute(block[-EDGE:], ("y", "core"), forward)
    high = lax.ppermute(block[:EDGE], ("y", "core"), backward)
    return low, high


def turn(block, steps):
    count = lax.axis_size("y")
    return lax.ppermute(block, "y", [(i, (i + steps) % count) for i in range(count)])


def swap(block):
    return lax.ppermute(block, "core", [(0, 1), (1, 0)])


def exchange(rows, groups):
    grouped = rows.reshape(groups, CAP, rows.shape[1])
    moved = lax.all_to_all(grouped, ("y", "exp"), split_axis=0, concat_axis=0, tiled=True)
    return moved.reshape(rows.shape)


def per_device(frames, conv_kernel, routes, gates, w_in, w_out, cotangent):
    n_y = lax.axis_size("y")
    n_exp = lax.axis_size("exp")
    groups = n_y * n_exp
    experts = w_in.shape[0] * n_exp
    y = lax.axis_index("y")
    frames, routes, gates, cotangent = frames[0], routes[0], gates[0], cotangent[0]
    slots = experts * CAP

    low, high = edges(frames)

    def gathered(weights):
        def block(steps):
            return lax.dynamic_index_in_dim(weights, (y + steps) % n_y, 0, keepdims=False)

        return [block(0)] + [turn(block(steps), steps) for steps in range(1, n_y)]

    w_ins = gathered(w_in)
    w_outs = gathered(w_out)

    send_down = down_slots(routes, gates, cotangent, experts, n_y)
    down = exchange(send_down, groups)
    mixing, hidden, send_up = conv_up(low, frames, high, conv_kernel, routes, experts, n_y)
    up = exchange(send_up, groups)
    downs = (down, swap(down))
    ups = (up, swap(up))

    acts, pres, grads_in, grads_out = [], [], [], []
    for steps in range(n_y):
        kept = F32 if steps == 0 else BF16
        act, pre, grad_in, grad_out = block_step(ups, downs, w_ins[steps], w_outs[steps], kept)
        acts.append(act)
        pres.append(pre)
        if steps:
            grad_in, grad_out = turn(grad_in, -steps), turn(grad_out, -steps)
        grads_in.append(grad_in)
        grads_out.append(grad_out)

    own, other = back_to_width(pres, w_ins, 1, slots)
    input_grad = exchange((own.astype(F32) + swap(other).astype(F32)).astype(BF16), groups)
    own, other = back_to_width(acts, w_outs, 0, slots)
    expert_out = exchange((own.astype(F32) + swap(other).astype(F32)).astype(BF16), groups)

    hidden_grad, back = grad_rows(routes, cotangent, mixing, input_grad, experts, n_y)
    low, high = edges(back)
    frames_grad = conv_down(low, back, high, conv_kernel, hidden_grad)
    mixed = mix_out(routes, gates, hidden, expert_out, experts, n_y)

    spots = jnp.stack([(y + steps) % n_y for steps in range(n_y)]).astype(jnp.int32)
    w_in_grad = place_grads(spots, grads_in)
    w_out_grad = place_grads(spots, grads_out)
    return (mixed[None], frames_grad[None], w_in_grad, w_out_grad)


def solution(mesh):
    cores = 2
    n_seq, n_exp = mesh.devices.shape
    split = Mesh(mesh.devices.reshape(n_seq // cores, cores, n_exp), ("y", "core", "exp"))
    seq = ("y", "core")
    in_specs = (
        P("exp", seq, None),
        P(),
        P("exp", seq, None),
        P("exp", seq, None),
        P("exp", None, seq),
        P("exp", seq, None),
        P("exp", seq, None),
    )
    out_specs = (
        P("exp", seq, None),
        P("exp", seq, None),
        P("exp", None, seq),
        P("exp", seq, None),
    )
    return jax.shard_map(
        per_device, mesh=split, in_specs=in_specs, out_specs=out_specs, check_vma=False
    )
```

time: 542 us -> 227 us (0.42); the launches traced: 533 us -> 224 us
  waiting for transfers between devices: 325 us -> 97.2 us
  local copies, waits for them, and re-layouts: 74.3 us -> 12.1 us
  matrix products: 48.3 us -> 0 us
  Pallas kernels: 0 us -> 43.5 us
  other arithmetic: 29.3 us -> 4.15 us
  starting transfers between devices: 55 us -> 66.5 us
    all_to_all x4, waiting for transfers between devices: 324 us -> 29.1 us  [exchange(): lax.all_to_all(grouped, ('y', 'exp'), split_axis=0, concat_axis=0, tiled=...]
    ppermute x4 -> x20, waiting for transfers between devices: 1.18 us -> 68.1 us  [the longest x12 60.4 us: turn(): lax.ppermute(block, 'y', [(i, (i + steps) % count) for i in range(count)])]
    dot_general x6 -> x0, matrix products: 48.3 us -> none  [the longest x1 15.1 us: per_device(): jnp.einsum('gecd,gech->edh', routed_up, pre_grad, preferred_element_type=...]
    pallas_call x0 -> x13, Pallas kernels: none -> 43.5 us  [the longest x4 17.4 us: block_step(): pl.pallas_call(body, out_shape=(shape_of((2 * rows, hidden), BF16), shape...]
    reshape x4 -> x0, local copies, waits for them, and re-layouts: 26.4 us -> none  [the longest x2 23.3 us: to_sources(): term_fn(0, groups).astype(jnp.bfloat16)]
    all_to_all x2 -> x0, local copies, waits for them, and re-layouts: 22.8 us -> none  [the longest x1 11.5 us: per_device(): lax.all_to_all(wide_up, ('seq', 'exp'), split_axis=0, concat_axis=0, tile...]
    ppermute x4 -> x20, starting transfers between devices: 12.6 us -> 34 us  [the longest x12 14.1 us: turn(): lax.ppermute(block, 'y', [(i, (i + steps) % count) for i in range(count)])]
    reduce_sum x5 -> x0, other arithmetic: 13.8 us -> none  [the longest x2 11.1 us: to_sources(): jnp.sum(arrived.reshape(n_seq, n_exp, per_dest, model_width).astype(jnp.f...]
  transfers between devices with their start and end apart: 8 -> 24, of which waited for: 5 -> 10; matrix products, arithmetic and copies ran while one was open for 22% -> 3% of each run, Pallas kernels for 0% -> 11%
where the time goes in v1:
time: 227 us; the launch traced here: 224 us
  waiting for transfers between devices  97.2 us (43%)
  starting transfers between devices  66.5 us (29%)
  Pallas kernels  43.5 us (19%)
  local copies, waits for them, and re-layouts  12.1 us (5%)
  other arithmetic  4.15 us (2%)
    ppermute x12, waiting for transfers between devices, turn(): lax.ppermute(block, 'y', [(i, (i + steps) % count) for i in range(count)])  60.4 us
    all_to_all x4, starting transfers between devices, exchange(): lax.all_to_all(grouped, ('y', 'exp'), split_axis=0, concat_axis=0, tiled=...  32.5 us
    all_to_all x4, waiting for transfers between devices, exchange(): lax.all_to_all(grouped, ('y', 'exp'), split_axis=0, concat_axis=0, tiled=...  29.1 us
    pallas_call x4, Pallas kernels, block_step(): pl.pallas_call(body, out_shape=(shape_of((2 * rows, hidden), BF16), shape...  17.4 us
    ppermute x12, starting transfers between devices, turn(): lax.ppermute(block, 'y', [(i, (i + steps) % count) for i in range(count)])  14.1 us
    ppermute x2, starting transfers between devices, edges(): low = lax.ppermute(block[-EDGE:], ('y', 'core'), forward)  12.5 us
    unnamed x50, local copies, waits for them, and re-layouts  10.1 us
    ppermute x2, waiting for transfers between devices, edges(): high = lax.ppermute(block[:EDGE], ('y', 'core'), backward)  7.69 us
  transfers between devices with their start and end apart: 24, of which 10 were waited for; matrix products, arithmetic and copies ran while one was open for 3% of the time, Pallas kernels for 11%

profile of v1, /device:TPU:5, one launch (start us, length us, event | category | flops | bytes accessed | tf_op | source)
XLA Modules:
  0.0 224.5 jit_solution(4060000548653919665)
XLA Ops:
  3.2 2.1 down_slots.1
  5.3 10.9 %all-to-all-start.1 = ((bf16[64,8,1024]{2,1,0:T(8,128)(2,1)}), bf16[64,8,1024]{2,1,0:T(8,128)(2,1)S(1)}, u32[]{:S(2)}, u32[]{:S(2)}) async-start(bf16[64,8,1024]{2,1,0:T(8,128)(2,1)} %bitcast.8), calls=%async_computation.1 | async-start | bytes 2097152 | tf_op jit(solution)/shard_map/all_to_all | solution.py:311
  16.2 3.1 %collective-permute-start.1 = (bf16[16,1024]{1,0:T(8,128)(2,1)S(1)}, bf16[16,1024]{1,0:T(8,128)(2,1)S(1)}, u32[]{:S(2)}, u32[]{:S(2)}) collective-permute-start(bf16[16,1024]{1,0:T(8,128)(2,1)S(1)} %get-tuple-element.64), channel_id=1, source_target_pairs={{16,0},{32,16},{48,32},{64,48},{80,64},{96,80},{112,96},{17,1},{33... | collective-permute-start | bytes 98312 | tf_op jit(solution)/shard_map/ppermute | solution.py:296
  19.4 3.0 %collective-permute-start = (bf16[16,1024]{1,0:T(8,128)(2,1)S(1)}, bf16[16,1024]{1,0:T(8,128)(2,1)S(1)}, u32[]{:S(2)}, u32[]{:S(2)}) collective-permute-start(bf16[16,1024]{1,0:T(8,128)(2,1)S(1)} %get-tuple-element.65), channel_id=1, source_target_pairs={{0,16},{16,32},{32,48},{48,64},{64,80},{80,96},{96,112},{1,17},{17... | collective-permute-start | bytes 98312 | tf_op jit(solution)/shard_map/ppermute | solution.py:295
  22.4 7.7 %collective-permute-done.1.high_ref = bf16[16,1024]{1,0:T(8,128)(2,1)S(1)} collective-permute-done((bf16[16,1024]{1,0:T(8,128)(2,1)S(1)}, bf16[16,1024]{1,0:T(8,128)(2,1)S(1)}, u32[]{:S(2)}, u32[]{:S(2)}) %collective-permute-start.1) | collective-permute-done | bytes 32800 | tf_op jit(solution)/shard_map/ppermute | solution.py:296
  30.1 4.7 %conv_up.1 = (f32[128,1024]{1,0:T(8,128)S(1)}, bf16[128,1024]{1,0:T(8,128)(2,1)S(1)}, bf16[512,1024]{1,0:T(8,128)(2,1)}) custom-call(bf16[16,1024]{1,0:T(8,128)(2,1)S(1)} %collective-permute-done.low_ref, bf16[128,1024]{1,0:T(8,128)(2,1)S(1)} %bitcast.55, bf16[16,1024]{1,0:T(8,128)(2,1)S(1)} %collective-permute-done.1.high_ref, f32[31,1024]{1,0:T(8,128)S(1)} %copy-done.12, ...), custom_call_target="tpu_custom_call" | custom-call | flops 268435456 | bytes 3145728 | tf_op jit(solution)/shard_map/conv_up/pallas_call | solution.py:123
  36.3 9.6 %all-to-all-start = ((bf16[64,8,1024]{2,1,0:T(8,128)(2,1)}), bf16[64,8,1024]{2,1,0:T(8,128)(2,1)S(1)}, u32[]{:S(2)}, u32[]{:S(2)}) async-start(bf16[64,8,1024]{2,1,0:T(8,128)(2,1)} %bitcast.5), calls=%async_computation | async-start | bytes 2097152 | tf_op jit(solution)/shard_map/all_to_all | solution.py:311
  45.9 17.7 %all-to-all-done = bf16[64,8,1024]{2,1,0:T(8,128)(2,1)S(1)} async-done(((bf16[64,8,1024]{2,1,0:T(8,128)(2,1)}), bf16[64,8,1024]{2,1,0:T(8,128)(2,1)S(1)}, u32[]{:S(2)}, u32[]{:S(2)}) %all-to-all-start) | async-done | bytes 1048608 | tf_op jit(solution)/shard_map/all_to_all | solution.py:311
  66.8 2.3 %collective-permute-start.7 = (bf16[256,1024]{1,0:T(8,128)(2,1)S(1)}, bf16[256,1024]{1,0:T(8,128)(2,1)S(1)}, u32[]{:S(2)}, u32[]{:S(2)}) collective-permute-start(bf16[256,1024]{1,0:T(8,128)(2,1)S(1)} %get-tuple-element.57), channel_id=1, source_target_pairs={{0,64},{32,96},{64,0},{96,32},{1,65},{33,97},{65,1},{97,33},{2,66}... | collective-permute-start | bytes 1572872 | tf_op jit(solution)/shard_map/ppermute | solution.py:302
  69.5 11.3 %collective-permute-done.6.wi.refs_6_ = bf16[1024,256]{1,0:T(8,128)(2,1)S(1)} collective-permute-done((bf16[1024,256]{1,0:T(8,128)(2,1)S(1)}, bf16[1024,256]{1,0:T(8,128)(2,1)S(1)}, u32[]{:S(2)}, u32[]{:S(2)}) %collective-permute-start.6) | collective-permute-done | bytes 524320 | tf_op jit(solution)/shard_map/ppermute | solution.py:302
  81.2 10.9 %collective-permute-done.7.wo.refs_6_ = bf16[256,1024]{1,0:T(8,128)(2,1)S(1)} collective-permute-done((bf16[256,1024]{1,0:T(8,128)(2,1)S(1)}, bf16[256,1024]{1,0:T(8,128)(2,1)S(1)}, u32[]{:S(2)}, u32[]{:S(2)}) %collective-permute-start.7) | collective-permute-done | bytes 524320 | tf_op jit(solution)/shard_map/ppermute | solution.py:302
  93.3 4.5 %block_step.6 = (bf16[1024,256]{1,0:T(8,128)(2,1)S(1)}, bf16[1024,256]{1,0:T(8,128)(2,1)S(1)}, bf16[1024,256]{1,0:T(8,128)(2,1)S(1)}, bf16[256,1024]{1,0:T(8,128)(2,1)S(1)}) custom-call(bf16[512,1024]{1,0:T(8,128)(2,1)S(1)} %bitcast.43, bf16[512,1024]{1,0:T(8,128)(2,1)S(1)} %collective-permute-done.2.ub, bf16[512,1024]{1,0:T(8,128)(2,1)} %bitcast.57, ...), custom_call_target="tpu_custom_call" | custom-call | flops 2147483648 | bytes 8388608 | tf_op jit(solution)/shard_map/block_step/pallas_call | solution.py:164
  99.4 4.4 %collective-permute-done.4.wi.refs_5_ = bf16[1024,256]{1,0:T(8,128)(2,1)S(1)} collective-permute-done((bf16[1024,256]{1,0:T(8,128)(2,1)S(1)}, bf16[1024,256]{1,0:T(8,128)(2,1)S(1)}, u32[]{:S(2)}, u32[]{:S(2)}) %collective-permute-start.4) | collective-permute-done | bytes 524320 | tf_op jit(solution)/shard_map/ppermute | solution.py:302
  103.7 11.2 %collective-permute-done.5.wo.refs_5_ = bf16[256,1024]{1,0:T(8,128)(2,1)S(1)} collective-permute-done((bf16[256,1024]{1,0:T(8,128)(2,1)S(1)}, bf16[256,1024]{1,0:T(8,128)(2,1)S(1)}, u32[]{:S(2)}, u32[]{:S(2)}) %collective-permute-start.5) | collective-permute-done | bytes 524320 | tf_op jit(solution)/shard_map/ppermute | solution.py:302
  115.0 4.1 %block_step.5 = (bf16[1024,256]{1,0:T(8,128)(2,1)S(1)}, bf16[1024,256]{1,0:T(8,128)(2,1)S(1)}, bf16[1024,256]{1,0:T(8,128)(2,1)S(1)}, bf16[256,1024]{1,0:T(8,128)(2,1)S(1)}) custom-call(bf16[512,1024]{1,0:T(8,128)(2,1)S(1)} %bitcast.44, bf16[512,1024]{1,0:T(8,128)(2,1)S(1)} %collective-permute-done.2.ub, bf16[512,1024]{1,0:T(8,128)(2,1)} %bitcast.58, ...), custom_call_target="tpu_custom_call" | custom-call | flops 2147483648 | bytes 8388608 | tf_op jit(solution)/shard_map/block_step/pallas_call | solution.py:164
  120.7 4.1 %block_step.7 = (bf16[1024,256]{1,0:T(8,128)(2,1)S(1)}, bf16[1024,256]{1,0:T(8,128)(2,1)S(1)}, bf16[1024,256]{1,0:T(8,128)(2,1)S(1)}, bf16[256,1024]{1,0:T(8,128)(2,1)S(1)}) custom-call(bf16[512,1024]{1,0:T(8,128)(2,1)S(1)} %bitcast.45, bf16[512,1024]{1,0:T(8,128)(2,1)S(1)} %collective-permute-done.2.ub, bf16[512,1024]{1,0:T(8,128)(2,1)} %bitcast.59, ...), custom_call_target="tpu_custom_call" | custom-call | flops 2147483648 | bytes 8388608 | tf_op jit(solution)/shard_map/block_step/pallas_call | solution.py:164
  124.8 4.8 %block_step.4 = (bf16[1024,256]{1,0:T(8,128)(2,1)S(1)}, bf16[1024,256]{1,0:T(8,128)(2,1)S(1)}, f32[1024,256]{1,0:T(8,128)S(1)}, f32[256,1024]{1,0:T(8,128)S(1)}) custom-call(bf16[512,1024]{1,0:T(8,128)(2,1)S(1)} %bitcast.46, bf16[512,1024]{1,0:T(8,128)(2,1)} %copy-done.15, bf16[512,1024]{1,0:T(8,128)(2,1)} %bitcast.60, ...), custom_call_target="tpu_custom_call" | custom-call | flops 2147483648 | bytes 8388608 | tf_op jit(solution)/shard_map/block_step/pallas_call | solution.py:164
  130.6 3.3 %back_to_width.3 = (bf16[512,1024]{1,0:T(8,128)(2,1)S(1)}, bf16[512,1024]{1,0:T(8,128)(2,1)}) custom-call(bf16[1024,256]{1,0:T(8,128)(2,1)S(1)} %get-tuple-element.38.refs_0_, bf16[1024,256]{1,0:T(8,128)(2,1)S(1)} %get-tuple-element.39.refs_1_, bf16[1024,256]{1,0:T(8,128)(2,1)S(1)} %get-tuple-element.40.refs_2_, ...), custom_call_target="tpu_custom_call" | custom-call | flops 2147483648 | bytes 8388608 | tf_op jit(solution)/shard_map/back_to_width/pallas_call | solution.py:193
  134.4 3.3 %back_to_width.2 = (bf16[512,1024]{1,0:T(8,128)(2,1)S(1)}, bf16[512,1024]{1,0:T(8,128)(2,1)}) custom-call(bf16[1024,256]{1,0:T(8,128)(2,1)S(1)} %get-tuple-element.31.refs_0_, bf16[1024,256]{1,0:T(8,128)(2,1)S(1)} %get-tuple-element.32.refs_1_, bf16[1024,256]{1,0:T(8,128)(2,1)S(1)} %get-tuple-element.33.refs_2_, ...), custom_call_target="tpu_custom_call" | custom-call | flops 2147483648 | bytes 8388608 | tf_op jit(solution)/shard_map/back_to_width/pallas_call | solution.py:193
  139.1 6.1 %all-to-all-start.3 = ((bf16[64,8,1024]{2,1,0:T(8,128)(2,1)}), bf16[64,8,1024]{2,1,0:T(8,128)(2,1)S(1)}, u32[]{:S(2)}, u32[]{:S(2)}) async-start(bf16[64,8,1024]{2,1,0:T(8,128)(2,1)} %fusion.1), calls=%async_computation.3 | async-start | bytes 2097152 | tf_op jit(solution)/shard_map/all_to_all | solution.py:311
  145.3 3.0 %collective-permute-start.18 = (bf16[256,1024]{1,0:T(8,128)(2,1)}, bf16[256,1024]{1,0:T(8,128)(2,1)}, u32[]{:S(2)}, u32[]{:S(2)}) collective-permute-start(bf16[256,1024]{1,0:T(8,128)(2,1)} %copy-done.20), channel_id=1, source_target_pairs={{0,64},{32,96},{64,0},{96,32},{1,65},{33,97},{65,1},{97,33},{2,66}... | collective-permute-start | bytes 1572872 | tf_op jit(solution)/shard_map/ppermute | solution.py:302
  148.2 2.7 %fusion = bf16[64,8,1024]{2,1,0:T(8,128)(2,1)} fusion(bf16[512,1024]{1,0:T(8,128)(2,1)} %collective-permute-done.10, bf16[512,1024]{1,0:T(8,128)(2,1)S(1)} %get-tuple-element.35), kind=kLoop, calls=%fused_computation.2 | loop fusion | flops 2097152 | bytes 3145728 | tf_op jit(solution)/shard_map/reshape | solution.py:310
  150.9 11.4 %all-to-all-done.3 = bf16[64,8,1024]{2,1,0:T(8,128)(2,1)S(1)} async-done(((bf16[64,8,1024]{2,1,0:T(8,128)(2,1)}), bf16[64,8,1024]{2,1,0:T(8,128)(2,1)S(1)}, u32[]{:S(2)}, u32[]{:S(2)}) %all-to-all-start.3) | async-done | bytes 1048608 | tf_op jit(solution)/shard_map/all_to_all | solution.py:311
  162.4 5.9 %all-to-all-start.2 = ((bf16[64,8,1024]{2,1,0:T(8,128)(2,1)}), bf16[64,8,1024]{2,1,0:T(8,128)(2,1)S(1)}, u32[]{:S(2)}, u32[]{:S(2)}) async-start(bf16[64,8,1024]{2,1,0:T(8,128)(2,1)} %fusion), calls=%async_computation.2 | async-start | bytes 2097152 | tf_op jit(solution)/shard_map/all_to_all | solution.py:311
  168.3 2.8 %collective-permute-start.17 = (bf16[256,1024]{1,0:T(8,128)(2,1)}, bf16[256,1024]{1,0:T(8,128)(2,1)S(1)}, u32[]{:S(2)}, u32[]{:S(2)}) collective-permute-start(bf16[256,1024]{1,0:T(8,128)(2,1)} %copy-done.19), channel_id=1, source_target_pairs={{0,96},{32,0},{64,32},{96,64},{1,97},{33,1},{65,33},{97,65},{2,98}... | collective-permute-start | bytes 1572872 | tf_op jit(solution)/shard_map/ppermute | solution.py:302
  177.0 15.7 %collective-permute-done.17.refs_1_ = bf16[256,1024]{1,0:T(8,128)(2,1)S(1)} collective-permute-done((bf16[256,1024]{1,0:T(8,128)(2,1)}, bf16[256,1024]{1,0:T(8,128)(2,1)S(1)}, u32[]{:S(2)}, u32[]{:S(2)}) %collective-permute-start.17) | collective-permute-done | bytes 524320 | tf_op jit(solution)/shard_map/ppermute | solution.py:302
  192.7 3.3 %collective-permute-start.13 = (bf16[16,1024]{1,0:T(8,128)(2,1)S(1)}, bf16[16,1024]{1,0:T(8,128)(2,1)S(1)}, u32[]{:S(2)}, u32[]{:S(2)}) collective-permute-start(bf16[16,1024]{1,0:T(8,128)(2,1)S(1)} %get-tuple-element.62), channel_id=1, source_target_pairs={{16,0},{32,16},{48,32},{64,48},{80,64},{96,80},{112,96},{17,1},{33... | collective-permute-start | bytes 98312 | tf_op jit(solution)/shard_map/ppermute | solution.py:296
  196.0 9.5 %collective-permute-start.12 = (bf16[16,1024]{1,0:T(8,128)(2,1)S(1)}, bf16[16,1024]{1,0:T(8,128)(2,1)S(1)}, u32[]{:S(2)}, u32[]{:S(2)}) collective-permute-start(bf16[16,1024]{1,0:T(8,128)(2,1)S(1)} %get-tuple-element.63), channel_id=1, source_target_pairs={{0,16},{16,32},{32,48},{48,64},{64,80},{80,96},{96,112},{1,17},{17... | collective-permute-start | bytes 98312 | tf_op jit(solution)/shard_map/ppermute | solution.py:295
  205.6 4.0 %place_grads.3 = f32[4,256,1024]{2,1,0:T(8,128)} custom-call(s32[4]{0:T(128)S(1)} %pad_add_fusion.spots_ref, f32[256,1024]{1,0:T(8,128)S(1)} %copy-done.1, bf16[256,1024]{1,0:T(8,128)(2,1)S(1)} %collective-permute-done.17.refs_1_, bf16[256,1024]{1,0:T(8,128)(2,1)} %collective-permute-done.18.refs_2_, bf16[256,1024]{1,0:T(8,128)(2,1)S(1)} %collective-permute-done.19.refs_3_), custom_call_target="tpu_custom_call" | custom-call | flops 1048576 | bytes 7340032 | tf_op jit(solution)/shard_map/place_grads/pallas_call | solution.py:274
  209.6 5.6 %collective-permute-done.14.refs_1_ = bf16[1024,256]{1,0:T(8,128)(2,1)S(1)} collective-permute-done((bf16[1024,256]{1,0:T(8,128)(2,1)}, bf16[1024,256]{1,0:T(8,128)(2,1)S(1)}, u32[]{:S(2)}, u32[]{:S(2)}) %collective-permute-start.14) | collective-permute-done | bytes 524320 | tf_op jit(solution)/shard_map/ppermute | solution.py:302
  216.5 3.0 %place_grads.2 = f32[4,1024,256]{2,1,0:T(8,128)} custom-call(s32[4]{0:T(128)S(1)} %pad_add_fusion.spots_ref, f32[1024,256]{1,0:T(8,128)S(1)} %get-tuple-element.46.refs_0_, bf16[1024,256]{1,0:T(8,128)(2,1)S(1)} %collective-permute-done.14.refs_1_, bf16[1024,256]{1,0:T(8,128)(2,1)S(1)} %collective-permute-done.15.refs_2_, ...), custom_call_target="tpu_custom_call" | custom-call | flops 1048576 | bytes 7340032 | tf_op jit(solution)/shard_map/place_grads/pallas_call | solution.py:274
  221.0 3.4 %conv_down.1 = bf16[128,1024]{1,0:T(8,128)(2,1)} custom-call(bf16[16,1024]{1,0:T(8,128)(2,1)S(1)} %collective-permute-done.12.low_ref, bf16[128,1024]{1,0:T(8,128)(2,1)S(1)} %copy-done.9, bf16[16,1024]{1,0:T(8,128)(2,1)S(1)} %collective-permute-done.13.high_ref, f32[31,1024]{1,0:T(8,128)S(1)} %copy-done.13, f32[128,1024]{1,0:T(8,128)S(1)} %copy-done.5), custom_call_target="tpu_custom_call" | custom-call | flops 134217728 | bytes 2097152 | tf_op jit(solution)/shard_map/conv_down/pallas_call | solution.py:252
  (86 shorter events, 24.1 us)
Async XLA Ops:
  0.6 29.5 %copy-start.12 = (f32[31,1024]{1,0:T(8,128)S(1)}, f32[31,1024]{1,0:T(8,128)}, u32[]{:S(2)}) copy-start(f32[31,1024]{1,0:T(8,128)} %kernel_ref.3) | copy-start | bytes 380932
  3.2 13.0 %copy-start.14 = (bf16[1,128,1024]{2,1,0:T(8,128)(2,1)S(1)}, bf16[1,128,1024]{2,1,0:T(8,128)(2,1)}, u32[]{:S(2)}) copy-start(bf16[1,128,1024]{2,1,0:T(8,128)(2,1)} %param.7) | copy-start | bytes 786436
  5.3 31.0 %all-to-all-start.1 = ((bf16[64,8,1024]{2,1,0:T(8,128)(2,1)}), bf16[64,8,1024]{2,1,0:T(8,128)(2,1)S(1)}, u32[]{:S(2)}, u32[]{:S(2)}) async-start(bf16[64,8,1024]{2,1,0:T(8,128)(2,1)} %bitcast.8), calls=%async_computation.1 | async-start | bytes 2097152 | tf_op jit(solution)/shard_map/all_to_all | solution.py:311
  16.2 13.8 %collective-permute-start.1 = (bf16[16,1024]{1,0:T(8,128)(2,1)S(1)}, bf16[16,1024]{1,0:T(8,128)(2,1)S(1)}, u32[]{:S(2)}, u32[]{:S(2)}) collective-permute-start(bf16[16,1024]{1,0:T(8,128)(2,1)S(1)} %get-tuple-element.64), channel_id=1, source_target_pairs={{16,0},{32,16},{48,32},{64,48},{80,64},{96,80},{112,96},{17,1},{33... | collective-permute-start | bytes 98312 | tf_op jit(solution)/shard_map/ppermute | solution.py:296
  19.4 10.7 %collective-permute-start = (bf16[16,1024]{1,0:T(8,128)(2,1)S(1)}, bf16[16,1024]{1,0:T(8,128)(2,1)S(1)}, u32[]{:S(2)}, u32[]{:S(2)}) collective-permute-start(bf16[16,1024]{1,0:T(8,128)(2,1)S(1)} %get-tuple-element.65), channel_id=1, source_target_pairs={{0,16},{16,32},{32,48},{48,64},{64,80},{80,96},{96,112},{1,17},{17... | collective-permute-start | bytes 98312 | tf_op jit(solution)/shard_map/ppermute | solution.py:295
  36.3 29.6 %copy-start.23 = (bf16[64,8,1024]{2,1,0:T(8,128)(2,1)}, bf16[64,8,1024]{2,1,0:T(8,128)(2,1)S(1)}, u32[]{:S(2)}) copy-start(bf16[64,8,1024]{2,1,0:T(8,128)(2,1)S(1)} %all-to-all-done.1) | copy-start | bytes 3145732
  36.3 27.3 %all-to-all-start = ((bf16[64,8,1024]{2,1,0:T(8,128)(2,1)}), bf16[64,8,1024]{2,1,0:T(8,128)(2,1)S(1)}, u32[]{:S(2)}, u32[]{:S(2)}) async-start(bf16[64,8,1024]{2,1,0:T(8,128)(2,1)} %bitcast.5), calls=%async_computation | async-start | bytes 2097152 | tf_op jit(solution)/shard_map/all_to_all | solution.py:311
  45.9 47.0 %collective-permute-start.3 = (bf16[512,1024]{1,0:T(8,128)(2,1)S(1)}, bf16[512,1024]{1,0:T(8,128)(2,1)}, u32[]{:S(2)}, u32[]{:S(2)}) collective-permute-start(bf16[512,1024]{1,0:T(8,128)(2,1)S(1)} %bitcast.56), channel_id=1, source_target_pairs={{0,16},{16,0},{1,17},{17,1},{2,18},{18,2},{3,19},{19,3},{4,20},{20... | collective-permute-start | bytes 3145736 | tf_op jit(solution)/shard_map/ppermute | solution.py:306
  63.6 29.7 %collective-permute-start.2 = (bf16[512,1024]{1,0:T(8,128)(2,1)S(1)}, bf16[512,1024]{1,0:T(8,128)(2,1)S(1)}, u32[]{:S(2)}, u32[]{:S(2)}) collective-permute-start(bf16[512,1024]{1,0:T(8,128)(2,1)S(1)} %bitcast.42), channel_id=1, source_target_pairs={{0,16},{16,0},{1,17},{17,1},{2,18},{18,2},{3,19},{19,3},{4,20},{20... | collective-permute-start | bytes 3145736 | tf_op jit(solution)/shard_map/ppermute | solution.py:306
  65.8 15.0 %collective-permute-start.6 = (bf16[1024,256]{1,0:T(8,128)(2,1)S(1)}, bf16[1024,256]{1,0:T(8,128)(2,1)S(1)}, u32[]{:S(2)}, u32[]{:S(2)}) collective-permute-start(bf16[1024,256]{1,0:T(8,128)(2,1)S(1)} %get-tuple-element.61), channel_id=1, source_target_pairs={{0,64},{32,96},{64,0},{96,32},{1,65},{33,97},{65,1},{97,33},{2,66}... | collective-permute-start | bytes 1572872 | tf_op jit(solution)/shard_map/ppermute | solution.py:302
  66.8 25.2 %collective-permute-start.7 = (bf16[256,1024]{1,0:T(8,128)(2,1)S(1)}, bf16[256,1024]{1,0:T(8,128)(2,1)S(1)}, u32[]{:S(2)}, u32[]{:S(2)}) collective-permute-start(bf16[256,1024]{1,0:T(8,128)(2,1)S(1)} %get-tuple-element.57), channel_id=1, source_target_pairs={{0,64},{32,96},{64,0},{96,32},{1,65},{33,97},{65,1},{97,33},{2,66}... | collective-permute-start | bytes 1572872 | tf_op jit(solution)/shard_map/ppermute | solution.py:302
  69.1 34.6 %collective-permute-start.4 = (bf16[1024,256]{1,0:T(8,128)(2,1)S(1)}, bf16[1024,256]{1,0:T(8,128)(2,1)S(1)}, u32[]{:S(2)}, u32[]{:S(2)}) collective-permute-start(bf16[1024,256]{1,0:T(8,128)(2,1)S(1)} %get-tuple-element.59), channel_id=1, source_target_pairs={{0,32},{32,64},{64,96},{96,0},{1,33},{33,65},{65,97},{97,1},{2,34}... | collective-permute-start | bytes 1572872 | tf_op jit(solution)/shard_map/ppermute | solution.py:302
  80.8 34.1 %collective-permute-start.5 = (bf16[256,1024]{1,0:T(8,128)(2,1)S(1)}, bf16[256,1024]{1,0:T(8,128)(2,1)S(1)}, u32[]{:S(2)}, u32[]{:S(2)}) collective-permute-start(bf16[256,1024]{1,0:T(8,128)(2,1)S(1)} %get-tuple-element.55), channel_id=1, source_target_pairs={{0,32},{32,64},{64,96},{96,0},{1,33},{33,65},{65,97},{97,1},{2,34}... | collective-permute-start | bytes 1572872 | tf_op jit(solution)/shard_map/ppermute | solution.py:302
  92.1 28.6 %collective-permute-start.8 = (bf16[1024,256]{1,0:T(8,128)(2,1)S(1)}, bf16[1024,256]{1,0:T(8,128)(2,1)S(1)}, u32[]{:S(2)}, u32[]{:S(2)}) collective-permute-start(bf16[1024,256]{1,0:T(8,128)(2,1)S(1)} %get-tuple-element.58), channel_id=1, source_target_pairs={{0,96},{32,0},{64,32},{96,64},{1,97},{33,1},{65,33},{97,65},{2,98}... | collective-permute-start | bytes 1572872 | tf_op jit(solution)/shard_map/ppermute | solution.py:302
  92.8 27.9 %collective-permute-start.9 = (bf16[256,1024]{1,0:T(8,128)(2,1)S(1)}, bf16[256,1024]{1,0:T(8,128)(2,1)S(1)}, u32[]{:S(2)}, u32[]{:S(2)}) collective-permute-start(bf16[256,1024]{1,0:T(8,128)(2,1)S(1)} %get-tuple-element.54), channel_id=1, source_target_pairs={{0,96},{32,0},{64,32},{96,64},{1,97},{33,1},{65,33},{97,65},{2,98}... | collective-permute-start | bytes 1572872 | tf_op jit(solution)/shard_map/ppermute | solution.py:302
  93.3 27.4 %copy-start.15 = (bf16[512,1024]{1,0:T(8,128)(2,1)}, bf16[512,1024]{1,0:T(8,128)(2,1)S(1)}, u32[]{:S(2)}) copy-start(bf16[512,1024]{1,0:T(8,128)(2,1)S(1)} %collective-permute-done.2.ub) | copy-start | bytes 3145732
  124.8 4.8 %copy-start.18 = (bf16[1024,256]{1,0:T(8,128)(2,1)}, bf16[1024,256]{1,0:T(8,128)(2,1)S(1)}, u32[]{:S(2)}) copy-start(bf16[1024,256]{1,0:T(8,128)(2,1)S(1)} %get-tuple-element.49) | copy-start | bytes 1572868
  133.9 3.8 %collective-permute-start.11 = (bf16[512,1024]{1,0:T(8,128)(2,1)}, bf16[512,1024]{1,0:T(8,128)(2,1)S(1)}, u32[]{:S(2)}, u32[]{:S(2)}) collective-permute-start(bf16[512,1024]{1,0:T(8,128)(2,1)} %get-tuple-element.43), channel_id=1, source_target_pairs={{0,16},{16,0},{1,17},{17,1},{2,18},{18,2},{3,19},{19,3},{4,20},{20... | collective-permute-start | bytes 3145736 | tf_op jit(solution)/shard_map/ppermute | solution.py:306
  137.7 10.5 %collective-permute-start.10 = (bf16[512,1024]{1,0:T(8,128)(2,1)}, bf16[512,1024]{1,0:T(8,128)(2,1)}, u32[]{:S(2)}, u32[]{:S(2)}) collective-permute-start(bf16[512,1024]{1,0:T(8,128)(2,1)} %get-tuple-element.36), channel_id=1, source_target_pairs={{0,16},{16,0},{1,17},{17,1},{2,18},{18,2},{3,19},{19,3},{4,20},{20... | collective-permute-start | bytes 3145736 | tf_op jit(solution)/shard_map/ppermute | solution.py:306
  139.1 23.2 %all-to-all-start.3 = ((bf16[64,8,1024]{2,1,0:T(8,128)(2,1)}), bf16[64,8,1024]{2,1,0:T(8,128)(2,1)S(1)}, u32[]{:S(2)}, u32[]{:S(2)}) async-start(bf16[64,8,1024]{2,1,0:T(8,128)(2,1)} %fusion.1), calls=%async_computation.3 | async-start | bytes 2097152 | tf_op jit(solution)/shard_map/all_to_all | solution.py:311
  145.3 28.6 %collective-permute-start.18 = (bf16[256,1024]{1,0:T(8,128)(2,1)}, bf16[256,1024]{1,0:T(8,128)(2,1)}, u32[]{:S(2)}, u32[]{:S(2)}) collective-permute-start(bf16[256,1024]{1,0:T(8,128)(2,1)} %copy-done.20), channel_id=1, source_target_pairs={{0,64},{32,96},{64,0},{96,32},{1,65},{33,97},{65,1},{97,33},{2,66}... | collective-permute-start | bytes 1572872 | tf_op jit(solution)/shard_map/ppermute | solution.py:302
  148.2 26.2 %copy-start.3 = (bf16[1,128,1024]{2,1,0:T(8,128)(2,1)S(1)}, bf16[1,128,1024]{2,1,0:T(8,128)(2,1)}, u32[]{:S(2)}) copy-start(bf16[1,128,1024]{2,1,0:T(8,128)(2,1)} %param.13) | copy-start | bytes 786436
  162.4 57.1 %all-to-all-start.2 = ((bf16[64,8,1024]{2,1,0:T(8,128)(2,1)}), bf16[64,8,1024]{2,1,0:T(8,128)(2,1)S(1)}, u32[]{:S(2)}, u32[]{:S(2)}) async-start(bf16[64,8,1024]{2,1,0:T(8,128)(2,1)} %fusion), calls=%async_computation.2 | async-start | bytes 2097152 | tf_op jit(solution)/shard_map/all_to_all | solution.py:311
  168.3 37.2 %copy-start.1 = (f32[256,1024]{1,0:T(8,128)S(1)}, f32[256,1024]{1,0:T(8,128)}, u32[]{:S(2)}) copy-start(f32[256,1024]{1,0:T(8,128)} %copy-done) | copy-start | bytes 3145732
  168.3 24.3 %collective-permute-start.17 = (bf16[256,1024]{1,0:T(8,128)(2,1)}, bf16[256,1024]{1,0:T(8,128)(2,1)S(1)}, u32[]{:S(2)}, u32[]{:S(2)}) collective-permute-start(bf16[256,1024]{1,0:T(8,128)(2,1)} %copy-done.19), channel_id=1, source_target_pairs={{0,96},{32,0},{64,32},{96,64},{1,97},{33,1},{65,33},{97,65},{2,98}... | collective-permute-start | bytes 1572872 | tf_op jit(solution)/shard_map/ppermute | solution.py:302
  171.1 24.8 %collective-permute-start.19 = (bf16[256,1024]{1,0:T(8,128)(2,1)}, bf16[256,1024]{1,0:T(8,128)(2,1)S(1)}, u32[]{:S(2)}, u32[]{:S(2)}) collective-permute-start(bf16[256,1024]{1,0:T(8,128)(2,1)} %copy-done.21), channel_id=1, source_target_pairs={{0,32},{32,64},{64,96},{96,0},{1,33},{33,65},{65,97},{97,1},{2,34}... | collective-permute-start | bytes 1572872 | tf_op jit(solution)/shard_map/ppermute | solution.py:302
  171.1 38.5 %collective-permute-start.15 = (bf16[1024,256]{1,0:T(8,128)(2,1)}, bf16[1024,256]{1,0:T(8,128)(2,1)S(1)}, u32[]{:S(2)}, u32[]{:S(2)}) collective-permute-start(bf16[1024,256]{1,0:T(8,128)(2,1)} %copy-done.16), channel_id=1, source_target_pairs={{0,64},{32,96},{64,0},{96,32},{1,65},{33,97},{65,1},{97,33},{2,66}... | collective-permute-start | bytes 1572872 | tf_op jit(solution)/shard_map/ppermute | solution.py:302
  172.8 42.4 %collective-permute-start.14 = (bf16[1024,256]{1,0:T(8,128)(2,1)}, bf16[1024,256]{1,0:T(8,128)(2,1)S(1)}, u32[]{:S(2)}, u32[]{:S(2)}) collective-permute-start(bf16[1024,256]{1,0:T(8,128)(2,1)} %copy-done.17), channel_id=1, source_target_pairs={{0,96},{32,0},{64,32},{96,64},{1,97},{33,1},{65,33},{97,65},{2,98}... | collective-permute-start | bytes 1572872 | tf_op jit(solution)/shard_map/ppermute | solution.py:302
  173.8 42.7 %collective-permute-start.16 = (bf16[1024,256]{1,0:T(8,128)(2,1)}, bf16[1024,256]{1,0:T(8,128)(2,1)S(1)}, u32[]{:S(2)}, u32[]{:S(2)}) collective-permute-start(bf16[1024,256]{1,0:T(8,128)(2,1)} %copy-done.18), channel_id=1, source_target_pairs={{0,32},{32,64},{64,96},{96,0},{1,33},{33,65},{65,97},{97,1},{2,34}... | collective-permute-start | bytes 1572872 | tf_op jit(solution)/shard_map/ppermute | solution.py:302
  177.0 32.6 %copy-start.8 = (bf16[128,1024]{1,0:T(8,128)(2,1)}, bf16[128,1024]{1,0:T(8,128)(2,1)S(1)}, u32[]{:S(2)}) copy-start(bf16[128,1024]{1,0:T(8,128)(2,1)S(1)} %get-tuple-element.44.back_ref) | copy-start | bytes 786436
  192.7 28.3 %collective-permute-start.13 = (bf16[16,1024]{1,0:T(8,128)(2,1)S(1)}, bf16[16,1024]{1,0:T(8,128)(2,1)S(1)}, u32[]{:S(2)}, u32[]{:S(2)}) collective-permute-start(bf16[16,1024]{1,0:T(8,128)(2,1)S(1)} %get-tuple-element.62), channel_id=1, source_target_pairs={{16,0},{32,16},{48,32},{64,48},{80,64},{96,80},{112,96},{17,1},{33... | collective-permute-start | bytes 98312 | tf_op jit(solution)/shard_map/ppermute | solution.py:296
  196.0 25.0 %collective-permute-start.12 = (bf16[16,1024]{1,0:T(8,128)(2,1)S(1)}, bf16[16,1024]{1,0:T(8,128)(2,1)S(1)}, u32[]{:S(2)}, u32[]{:S(2)}) collective-permute-start(bf16[16,1024]{1,0:T(8,128)(2,1)S(1)} %get-tuple-element.63), channel_id=1, source_target_pairs={{0,16},{16,32},{32,48},{48,64},{64,80},{80,96},{96,112},{1,17},{17... | collective-permute-start | bytes 98312 | tf_op jit(solution)/shard_map/ppermute | solution.py:295
  (16 other events, 32.5 us)

commit v2 on v1

v2 whole, which is shorter than its diff:
```python
import jax
import jax.numpy as jnp
from jax import lax
from jax.experimental import pallas as pl
from jax.experimental.pallas import tpu as pltpu
from jax.sharding import Mesh, PartitionSpec as P

KERNEL = 31
MARGIN = (KERNEL - 1) // 2
CAP = 8
EDGE = 16
BF16 = jnp.bfloat16
F32 = jnp.float32


def shape_of(dims, dtype):
    return jax.ShapeDtypeStruct(dims, dtype)


def params(mib):
    return pltpu.CompilerParams(vmem_limit_bytes=mib << 20)


COST = pl.CostEstimate(flops=1, bytes_accessed=1, transcendentals=0)


def silu_slope(values):
    logistic = jax.nn.sigmoid(values)
    return logistic * (1.0 + values * (1.0 - logistic))


def dot(left, right, dims):
    return lax.dot_general(left, right, ((dims[:1], dims[1:]), ((), ())), preferred_element_type=F32)


def slot_masks(routes_ref, experts, n_y):
    length = routes_ref.shape[0]
    n_exp = experts // n_y
    slots = experts * CAP
    routes = routes_ref[...]
    lane = lax.broadcasted_iota(jnp.int32, (length, experts), 1)
    before = (
        lax.broadcasted_iota(jnp.int32, (length, length), 1)
        < lax.broadcasted_iota(jnp.int32, (length, length), 0)
    ).astype(F32).astype(BF16)
    place = lax.broadcasted_iota(jnp.int32, (length, slots), 1)
    base = jnp.zeros((1, experts), F32)
    masks = []
    for choice in range(2):
        expert = routes[:, choice : choice + 1]
        named = (lane == expert).astype(F32)
        earlier = dot(before, named.astype(BF16), (1, 0)) + base
        rank = jnp.sum(named * earlier, axis=1, keepdims=True).astype(jnp.int32)
        base = base + jnp.sum(named, axis=0, keepdims=True)
        start = (expert % n_y) * n_exp + expert // n_y
        masks.append((place == start * CAP + rank).astype(F32).astype(BF16))
    return masks


def down_slots(routes, gates, cotangent, experts, n_y):
    length, width = cotangent.shape

    def body(routes_ref, gates_ref, cot_ref, out_ref):
        masks = slot_masks(routes_ref, experts, n_y)
        cot = cot_ref[...].astype(F32)
        gate = gates_ref[...]
        total = None
        for choice in range(2):
            rows = (gate[:, choice : choice + 1] * cot).astype(BF16)
            part = dot(masks[choice], rows, (0, 0))
            total = part if total is None else total + part
        out_ref[...] = total.astype(BF16)

    return pl.pallas_call(
        body,
        grid=(1,),
        in_specs=[
            pl.BlockSpec(routes.shape, lambda i: (0, 0)),
            pl.BlockSpec(gates.shape, lambda i: (0, 0)),
            pl.BlockSpec(cotangent.shape, lambda i: (0, 0)),
        ],
        out_specs=pl.BlockSpec((experts * CAP, width), lambda i: (0, 1)),
        out_shape=shape_of((experts * CAP, 2 * width), BF16),
        compiler_params=params(32),
        cost_estimate=COST,
        name="down_slots",
    )(routes, gates, cotangent)


def tap_sum(pad_ref, kernel_ref, columns, length, reverse):
    padded = pad_ref[:, columns]
    taps = kernel_ref[:, columns]
    total = jnp.zeros((length, padded.shape[1]), F32)
    for residue in range(8):
        offsets = [
            tap for tap in range(KERNEL) if (EDGE - MARGIN + tap) % 8 == residue
        ]
        shifted = padded[residue : residue + length + 24, :]
        for tap in offsets:
            start = EDGE - MARGIN + tap - residue
            weight = KERNEL - 1 - tap if reverse else tap
            total = total + taps[weight : weight + 1, :] * shifted[start : start + length, :]
    return total


COLUMNS = 128


def conv_up(low, frames, high, kernel, routes, send, experts, n_y):
    length, width = frames.shape
    slots = experts * CAP

    def body(low_ref, frames_ref, high_ref, kernel_ref, routes_ref, _, mix_ref, hid_ref, out_ref, pad):
        pad[:EDGE] = low_ref[...].astype(F32)
        pad[EDGE : EDGE + length] = frames_ref[...].astype(F32)
        pad[EDGE + length :] = high_ref[...].astype(F32)

        def step(index, carry):
            columns = pl.ds(pl.multiple_of(index * COLUMNS, COLUMNS), COLUMNS)
            mixing = tap_sum(pad, kernel_ref, columns, length, False)
            mix_ref[:, columns] = mixing
            own = pad[EDGE : EDGE + length, columns]
            hid_ref[:, columns] = (own + mixing * jax.nn.sigmoid(mixing)).astype(BF16)
            return carry

        lax.fori_loop(0, width // COLUMNS, step, 0)
        first, second = slot_masks(routes_ref, experts, n_y)
        out_ref[...] = dot(first + second, hid_ref[...], (0, 0)).astype(BF16)

    operands = (low, frames, high, kernel, routes)
    return pl.pallas_call(
        body,
        grid=(1,),
        in_specs=[pl.BlockSpec(o.shape, lambda i: (0, 0)) for o in operands]
        + [pl.BlockSpec(memory_space=pl.ANY)],
        out_specs=(
            pl.BlockSpec((length, width), lambda i: (0, 0)),
            pl.BlockSpec((length, width), lambda i: (0, 0)),
            pl.BlockSpec((slots, width), lambda i: (0, 0)),
        ),
        out_shape=(
            shape_of((length, width), F32),
            shape_of((length, width), BF16),
            shape_of((slots, 2 * width), BF16),
        ),
        input_output_aliases={5: 2},
        scratch_shapes=[pltpu.VMEM((length + 2 * EDGE, width), F32)],
        compiler_params=params(32),
        cost_estimate=COST,
        name="conv_up",
    )(*operands, send)


TILE = 256


def copy_all(copies):
    for copy in copies:
        copy.start()
    for copy in copies:
        copy.wait()


def pack_weights(spots, w_in, w_out):
    _, width, hidden = w_in.shape
    pieces = width // hidden
    half = width // 2

    def body(spots_ref, in_ref, out_ref, own_ref, first_up, first_down, next_up, next_down, sems):
        copies = []

        def move(source, target):
            copies.append(pltpu.make_async_copy(source, target, sems.at[len(copies)]))

        def pack(steps, low, high, ref, offset):
            spot = spots_ref[steps]
            move(
                in_ref.at[spot, pl.ds(low, high - low)],
                ref.at[pl.ds(offset, high - low), :hidden],
            )
            for start in range(low, high, hidden):
                move(
                    out_ref.at[spot, :, pl.ds(start, hidden)],
                    ref.at[pl.ds(offset + start - low, hidden), hidden:],
                )

        pack(2, 0, half, first_up, 0)
        pack(2, half, width, first_down, 0)
        pack(1, 0, width, next_up, half)
        pack(3, 0, width, next_down, half)
        pack(0, 0, width, own_ref, 0)
        copy_all(copies)

    rows = (width, half, half, width + half, width + half)
    return pl.pallas_call(
        body,
        in_specs=[pl.BlockSpec(memory_space=pltpu.SMEM)] + [pl.BlockSpec(memory_space=pl.ANY)] * 2,
        out_specs=[pl.BlockSpec(memory_space=pl.ANY)] * len(rows),
        out_shape=[shape_of((count, 2 * hidden), BF16) for count in rows],
        scratch_shapes=[pltpu.SemaphoreType.DMA((4 * (1 + pieces) + 1,))],
        compiler_params=params(16),
        cost_estimate=COST,
        name="pack_weights",
    )(spots, w_in, w_out)


def fill_first(parts, wholes):
    count = parts[0].shape[0]

    def body(*refs):
        sems = refs[-1]
        copy_all(
            [
                pltpu.make_async_copy(refs[i], refs[4 + i].at[:count], sems.at[i])
                for i in range(2)
            ]
        )

    return pl.pallas_call(
        body,
        in_specs=[pl.BlockSpec(memory_space=pl.ANY)] * 4,
        out_specs=[pl.BlockSpec(memory_space=pl.ANY)] * 2,
        out_shape=[shape_of(whole.shape, BF16) for whole in wholes],
        input_output_aliases={2: 0, 3: 1},
        scratch_shapes=[pltpu.SemaphoreType.DMA((2,))],
        compiler_params=params(16),
        cost_estimate=COST,
        name="fill_first",
    )(*parts, *wholes)


def half_specs(halves):
    rows = []
    for array, index in halves:
        block = (array.shape[1], array.shape[1])
        rows.append(pl.BlockSpec(block, lambda i, index=index: (index, 0)))
    return rows


def whole_spec(array):
    return pl.BlockSpec(array.shape, lambda i: (0, 0))


def split_in(lows, halves, hidden):
    total = None
    step = halves[0].shape[0]
    for index, ref in enumerate(halves):
        part = dot(lows[:, index * step : (index + 1) * step], ref[:, :hidden], (1, 0))
        total = part if total is None else total + part
    return total


def out_piece(halves, piece, hidden):
    step = halves[0].shape[0]
    ref = halves[piece // step]
    start = piece % step
    return ref[start : start + hidden, hidden:]


def activate(rows, refs, halves, act_ref, pre_ref):
    hidden = halves[0].shape[1] // 2
    width = refs[0].shape[1] // 2
    for half, ref in enumerate(refs):
        for start in range(0, rows, TILE):
            part = slice(start, start + TILE)
            held = slice(half * rows + start, half * rows + start + TILE)
            pre = split_in(ref[part, :width], halves, hidden)
            logistic = jax.nn.sigmoid(pre)
            act_ref[held, :] = (pre * logistic).astype(BF16)
            back = None
            for piece in range(0, width, hidden):
                term = dot(
                    ref[part, width + piece : width + piece + hidden],
                    out_piece(halves, piece, hidden),
                    (1, 1),
                )
                back = term if back is None else back + term
            slope = logistic * (1.0 + pre * (1.0 - logistic))
            pre_ref[held, :] = (back * slope).astype(BF16)


def weigh(rows, refs, act_ref, pre_ref, grad_ref):
    width, hidden = grad_ref.shape[0], grad_ref.shape[1] // 2
    first, second = refs
    for piece in range(0, width, hidden):
        part = slice(piece, piece + hidden)
        shifted = slice(width + piece, width + piece + hidden)
        out = dot(act_ref[:rows, :], first[:, shifted], (0, 0))
        out = out + dot(act_ref[rows:, :], second[:, shifted], (0, 0))
        grad_ref[part, hidden:] = out.astype(grad_ref.dtype)
        out = dot(first[:, part], pre_ref[:rows, :], (0, 0))
        out = out + dot(second[:, part], pre_ref[rows:, :], (0, 0))
        grad_ref[part, :hidden] = out.astype(grad_ref.dtype)


def block_step(own, other, halves, grad_type):
    rows, width = own.shape[0], own.shape[1] // 2
    hidden = halves[0][0].shape[1] // 2
    result = [shape_of((2 * rows, hidden), BF16), shape_of((2 * rows, hidden), BF16)]
    if grad_type is not None:
        result.append(shape_of((width, 2 * hidden), grad_type))

    def body(own_ref, other_ref, low_ref, high_ref, act_ref, pre_ref, *grads):
        activate(rows, (own_ref, other_ref), (low_ref, high_ref), act_ref, pre_ref)
        for grad_ref in grads:
            weigh(rows, (own_ref, other_ref), act_ref, pre_ref, grad_ref)

    return pl.pallas_call(
        body,
        grid=(1,),
        in_specs=[whole_spec(own), whole_spec(other)] + half_specs(halves),
        out_specs=[whole_spec(array) for array in result],
        out_shape=result,
        compiler_params=params(48),
        cost_estimate=COST,
        name="block_step",
    )(own, other, *[array for array, _ in halves])


def block_grads(own, other, act, pre, grad_type):
    rows, width = own.shape[0], own.shape[1] // 2
    hidden = act.shape[1]

    def body(own_ref, other_ref, act_ref, pre_ref, grad_ref):
        weigh(rows, (own_ref, other_ref), act_ref, pre_ref, grad_ref)

    return pl.pallas_call(
        body,
        out_shape=shape_of((width, 2 * hidden), grad_type),
        compiler_params=params(48),
        cost_estimate=COST,
        name="block_grads",
    )(own, other, act, pre)


def back_to_width(half, acts, pres, packed, arrived):
    hidden = acts[0].shape[1]
    rows = acts[0].shape[0] // 2
    count = len(acts)
    width = hidden * count
    extra = [] if arrived is None else [arrived]

    def body(*refs):
        act_refs, pre_refs = refs[:count], refs[count : 2 * count]
        w_refs = [refs[2 * count + 2 * i : 2 * count + 2 * i + 2] for i in range(count)]
        out_ref = refs[-1]
        for start in range(0, rows, TILE):
            held = slice(start, start + TILE)

            def emit(columns, total):
                if extra:
                    total = total + refs[4 * count][held, columns].astype(F32)
                out_ref[held, columns] = total.astype(BF16)

            for piece in range(0, width, hidden):
                total = None
                for part_ref, halves in zip(act_refs, w_refs):
                    part = dot(part_ref[held, :], out_piece(halves, piece, hidden), (1, 0))
                    total = part if total is None else total + part
                emit(slice(piece, piece + hidden), total)
            for side in range(2):
                total = None
                for part_ref, halves in zip(pre_refs, w_refs):
                    part = dot(part_ref[held, :], halves[side][:, :hidden], (1, 1))
                    total = part if total is None else total + part
                step = width // 2
                emit(slice(width + side * step, width + (side + 1) * step), total)

    one = pl.BlockSpec((rows, hidden), lambda i: (half, 0))
    result = shape_of((rows, 2 * width), BF16)
    listed = [pair for halves in packed for pair in halves]
    return pl.pallas_call(
        body,
        grid=(1,),
        in_specs=[one] * (2 * count) + half_specs(listed) + [whole_spec(result)] * len(extra),
        out_specs=whole_spec(result),
        out_shape=result,
        compiler_params=params(48),
        cost_estimate=COST,
        name="back_to_width",
    )(*acts, *pres, *[array for array, _ in listed], *extra)


def mix_out(routes, gates, hidden, returned, experts, n_y):
    def body(routes_ref, gates_ref, hid_ref, out_ref, mixed_ref):
        masks = slot_masks(routes_ref, experts, n_y)
        gate = gates_ref[...]
        total = hid_ref[...].astype(F32)
        for choice in range(2):
            total = total + gate[:, choice : choice + 1] * dot(masks[choice], out_ref[...], (1, 0))
        mixed_ref[...] = total.astype(BF16)

    return pl.pallas_call(
        body,
        grid=(1,),
        in_specs=[
            pl.BlockSpec(routes.shape, lambda i: (0, 0)),
            pl.BlockSpec(gates.shape, lambda i: (0, 0)),
            pl.BlockSpec(hidden.shape, lambda i: (0, 0)),
            pl.BlockSpec((returned.shape[0], hidden.shape[1]), lambda i: (0, 0)),
        ],
        out_specs=pl.BlockSpec(hidden.shape, lambda i: (0, 0)),
        out_shape=shape_of(hidden.shape, BF16),
        compiler_params=params(32),
        cost_estimate=COST,
        name="mix_out",
    )(routes, gates, hidden, returned)


def grad_rows(routes, cotangent, mixing, returned, experts, n_y):
    def body(routes_ref, cot_ref, mix_ref, grad_ref, hidden_ref, back_ref):
        first, second = slot_masks(routes_ref, experts, n_y)
        grad = cot_ref[...].astype(F32) + dot(first + second, grad_ref[...], (1, 0))
        hidden_ref[...] = grad
        back_ref[...] = (grad * silu_slope(mix_ref[...])).astype(BF16)

    return pl.pallas_call(
        body,
        grid=(1,),
        in_specs=[
            pl.BlockSpec(routes.shape, lambda i: (0, 0)),
            pl.BlockSpec(cotangent.shape, lambda i: (0, 0)),
            pl.BlockSpec(mixing.shape, lambda i: (0, 0)),
            pl.BlockSpec((returned.shape[0], mixing.shape[1]), lambda i: (0, 1)),
        ],
        out_specs=(
            pl.BlockSpec(cotangent.shape, lambda i: (0, 0)),
            pl.BlockSpec(cotangent.shape, lambda i: (0, 0)),
        ),
        out_shape=(shape_of(cotangent.shape, F32), shape_of(cotangent.shape, BF16)),
        compiler_params=params(32),
        cost_estimate=COST,
        name="grad_rows",
    )(routes, cotangent, mixing, returned)


def conv_down(low, back, high, kernel, hidden_grad):
    length, width = back.shape

    def body(low_ref, back_ref, high_ref, kernel_ref, grad_ref, out_ref, pad):
        pad[:EDGE] = low_ref[...].astype(F32)
        pad[EDGE : EDGE + length] = back_ref[...].astype(F32)
        pad[EDGE + length :] = high_ref[...].astype(F32)

        def step(index, carry):
            columns = pl.ds(pl.multiple_of(index * COLUMNS, COLUMNS), COLUMNS)
            spread = tap_sum(pad, kernel_ref, columns, length, True)
            out_ref[:, columns] = (grad_ref[:, columns] + spread).astype(BF16)
            return carry

        lax.fori_loop(0, width // COLUMNS, step, 0)

    return pl.pallas_call(
        body,
        out_shape=shape_of((length, width), BF16),
        scratch_shapes=[pltpu.VMEM((length + 2 * EDGE, width), F32)],
        compiler_params=params(32),
        cost_estimate=COST,
        name="conv_down",
    )(low, back, high, kernel, hidden_grad)


def place_grads(spot, packed, count, held):
    width, hidden = packed.shape[0], packed.shape[1] // 2

    def body(spot_ref, packed_ref, *refs):
        in_ref, out_ref = refs[-2:]
        in_ref[0] = packed_ref[:, :hidden].astype(F32)
        for piece in range(0, width, hidden):
            part = slice(piece, piece + hidden)
            out_ref[0, :, part] = packed_ref[part, hidden:].astype(F32)

    return pl.pallas_call(
        body,
        grid_spec=pltpu.PrefetchScalarGridSpec(
            num_scalar_prefetch=1,
            grid=(1,),
            in_specs=[pl.BlockSpec(packed.shape, lambda i, spot: (0, 0))]
            + [pl.BlockSpec(memory_space=pl.ANY)] * len(held),
            out_specs=(
                pl.BlockSpec((1, width, hidden), lambda i, spot: (spot[0], 0, 0)),
                pl.BlockSpec((1, hidden, width), lambda i, spot: (spot[0], 0, 0)),
            ),
        ),
        out_shape=(
            shape_of((count, width, hidden), F32),
            shape_of((count, hidden, width), F32),
        ),
        input_output_aliases={2 + index: index for index in range(len(held))},
        compiler_params=params(32),
        cost_estimate=COST,
        name="place_grads",
    )(spot, packed, *held)


def edges(block):
    count = lax.axis_size("y") * lax.axis_size("core")
    forward = [(i, i + 1) for i in range(count - 1)]
    backward = [(target, source) for source, target in forward]
    low = lax.ppermute(block[-EDGE:], ("y", "core"), forward)
    high = lax.ppermute(block[:EDGE], ("y", "core"), backward)
    return low, high


def turn(block, steps):
    count = lax.axis_size("y")
    return lax.ppermute(block, "y", [(i, (i + steps) % count) for i in range(count)])


def swap(block):
    return lax.ppermute(block, "core", [(0, 1), (1, 0)])


def together(rows):
    half = rows.shape[0] // 2
    return jnp.concatenate([swap(rows[:half]), swap(rows[half:])])


def exchange(rows, groups):
    grouped = rows.reshape(groups, CAP, rows.shape[1])
    moved = lax.all_to_all(grouped, ("y", "exp"), split_axis=0, concat_axis=0, tiled=True)
    return moved.reshape(rows.shape)


def per_device(frames, conv_kernel, routes, gates, w_in, w_out, cotangent):
    n_y = lax.axis_size("y")
    n_exp = lax.axis_size("exp")
    groups = n_y * n_exp
    experts = w_in.shape[0] * n_exp
    y = lax.axis_index("y")
    frames, routes, gates, cotangent = frames[0], routes[0], gates[0], cotangent[0]
    spots = (y + jnp.arange(n_y, dtype=jnp.int32)) % n_y

    low, high = edges(frames)
    own_block, first_up, first_down, next_up, next_down = pack_weights(spots, w_in, w_out)
    first_up, first_down = turn(first_up, 1), turn(first_down, -1)

    send = down_slots(routes, gates, cotangent, experts, n_y)
    mixing, hidden, send = conv_up(low, frames, high, conv_kernel, routes, send, experts, n_y)
    send, first_up, first_down = lax.optimization_barrier((send, first_up, first_down))
    own = exchange(send, groups)
    next_up, next_down = fill_first((first_up, first_down), (next_up, next_down))
    next_up, next_down = turn(next_up, 1), turn(next_down, -1)
    other = together(own)

    order = [0, 1, 3, 2]
    acts, pres, grads = {}, {}, {}
    packed = {0: [(own_block, 0), (own_block, 1)]}
    acts[0], pres[0], grads[0] = block_step(own, other, packed[0], F32)
    acts[0], next_up, next_down = lax.optimization_barrier((acts[0], next_up, next_down))
    packed[1] = [(next_up, 1), (next_up, 2)]
    packed[3] = [(next_down, 1), (next_down, 2)]
    packed[2] = [(next_up, 0), (next_down, 0)]
    for steps in (1, 3):
        acts[steps], pres[steps], grads[steps] = block_step(own, other, packed[steps], BF16)
        grads[steps] = turn(grads[steps], -steps)
    acts[2], pres[2] = block_step(own, other, packed[2], None)
    listed = [[held[steps] for steps in order] for held in (acts, pres, packed)]
    arrived = swap(back_to_width(1, *listed, None))
    grads[2] = block_grads(own, other, acts[2], pres[2], BF16)
    arrived, grads[2] = lax.optimization_barrier((arrived, grads[2]))
    grads[2] = turn(grads[2], -2)
    result = back_to_width(0, *listed, arrived)
    result, grads[1], grads[3] = lax.optimization_barrier((result, grads[1], grads[3]))
    returned = exchange(result, groups)

    hidden_grad, back = grad_rows(routes, cotangent, mixing, returned, experts, n_y)
    low, high = edges(back)
    frames_grad = conv_down(low, back, high, conv_kernel, hidden_grad)
    mixed = mix_out(routes, gates, hidden, returned, experts, n_y)

    held = ()
    for steps in order:
        held = place_grads(spots[steps : steps + 1], grads[steps], n_y, held)
    w_in_grad, w_out_grad = held
    return (mixed[None], frames_grad[None], w_in_grad, w_out_grad)


def solution(mesh):
    cores = 2
    n_seq, n_exp = mesh.devices.shape
    split = Mesh(mesh.devices.reshape(n_seq // cores, cores, n_exp), ("y", "core", "exp"))
    seq = ("y", "core")
    in_specs = (
        P("exp", seq, None),
        P(),
        P("exp", seq, None),
        P("exp", seq, None),
        P("exp", None, seq),
        P("exp", seq, None),
        P("exp", seq, None),
    )
    out_specs = (
        P("exp", seq, None),
        P("exp", seq, None),
        P("exp", None, seq),
        P("exp", seq, None),
    )
    return jax.shard_map(
        per_device, mesh=split, in_specs=in_specs, out_specs=out_specs, check_vma=False
    )
```

time: 227 us -> 224 us (0.987)
  the two profiles are of different devices: /device:TPU:5 before, /device:TPU:11 now
where the time goes in v2:
time: 224 us
  waiting for transfers between devices  85.9 us (38%)
  starting transfers between devices  62 us (28%)
  Pallas kernels  59 us (26%)
  local copies, waits for them, and re-layouts  15.9 us (7%)
    all_to_all x2, waiting for transfers between devices, exchange(): lax.all_to_all(grouped, ('y', 'exp'), split_axis=0, concat_axis=0, tiled=...  49 us
    ppermute x7, waiting for transfers between devices, turn(): lax.ppermute(block, 'y', [(i, (i + steps) % count) for i in range(count)])  28.1 us
    ppermute x2, starting transfers between devices, edges(): low = lax.ppermute(block[-EDGE:], ('y', 'core'), forward)  25.5 us
    all_to_all x2, starting transfers between devices, exchange(): lax.all_to_all(grouped, ('y', 'exp'), split_axis=0, concat_axis=0, tiled=...  20.7 us
    pallas_call x4, Pallas kernels, block_step(): pl.pallas_call(body, grid=(1,), in_specs=[whole_spec(own), whole_spec(oth...  18.9 us
    unnamed x51, local copies, waits for them, and re-layouts  13.4 us
    pallas_call x2, Pallas kernels, back_to_width(): pl.pallas_call(body, grid=(1,), in_specs=[one] * (2 * count) + half_specs...  11.8 us
    pallas_call x4, Pallas kernels, place_grads(): pl.pallas_call(body, grid_spec=pltpu.PrefetchScalarGridSpec(num_scalar_pr...  9.41 us
  transfers between devices with their start and end apart: 16, of which 9 were waited for; matrix products, arithmetic and copies ran while one was open for 1% of the time, Pallas kernels for 15%

profile of v2, /device:TPU:11, one launch (start us, length us, event | category | flops | bytes accessed | tf_op | source)
XLA Modules:
  0.0 223.7 jit_solution(13997689650657607471)
XLA Ops:
  0.7 1.6 copy-done.6
  2.2 1.6 copy-done.7
  3.8 2.0 pack_weights.1
  8.4 3.1 %collective-permute-start.1 = (bf16[16,1024]{1,0:T(8,128)(2,1)S(1)}, bf16[16,1024]{1,0:T(8,128)(2,1)S(1)}, u32[]{:S(2)}, u32[]{:S(2)}) collective-permute-start(bf16[16,1024]{1,0:T(8,128)(2,1)S(1)} %get-tuple-element.92), channel_id=1, source_target_pairs={{16,0},{32,16},{48,32},{64,48},{80,64},{96,80},{112,96},{17,1},{33... | collective-permute-start | bytes 98312 | tf_op jit(solution)/shard_map/ppermute | solution.py:501
  11.5 3.1 %collective-permute-start = (bf16[16,1024]{1,0:T(8,128)(2,1)S(1)}, bf16[16,1024]{1,0:T(8,128)(2,1)S(1)}, u32[]{:S(2)}, u32[]{:S(2)}) collective-permute-start(bf16[16,1024]{1,0:T(8,128)(2,1)S(1)} %get-tuple-element.93), channel_id=1, source_target_pairs={{0,16},{16,32},{32,48},{48,64},{64,80},{80,96},{96,112},{1,17},{17... | collective-permute-start | bytes 98312 | tf_op jit(solution)/shard_map/ppermute | solution.py:500
  14.9 2.1 down_slots.1._
  17.0 5.4 %collective-permute-done.1.high_ref = bf16[16,1024]{1,0:T(8,128)(2,1)S(1)} collective-permute-done((bf16[16,1024]{1,0:T(8,128)(2,1)S(1)}, bf16[16,1024]{1,0:T(8,128)(2,1)S(1)}, u32[]{:S(2)}, u32[]{:S(2)}) %collective-permute-start.1) | collective-permute-done | bytes 32800 | tf_op jit(solution)/shard_map/ppermute | solution.py:501
  22.4 4.7 %conv_up.1 = (f32[128,1024]{1,0:T(8,128)S(1)}, bf16[128,1024]{1,0:T(8,128)(2,1)S(1)}, bf16[512,2048]{1,0:T(8,128)(2,1)}) custom-call(bf16[16,1024]{1,0:T(8,128)(2,1)S(1)} %collective-permute-done.low_ref, bf16[128,1024]{1,0:T(8,128)(2,1)S(1)} %bitcast.28, bf16[16,1024]{1,0:T(8,128)(2,1)S(1)} %collective-permute-done.1.high_ref, ...), custom_call_target="tpu_custom_call", output_to_operand_aliasing={{2}: (5, {})} | custom-call | flops 1 | bytes 1 | tf_op jit(solution)/shard_map/conv_up/pallas_call | solution.py:131
  28.6 10.7 %all-to-all-start = ((bf16[64,8,2048]{2,1,0:T(8,128)(2,1)}), bf16[64,8,2048]{2,1,0:T(8,128)(2,1)}, u32[]{:S(2)}, u32[]{:S(2)}) async-start(bf16[64,8,2048]{2,1,0:T(8,128)(2,1)} %bitcast.6), calls=%async_computation | async-start | bytes 4194304 | tf_op jit(solution)/shard_map/all_to_all | solution.py:521
  42.8 24.7 %all-to-all-done = bf16[64,8,2048]{2,1,0:T(8,128)(2,1)} async-done(((bf16[64,8,2048]{2,1,0:T(8,128)(2,1)}), bf16[64,8,2048]{2,1,0:T(8,128)(2,1)}, u32[]{:S(2)}, u32[]{:S(2)}) %all-to-all-start) | async-done | bytes 2097184 | tf_op jit(solution)/shard_map/all_to_all | solution.py:521
  67.5 1.8 slice_bitcast_fusion
  70.0 2.0 collective-permute-done.4
  75.0 4.9 %block_step.4 = (bf16[1024,256]{1,0:T(8,128)(2,1)S(1)}, bf16[1024,256]{1,0:T(8,128)(2,1)S(1)}, f32[1024,512]{1,0:T(8,128)S(1)}) custom-call(bf16[512,2048]{1,0:T(8,128)(2,1)} %bitcast.7.own_ref, bf16[512,2048]{1,0:T(8,128)(2,1)} %copy-done.20, bf16[1024,512]{1,0:T(8,128)(2,1)S(1)} %copy-done.3, bf16[1024,512]{1,0:T(8,128)(2,1)S(1)} %copy-done.3), custom_call_target="tpu_custom_call" | custom-call | flops 1 | bytes 1 | tf_op jit(solution)/shard_map/block_step/pallas_call | solution.py:308
  81.2 15.0 %collective-permute-done.6.low_ref.high_ref.refs_10_.refs_11_.refs_14_ = bf16[1536,512]{1,0:T(8,128)(2,1)S(1)} collective-permute-done((bf16[1536,512]{1,0:T(8,128)(2,1)}, bf16[1536,512]{1,0:T(8,128)(2,1)S(1)}, u32[]{:S(2)}, u32[]{:S(2)}) %collective-permute-start.6) | collective-permute-done | bytes 1572896 | tf_op jit(solution)/shard_map/ppermute | solution.py:507
  97.1 5.5 %block_step.5 = (bf16[1024,256]{1,0:T(8,128)(2,1)S(1)}, bf16[1024,256]{1,0:T(8,128)(2,1)S(1)}, bf16[1024,512]{1,0:T(8,128)(2,1)S(1)}) custom-call(bf16[512,2048]{1,0:T(8,128)(2,1)} %bitcast.7.own_ref, bf16[512,2048]{1,0:T(8,128)(2,1)} %copy-done.20, bf16[1536,512]{1,0:T(8,128)(2,1)S(1)} %collective-permute-done.6.low_ref.high_ref.refs_10_.refs_11_.refs_14_, ...), custom_call_target="tpu_custom_call" | custom-call | flops 1 | bytes 1 | tf_op jit(solution)/shard_map/block_step/pallas_call | solution.py:308
  102.6 3.7 %block_step.7 = (bf16[1024,256]{1,0:T(8,128)(2,1)S(1)}, bf16[1024,256]{1,0:T(8,128)(2,1)S(1)}) custom-call(bf16[512,2048]{1,0:T(8,128)(2,1)} %bitcast.7.own_ref, bf16[512,2048]{1,0:T(8,128)(2,1)} %copy-done.20, bf16[1536,512]{1,0:T(8,128)(2,1)S(1)} %collective-permute-done.6.low_ref.high_ref.refs_10_.refs_11_.refs_14_, ...), custom_call_target="tpu_custom_call" | custom-call | flops 1 | bytes 1 | tf_op jit(solution)/shard_map/block_step/pallas_call | solution.py:308
  106.3 4.9 %block_step.6 = (bf16[1024,256]{1,0:T(8,128)(2,1)S(1)}, bf16[1024,256]{1,0:T(8,128)(2,1)S(1)}, bf16[1024,512]{1,0:T(8,128)(2,1)S(1)}) custom-call(bf16[512,2048]{1,0:T(8,128)(2,1)} %bitcast.7.own_ref, bf16[512,2048]{1,0:T(8,128)(2,1)} %copy-done.20, bf16[1536,512]{1,0:T(8,128)(2,1)S(1)} %collective-permute-done.7.low_ref.high_ref.refs_12_.refs_13_.refs_15_, ...), custom_call_target="tpu_custom_call" | custom-call | flops 1 | bytes 1 | tf_op jit(solution)/shard_map/block_step/pallas_call | solution.py:308
  111.2 5.5 %back_to_width.2 = bf16[512,2048]{1,0:T(8,128)(2,1)} custom-call(bf16[1024,256]{1,0:T(8,128)(2,1)S(1)} %get-tuple-element.59.refs_0_, bf16[1024,256]{1,0:T(8,128)(2,1)S(1)} %get-tuple-element.61.refs_1_, bf16[1024,256]{1,0:T(8,128)(2,1)S(1)} %get-tuple-element.63.refs_2_, bf16[1024,256]{1,0:T(8,128)(2,1)S(1)} %get-tuple-element.64.refs_3_.act_ref, ...), custom_call_target="tpu_custom_call" | custom-call | flops 1 | bytes 1 | tf_op jit(solution)/shard_map/back_to_width/pallas_call | solution.py:372
  117.1 2.2 collective-permute-start.9
  119.3 3.6 %block_grads.1 = bf16[1024,512]{1,0:T(8,128)(2,1)S(1)} custom-call(bf16[512,2048]{1,0:T(8,128)(2,1)} %bitcast.7.own_ref, bf16[512,2048]{1,0:T(8,128)(2,1)} %copy-done.20, bf16[1024,256]{1,0:T(8,128)(2,1)S(1)} %get-tuple-element.64.refs_3_.act_ref, bf16[1024,256]{1,0:T(8,128)(2,1)S(1)} %get-tuple-element.68.refs_7_.pre_ref), custom_call_target="tpu_custom_call" | custom-call | flops 1 | bytes 1 | tf_op jit(solution)/shard_map/block_grads/pallas_call | solution.py:327
  124.3 6.3 %back_to_width.3 = bf16[512,2048]{1,0:T(8,128)(2,1)} custom-call(bf16[1024,256]{1,0:T(8,128)(2,1)S(1)} %get-tuple-element.59.refs_0_, bf16[1024,256]{1,0:T(8,128)(2,1)S(1)} %get-tuple-element.61.refs_1_, bf16[1024,256]{1,0:T(8,128)(2,1)S(1)} %get-tuple-element.63.refs_2_, bf16[1024,256]{1,0:T(8,128)(2,1)S(1)} %get-tuple-element.64.refs_3_.act_ref, ...), custom_call_target="tpu_custom_call" | custom-call | flops 1 | bytes 1 | tf_op jit(solution)/shard_map/back_to_width/pallas_call | solution.py:372
  130.6 11.3 %collective-permute-done.9.packed_ref = bf16[1024,512]{1,0:T(8,128)(2,1)S(1)} collective-permute-done((bf16[1024,512]{1,0:T(8,128)(2,1)S(1)}, bf16[1024,512]{1,0:T(8,128)(2,1)S(1)}, u32[]{:S(2)}, u32[]{:S(2)}) %collective-permute-start.9) | collective-permute-done | bytes 1048608 | tf_op jit(solution)/shard_map/ppermute | solution.py:507
  143.7 10.0 %all-to-all-start.1 = ((bf16[64,8,2048]{2,1,0:T(8,128)(2,1)}), bf16[64,8,2048]{2,1,0:T(8,128)(2,1)S(1)}, u32[]{:S(2)}, u32[]{:S(2)}) async-start(bf16[64,8,2048]{2,1,0:T(8,128)(2,1)} %bitcast.29), calls=%async_computation.1 | async-start | bytes 4194304 | tf_op jit(solution)/shard_map/all_to_all | solution.py:521
  153.7 2.1 collective-permute-start.13
  155.8 24.3 %all-to-all-done.1 = bf16[64,8,2048]{2,1,0:T(8,128)(2,1)S(1)} async-done(((bf16[64,8,2048]{2,1,0:T(8,128)(2,1)}), bf16[64,8,2048]{2,1,0:T(8,128)(2,1)S(1)}, u32[]{:S(2)}, u32[]{:S(2)}) %all-to-all-start.1) | async-done | bytes 2097184 | tf_op jit(solution)/shard_map/all_to_all | solution.py:521
  182.0 4.2 %collective-permute-start.12 = (bf16[16,1024]{1,0:T(8,128)(2,1)S(1)}, bf16[16,1024]{1,0:T(8,128)(2,1)S(1)}, u32[]{:S(2)}, u32[]{:S(2)}) collective-permute-start(bf16[16,1024]{1,0:T(8,128)(2,1)S(1)} %get-tuple-element.90), channel_id=1, source_target_pairs={{16,0},{32,16},{48,32},{64,48},{80,64},{96,80},{112,96},{17,1},{33... | collective-permute-start | bytes 98312 | tf_op jit(solution)/shard_map/ppermute | solution.py:501
  186.3 22.4 %collective-permute-start.11 = (bf16[16,1024]{1,0:T(8,128)(2,1)S(1)}, bf16[16,1024]{1,0:T(8,128)(2,1)S(1)}, u32[]{:S(2)}, u32[]{:S(2)}) collective-permute-start(bf16[16,1024]{1,0:T(8,128)(2,1)S(1)} %get-tuple-element.91), channel_id=1, source_target_pairs={{0,16},{16,32},{32,48},{48,64},{64,80},{80,96},{96,112},{1,17},{17... | collective-permute-start | bytes 98312 | tf_op jit(solution)/shard_map/ppermute | solution.py:500
  209.3 2.1 place_grads.4
  211.5 2.1 place_grads.5
  213.5 2.0 place_grads.6
  215.6 3.2 %place_grads.7 = (f32[4,1024,256]{2,1,0:T(8,128)}, f32[4,256,1024]{2,1,0:T(8,128)}) custom-call(s32[1]{0:T(128)} %get-tuple-element.97.spot_ref, bf16[1024,512]{1,0:T(8,128)(2,1)} %collective-permute-done.13.packed_ref, f32[4,1024,256]{2,1,0:T(8,128)} %get-tuple-element.84.refs_0_, ...), custom_call_target="tpu_custom_call", output_to_operand_aliasing={{0}: (2, {}), {1}: (3, {})} | custom-call | flops 1 | bytes 1 | tf_op jit(solution)/shard_map/place_grads/pallas_call | solution.py:473
  220.3 3.5 %conv_down.1 = bf16[128,1024]{1,0:T(8,128)(2,1)} custom-call(bf16[16,1024]{1,0:T(8,128)(2,1)S(1)} %collective-permute-done.11.low_ref, bf16[128,1024]{1,0:T(8,128)(2,1)S(1)} %get-tuple-element.74.back_ref, bf16[16,1024]{1,0:T(8,128)(2,1)S(1)} %collective-permute-done.12.high_ref, f32[31,1024]{1,0:T(8,128)S(1)} %copy-done.14, ...), custom_call_target="tpu_custom_call" | custom-call | flops 1 | bytes 1 | tf_op jit(solution)/shard_map/conv_down/pallas_call | solution.py:453
  (75 shorter events, 21.3 us)
Async XLA Ops:
  0.6 1.6 copy-start.6
  2.2 1.6 copy-start.7
  3.8 4.5 %copy-start.17 = (bf16[1,128,1024]{2,1,0:T(8,128)(2,1)S(1)}, bf16[1,128,1024]{2,1,0:T(8,128)(2,1)}, u32[]{:S(2)}) copy-start(bf16[1,128,1024]{2,1,0:T(8,128)(2,1)} %param.7) | copy-start | bytes 786436
  3.8 10.8 %copy-start.22 = (s32[1,128,2]{1,2,0:T(2,128)S(1)}, s32[1,128,2]{1,2,0:T(2,128)}, u32[]{:S(2)}) copy-start(s32[1,128,2]{1,2,0:T(2,128)} %param.9) | copy-start | bytes 3076
  3.8 10.9 %copy-start.23 = (f32[1,128,2]{1,2,0:T(2,128)S(1)}, f32[1,128,2]{1,2,0:T(2,128)}, u32[]{:S(2)}) copy-start(f32[1,128,2]{1,2,0:T(2,128)} %param.10) | copy-start | bytes 3076
  3.8 11.0 %copy-start.11 = (bf16[1,128,1024]{2,1,0:T(8,128)(2,1)S(1)}, bf16[1,128,1024]{2,1,0:T(8,128)(2,1)}, u32[]{:S(2)}) copy-start(bf16[1,128,1024]{2,1,0:T(8,128)(2,1)} %param.13) | copy-start | bytes 786436
  6.9 15.5 %copy-start.13 = (f32[31,1024]{1,0:T(8,128)S(1)}, f32[31,1024]{1,0:T(8,128)}, u32[]{:S(2)}) copy-start(f32[31,1024]{1,0:T(8,128)} %kernel_ref.3) | copy-start | bytes 380932
  6.9 21.7 %collective-permute-start.2 = (bf16[512,512]{1,0:T(8,128)(2,1)}, bf16[512,512]{1,0:T(8,128)(2,1)S(1)}, u32[]{:S(2)}, u32[]{:S(2)}) collective-permute-start(bf16[512,512]{1,0:T(8,128)(2,1)} %get-tuple-element.48), channel_id=1, source_target_pairs={{0,32},{32,64},{64,96},{96,0},{1,33},{33,65},{65,97},{97,1},{2,34}... | collective-permute-start | bytes 1572872 | tf_op jit(solution)/shard_map/ppermute | solution.py:507
  8.2 20.4 %collective-permute-start.3 = (bf16[512,512]{1,0:T(8,128)(2,1)}, bf16[512,512]{1,0:T(8,128)(2,1)S(1)}, u32[]{:S(2)}, u32[]{:S(2)}) collective-permute-start(bf16[512,512]{1,0:T(8,128)(2,1)} %get-tuple-element.49), channel_id=1, source_target_pairs={{0,96},{32,0},{64,32},{96,64},{1,97},{33,1},{65,33},{97,65},{2,98}... | collective-permute-start | bytes 1572872 | tf_op jit(solution)/shard_map/ppermute | solution.py:507
  8.4 14.0 %collective-permute-start.1 = (bf16[16,1024]{1,0:T(8,128)(2,1)S(1)}, bf16[16,1024]{1,0:T(8,128)(2,1)S(1)}, u32[]{:S(2)}, u32[]{:S(2)}) collective-permute-start(bf16[16,1024]{1,0:T(8,128)(2,1)S(1)} %get-tuple-element.92), channel_id=1, source_target_pairs={{16,0},{32,16},{48,32},{64,48},{80,64},{96,80},{112,96},{17,1},{33... | collective-permute-start | bytes 98312 | tf_op jit(solution)/shard_map/ppermute | solution.py:501
  11.5 10.9 %collective-permute-start = (bf16[16,1024]{1,0:T(8,128)(2,1)S(1)}, bf16[16,1024]{1,0:T(8,128)(2,1)S(1)}, u32[]{:S(2)}, u32[]{:S(2)}) collective-permute-start(bf16[16,1024]{1,0:T(8,128)(2,1)S(1)} %get-tuple-element.93), channel_id=1, source_target_pairs={{0,16},{16,32},{32,48},{48,64},{64,80},{80,96},{96,112},{1,17},{17... | collective-permute-start | bytes 98312 | tf_op jit(solution)/shard_map/ppermute | solution.py:500
  28.6 38.8 %all-to-all-start = ((bf16[64,8,2048]{2,1,0:T(8,128)(2,1)}), bf16[64,8,2048]{2,1,0:T(8,128)(2,1)}, u32[]{:S(2)}, u32[]{:S(2)}) async-start(bf16[64,8,2048]{2,1,0:T(8,128)(2,1)} %bitcast.6), calls=%async_computation | async-start | bytes 4194304 | tf_op jit(solution)/shard_map/all_to_all | solution.py:521
  41.3 54.9 %collective-permute-start.6 = (bf16[1536,512]{1,0:T(8,128)(2,1)}, bf16[1536,512]{1,0:T(8,128)(2,1)S(1)}, u32[]{:S(2)}, u32[]{:S(2)}) collective-permute-start(bf16[1536,512]{1,0:T(8,128)(2,1)} %get-tuple-element.57), channel_id=1, source_target_pairs={{0,32},{32,64},{64,96},{96,0},{1,33},{33,65},{65,97},{97,1},{2,34}... | collective-permute-start | bytes 4718600 | tf_op jit(solution)/shard_map/ppermute | solution.py:507
  42.6 54.5 %collective-permute-start.7 = (bf16[1536,512]{1,0:T(8,128)(2,1)}, bf16[1536,512]{1,0:T(8,128)(2,1)S(1)}, u32[]{:S(2)}, u32[]{:S(2)}) collective-permute-start(bf16[1536,512]{1,0:T(8,128)(2,1)} %copy-done.8), channel_id=1, source_target_pairs={{0,96},{32,0},{64,32},{96,64},{1,97},{33,1},{65,33},{97,65},{2,98}... | collective-permute-start | bytes 4718600 | tf_op jit(solution)/shard_map/ppermute | solution.py:507
  69.3 2.7 %collective-permute-start.4 = (bf16[256,2048]{1,0:T(8,128)(2,1)S(1)}, bf16[256,2048]{1,0:T(8,128)(2,1)S(1)}, u32[]{:S(2)}, u32[]{:S(2)}) collective-permute-start(bf16[256,2048]{1,0:T(8,128)(2,1)S(1)} %get-tuple-element.89), channel_id=1, source_target_pairs={{0,16},{16,0},{1,17},{17,1},{2,18},{18,2},{3,19},{19,3},{4,20},{20... | collective-permute-start | bytes 3145736 | tf_op jit(solution)/shard_map/ppermute | solution.py:511
  69.7 5.2 %copy-start.3 = (bf16[1024,512]{1,0:T(8,128)(2,1)S(1)}, bf16[1024,512]{1,0:T(8,128)(2,1)}, u32[]{:S(2)}) copy-start(bf16[1024,512]{1,0:T(8,128)(2,1)} %copy-done.2) | copy-start | bytes 3145732
  69.7 3.8 %collective-permute-start.5 = (bf16[256,2048]{1,0:T(8,128)(2,1)S(1)}, bf16[256,2048]{1,0:T(8,128)(2,1)S(1)}, u32[]{:S(2)}, u32[]{:S(2)}) collective-permute-start(bf16[256,2048]{1,0:T(8,128)(2,1)S(1)} %get-tuple-element.88), channel_id=1, source_target_pairs={{0,16},{16,0},{1,17},{17,1},{2,18},{18,2},{3,19},{19,3},{4,20},{20... | collective-permute-start | bytes 3145736 | tf_op jit(solution)/shard_map/ppermute | solution.py:511
  96.2 6.4 %copy-start = (bf16[1536,512]{1,0:T(8,128)(2,1)}, bf16[1536,512]{1,0:T(8,128)(2,1)S(1)}, u32[]{:S(2)}) copy-start(bf16[1536,512]{1,0:T(8,128)(2,1)S(1)} %collective-permute-done.6.low_ref.high_ref.refs_10_.refs_11_.refs_14_) | copy-start | bytes 4718596
  97.1 9.2 %copy-start.1 = (bf16[1536,512]{1,0:T(8,128)(2,1)}, bf16[1536,512]{1,0:T(8,128)(2,1)S(1)}, u32[]{:S(2)}) copy-start(bf16[1536,512]{1,0:T(8,128)(2,1)S(1)} %collective-permute-done.7.low_ref.high_ref.refs_12_.refs_13_.refs_15_) | copy-start | bytes 4718596
  116.7 6.2 %collective-permute-start.8 = (bf16[512,2048]{1,0:T(8,128)(2,1)}, bf16[512,2048]{1,0:T(8,128)(2,1)S(1)}, u32[]{:S(2)}, u32[]{:S(2)}) collective-permute-start(bf16[512,2048]{1,0:T(8,128)(2,1)} %back_to_width.2), channel_id=1, source_target_pairs={{0,16},{16,0},{1,17},{17,1},{2,18},{18,2},{3,19},{19,3},{4,20},{20... | collective-permute-start | bytes 6291464 | tf_op jit(solution)/shard_map/ppermute | solution.py:511
  117.1 24.7 %collective-permute-start.9 = (bf16[1024,512]{1,0:T(8,128)(2,1)S(1)}, bf16[1024,512]{1,0:T(8,128)(2,1)S(1)}, u32[]{:S(2)}, u32[]{:S(2)}) collective-permute-start(bf16[1024,512]{1,0:T(8,128)(2,1)S(1)} %get-tuple-element.70), channel_id=1, source_target_pairs={{0,96},{32,0},{64,32},{96,64},{1,97},{33,1},{65,33},{97,65},{2,98}... | collective-permute-start | bytes 3145736 | tf_op jit(solution)/shard_map/ppermute | solution.py:507
  119.3 24.4 %collective-permute-start.10 = (bf16[1024,512]{1,0:T(8,128)(2,1)S(1)}, bf16[1024,512]{1,0:T(8,128)(2,1)S(1)}, u32[]{:S(2)}, u32[]{:S(2)}) collective-permute-start(bf16[1024,512]{1,0:T(8,128)(2,1)S(1)} %get-tuple-element.71), channel_id=1, source_target_pairs={{0,32},{32,64},{64,96},{96,0},{1,33},{33,65},{65,97},{97,1},{2,34}... | collective-permute-start | bytes 3145736 | tf_op jit(solution)/shard_map/ppermute | solution.py:507
  122.9 7.6 %copy-start.12 = (bf16[1024,512]{1,0:T(8,128)(2,1)}, bf16[1024,512]{1,0:T(8,128)(2,1)S(1)}, u32[]{:S(2)}) copy-start(bf16[1024,512]{1,0:T(8,128)(2,1)S(1)} %block_grads.1) | copy-start | bytes 3145732
  122.9 1.4 copy-start.21
  143.7 36.4 %all-to-all-start.1 = ((bf16[64,8,2048]{2,1,0:T(8,128)(2,1)}), bf16[64,8,2048]{2,1,0:T(8,128)(2,1)S(1)}, u32[]{:S(2)}, u32[]{:S(2)}) async-start(bf16[64,8,2048]{2,1,0:T(8,128)(2,1)} %bitcast.29), calls=%async_computation.1 | async-start | bytes 4194304 | tf_op jit(solution)/shard_map/all_to_all | solution.py:521
  153.7 61.9 %collective-permute-start.13 = (bf16[1024,512]{1,0:T(8,128)(2,1)}, bf16[1024,512]{1,0:T(8,128)(2,1)}, u32[]{:S(2)}, u32[]{:S(2)}) collective-permute-start(bf16[1024,512]{1,0:T(8,128)(2,1)} %copy-done.12), channel_id=1, source_target_pairs={{0,64},{32,96},{64,0},{96,32},{1,65},{33,97},{65,1},{97,33},{2,66}... | collective-permute-start | bytes 3145736 | tf_op jit(solution)/shard_map/ppermute | solution.py:507
  180.1 29.3 %copy-start.5 = (f32[1024,512]{1,0:T(8,128)S(1)}, f32[1024,512]{1,0:T(8,128)}, u32[]{:S(2)}) copy-start(f32[1024,512]{1,0:T(8,128)} %copy-done.4) | copy-start | bytes 6291460
  181.3 30.2 %copy-start.10 = (bf16[1024,512]{1,0:T(8,128)(2,1)S(1)}, bf16[1024,512]{1,0:T(8,128)(2,1)}, u32[]{:S(2)}) copy-start(bf16[1024,512]{1,0:T(8,128)(2,1)} %copy-done.9) | copy-start | bytes 3145732
  182.0 38.2 %collective-permute-start.12 = (bf16[16,1024]{1,0:T(8,128)(2,1)S(1)}, bf16[16,1024]{1,0:T(8,128)(2,1)S(1)}, u32[]{:S(2)}, u32[]{:S(2)}) collective-permute-start(bf16[16,1024]{1,0:T(8,128)(2,1)S(1)} %get-tuple-element.90), channel_id=1, source_target_pairs={{16,0},{32,16},{48,32},{64,48},{80,64},{96,80},{112,96},{17,1},{33... | collective-permute-start | bytes 98312 | tf_op jit(solution)/shard_map/ppermute | solution.py:501
  186.3 34.0 %collective-permute-start.11 = (bf16[16,1024]{1,0:T(8,128)(2,1)S(1)}, bf16[16,1024]{1,0:T(8,128)(2,1)S(1)}, u32[]{:S(2)}, u32[]{:S(2)}) collective-permute-start(bf16[16,1024]{1,0:T(8,128)(2,1)S(1)} %get-tuple-element.91), channel_id=1, source_target_pairs={{0,16},{16,32},{32,48},{48,64},{64,80},{80,96},{96,112},{1,17},{17... | collective-permute-start | bytes 98312 | tf_op jit(solution)/shard_map/ppermute | solution.py:500
  215.6 3.2 %copy-start.19 = (bf16[128,1024]{1,0:T(8,128)(2,1)S(1)}, bf16[128,1024]{1,0:T(8,128)(2,1)}, u32[]{:S(2)}) copy-start(bf16[128,1024]{1,0:T(8,128)(2,1)} %copy-done.18) | copy-start | bytes 786436
  218.8 1.5 copy-start.14
  (8 other events, 8.5 us)

commit v3 on v2

--- a/solution.py
+++ b/solution.py
@@ -151,7 +151,7 @@
     )(*operands, send)
 
 
-TILE = 256
+TILE = 512
 
 
 def copy_all(copies):
@@ -229,108 +229,81 @@
     )(*parts, *wholes)
 
 
-def half_specs(halves):
-    rows = []
-    for array, index in halves:
-        block = (array.shape[1], array.shape[1])
-        rows.append(pl.BlockSpec(block, lambda i, index=index: (index, 0)))
-    return rows
-
-
-def whole_spec(array):
-    return pl.BlockSpec(array.shape, lambda i: (0, 0))
-
-
-def split_in(lows, halves, hidden):
-    total = None
-    step = halves[0].shape[0]
-    for index, ref in enumerate(halves):
-        part = dot(lows[:, index * step : (index + 1) * step], ref[:, :hidden], (1, 0))
-        total = part if total is None else total + part
-    return total
-
-
-def out_piece(halves, piece, hidden):
-    step = halves[0].shape[0]
-    ref = halves[piece // step]
-    start = piece % step
-    return ref[start : start + hidden, hidden:]
-
-
-def activate(rows, refs, halves, act_ref, pre_ref):
-    hidden = halves[0].shape[1] // 2
+def listed_refs(quarters, refs, arrays):
+    return [(refs[[id(a) for a in arrays].index(id(array))], offset) for array, offset in quarters]
+
+
+def distinct(quarters):
+    arrays = []
+    for array, _ in quarters:
+        if all(array is not other for other in arrays):
+            arrays.append(array)
+    return arrays
+
+
+def in_block(quarters, hidden):
+    return jnp.concatenate([ref[at : at + hidden, :hidden] for ref, at in quarters])
+
+
+def out_block(quarters, hidden):
+    return jnp.concatenate([ref[at : at + hidden, hidden:] for ref, at in quarters], axis=1)
+
+
+def out_piece(quarters, piece, hidden):
+    ref, offset = quarters[piece // hidden]
+    return ref[offset : offset + hidden, hidden:]
+
+
+def activate(refs, quarters, act_ref, pre_ref):
+    hidden = act_ref.shape[1]
     width = refs[0].shape[1] // 2
-    for half, ref in enumerate(refs):
-        for start in range(0, rows, TILE):
-            part = slice(start, start + TILE)
-            held = slice(half * rows + start, half * rows + start + TILE)
-            pre = split_in(ref[part, :width], halves, hidden)
-            logistic = jax.nn.sigmoid(pre)
-            act_ref[held, :] = (pre * logistic).astype(BF16)
-            back = None
-            for piece in range(0, width, hidden):
-                term = dot(
-                    ref[part, width + piece : width + piece + hidden],
-                    out_piece(halves, piece, hidden),
-                    (1, 1),
-                )
-                back = term if back is None else back + term
-            slope = logistic * (1.0 + pre * (1.0 - logistic))
-            pre_ref[held, :] = (back * slope).astype(BF16)
-
-
-def weigh(rows, refs, act_ref, pre_ref, grad_ref):
-    width, hidden = grad_ref.shape[0], grad_ref.shape[1] // 2
-    first, second = refs
+    start = 0
+    for ref in refs:
+        held = slice(start, start + ref.shape[0])
+        start += ref.shape[0]
+        pre = dot(ref[:, :width], in_block(quarters, hidden), (1, 0))
+        logistic = jax.nn.sigmoid(pre)
+        act_ref[held, :] = (pre * logistic).astype(BF16)
+        back = dot(ref[:, width:], out_block(quarters, hidden), (1, 1))
+        slope = logistic * (1.0 + pre * (1.0 - logistic))
+        pre_ref[held, :] = (back * slope).astype(BF16)
+
+
+def weigh(refs, act_ref, pre_ref, grad_refs):
+    hidden = act_ref.shape[1]
+    width = refs[0].shape[1] // 2
+    share = width // len(grad_refs)
     for piece in range(0, width, hidden):
-        part = slice(piece, piece + hidden)
+        grad_ref = grad_refs[piece // share]
+        inner = slice(piece % share, piece % share + hidden)
         shifted = slice(width + piece, width + piece + hidden)
-        out = dot(act_ref[:rows, :], first[:, shifted], (0, 0))
-        out = out + dot(act_ref[rows:, :], second[:, shifted], (0, 0))
-        grad_ref[part, hidden:] = out.astype(grad_ref.dtype)
-        out = dot(first[:, part], pre_ref[:rows, :], (0, 0))
-        out = out + dot(second[:, part], pre_ref[rows:, :], (0, 0))
-        grad_ref[part, :hidden] = out.astype(grad_ref.dtype)
-
-
-def block_step(own, other, halves, grad_type):
-    rows, width = own.shape[0], own.shape[1] // 2
-    hidden = halves[0][0].shape[1] // 2
-    result = [shape_of((2 * rows, hidden), BF16), shape_of((2 * rows, hidden), BF16)]
-    if grad_type is not None:
-        result.append(shape_of((width, 2 * hidden), grad_type))
-
-    def body(own_ref, other_ref, low_ref, high_ref, act_ref, pre_ref, *grads):
-        activate(rows, (own_ref, other_ref), (low_ref, high_ref), act_ref, pre_ref)
-        for grad_ref in grads:
-            weigh(rows, (own_ref, other_ref), act_ref, pre_ref, grad_ref)
-
-    return pl.pallas_call(
-        body,
-        grid=(1,),
-        in_specs=[whole_spec(own), whole_spec(other)] + half_specs(halves),
-        out_specs=[whole_spec(array) for array in result],
+        rows = jnp.concatenate([ref[:, shifted] for ref in refs])
+        grad_ref[inner, hidden:] = dot(act_ref[...], rows, (0, 0)).astype(grad_ref.dtype)
+        rows = jnp.concatenate([ref[:, piece : piece + hidden] for ref in refs])
+        grad_ref[inner, :hidden] = dot(rows, pre_ref[...], (0, 0)).astype(grad_ref.dtype)
+
+
+def block_step(rows, quarters, grad_type, shares):
+    total, width = sum(part.shape[0] for part in rows), rows[0].shape[1] // 2
+    hidden = quarters[0][0].shape[1] // 2
+    result = [shape_of((total, hidden), BF16), shape_of((total, hidden), BF16)]
+    result += [shape_of((width // shares, 2 * hidden), grad_type)] * shares
+    arrays = distinct(quarters)
+
+    def body(*refs):
+        row_refs, refs = refs[: len(rows)], refs[len(rows) :]
+        held = listed_refs(quarters, refs[: len(arrays)], arrays)
+        act_ref, pre_ref, *grads = refs[len(arrays) :]
+        activate(row_refs, held, act_ref, pre_ref)
+        weigh(row_refs, act_ref, pre_ref, grads)
+
+    return pl.pallas_call(
+        body,
         out_shape=result,
         compiler_params=params(48),
         cost_estimate=COST,
         name="block_step",
-    )(own, other, *[array for array, _ in halves])
-
-
-def block_grads(own, other, act, pre, grad_type):
-    rows, width = own.shape[0], own.shape[1] // 2
-    hidden = act.shape[1]
-
-    def body(own_ref, other_ref, act_ref, pre_ref, grad_ref):
-        weigh(rows, (own_ref, other_ref), act_ref, pre_ref, grad_ref)
-
-    return pl.pallas_call(
-        body,
-        out_shape=shape_of((width, 2 * hidden), grad_type),
-        compiler_params=params(48),
-        cost_estimate=COST,
-        name="block_grads",
-    )(own, other, act, pre)
+    )(*rows, *arrays)
 
 
 def back_to_width(half, acts, pres, packed, arrived):
@@ -338,47 +311,38 @@
     rows = acts[0].shape[0] // 2
     count = len(acts)
     width = hidden * count
-    extra = [] if arrived is None else [arrived]
+    arrays = distinct([pair for quarters in packed for pair in quarters])
 
     def body(*refs):
         act_refs, pre_refs = refs[:count], refs[count : 2 * count]
-        w_refs = [refs[2 * count + 2 * i : 2 * count + 2 * i + 2] for i in range(count)]
-        out_ref = refs[-1]
-        for start in range(0, rows, TILE):
-            held = slice(start, start + TILE)
-
-            def emit(columns, total):
-                if extra:
-                    total = total + refs[4 * count][held, columns].astype(F32)
-                out_ref[held, columns] = total.astype(BF16)
-
-            for piece in range(0, width, hidden):
-                total = None
-                for part_ref, halves in zip(act_refs, w_refs):
-                    part = dot(part_ref[held, :], out_piece(halves, piece, hidden), (1, 0))
-                    total = part if total is None else total + part
-                emit(slice(piece, piece + hidden), total)
-            for side in range(2):
-                total = None
-                for part_ref, halves in zip(pre_refs, w_refs):
-                    part = dot(part_ref[held, :], halves[side][:, :hidden], (1, 1))
-                    total = part if total is None else total + part
-                step = width // 2
-                emit(slice(width + side * step, width + (side + 1) * step), total)
-
-    one = pl.BlockSpec((rows, hidden), lambda i: (half, 0))
-    result = shape_of((rows, 2 * width), BF16)
-    listed = [pair for halves in packed for pair in halves]
-    return pl.pallas_call(
-        body,
-        grid=(1,),
-        in_specs=[one] * (2 * count) + half_specs(listed) + [whole_spec(result)] * len(extra),
-        out_specs=whole_spec(result),
-        out_shape=result,
+        base = 2 * count + len(arrays)
+        w_refs = [listed_refs(quarters, refs[2 * count : base], arrays) for quarters in packed]
+        came, out_ref = refs[base:-1], refs[-1]
+        held = slice(half * rows, (half + 1) * rows)
+
+        def emit(columns, total):
+            for ref in came:
+                total = total + ref[:, columns].astype(F32)
+            out_ref[:, columns] = total.astype(BF16)
+
+        acted = jnp.concatenate([ref[held, :] for ref in act_refs], axis=1)
+        graded = jnp.concatenate([ref[held, :] for ref in pre_refs], axis=1)
+        for piece in range(0, width, hidden):
+            spot = piece // hidden
+            weight = jnp.concatenate([out_piece(quarters, piece, hidden) for quarters in w_refs])
+            emit(slice(piece, piece + hidden), dot(acted, weight, (1, 0)))
+            weight = jnp.concatenate(
+                [q[spot][0][q[spot][1] : q[spot][1] + hidden, :hidden] for q in w_refs], axis=1
+            )
+            emit(slice(width + piece, width + piece + hidden), dot(graded, weight, (1, 1)))
+
+    return pl.pallas_call(
+        body,
+        out_shape=shape_of((rows, 2 * width), BF16),
         compiler_params=params(48),
         cost_estimate=COST,
         name="back_to_width",
-    )(*acts, *pres, *[array for array, _ in listed], *extra)
+    )(*acts, *pres, *arrays, *arrived)
 
 
 def mix_out(routes, gates, hidden, returned, experts, n_y):
@@ -460,22 +424,26 @@
     )(low, back, high, kernel, hidden_grad)
 
 
-def place_grads(spot, packed, count, held):
-    width, hidden = packed.shape[0], packed.shape[1] // 2
-
-    def body(spot_ref, packed_ref, *refs):
+def place_grads(spot, parts, count, held):
+    hidden = parts[0].shape[1] // 2
+    width = parts[0].shape[0] * len(parts)
+    share = parts[0].shape[0]
+
+    def body(spot_ref, *refs):
+        part_refs = refs[: len(parts)]
         in_ref, out_ref = refs[-2:]
-        in_ref[0] = packed_ref[:, :hidden].astype(F32)
-        for piece in range(0, width, hidden):
-            part = slice(piece, piece + hidden)
-            out_ref[0, :, part] = packed_ref[part, hidden:].astype(F32)
+        for index, ref in enumerate(part_refs):
+            in_ref[0, index * share : (index + 1) * share] = ref[:, :hidden].astype(F32)
+            for piece in range(0, share, hidden):
+                target = slice(index * share + piece, index * share + piece + hidden)
+                out_ref[0, :, target] = ref[piece : piece + hidden, hidden:].astype(F32)
 
     return pl.pallas_call(
         body,
         grid_spec=pltpu.PrefetchScalarGridSpec(
             num_scalar_prefetch=1,
             grid=(1,),
-            in_specs=[pl.BlockSpec(packed.shape, lambda i, spot: (0, 0))]
+            in_specs=[pl.BlockSpec(part.shape, lambda i, spot: (0, 0)) for part in parts]
             + [pl.BlockSpec(memory_space=pl.ANY)] * len(held),
             out_specs=(
                 pl.BlockSpec((1, width, hidden), lambda i, spot: (spot[0], 0, 0)),
@@ -486,11 +454,11 @@
             shape_of((count, width, hidden), F32),
             shape_of((count, hidden, width), F32),
         ),
-        input_output_aliases={2 + index: index for index in range(len(held))},
+        input_output_aliases={1 + len(parts) + index: index for index in range(len(held))},
         compiler_params=params(32),
         cost_estimate=COST,
         name="place_grads",
-    )(spot, packed, *held)
+    )(spot, *parts, *held)
 
 
 def edges(block):
@@ -509,11 +477,6 @@
 
 def swap(block):
     return lax.ppermute(block, "core", [(0, 1), (1, 0)])
-
-
-def together(rows):
-    half = rows.shape[0] // 2
-    return jnp.concatenate([swap(rows[:half]), swap(rows[half:])])
 
 
 def exchange(rows, groups):
@@ -541,36 +504,42 @@
     own = exchange(send, groups)
     next_up, next_down = fill_first((first_up, first_down), (next_up, next_down))
     next_up, next_down = turn(next_up, 1), turn(next_down, -1)
-    other = together(own)
-
-    order = [0, 1, 3, 2]
-    acts, pres, grads = {}, {}, {}
-    packed = {0: [(own_block, 0), (own_block, 1)]}
-    acts[0], pres[0], grads[0] = block_step(own, other, packed[0], F32)
+    middle = own.shape[0] // 2
+    rows = [own, swap(own[:middle]), swap(own[middle:])]
+
+    step = w_in.shape[2]
+
+    def quarters(array, begin, count):
+        return [(array, begin + index * step) for index in range(count)]
+
+    acts, pres, grads, packed = {}, {}, {}, {0: quarters(own_block, 0, 4)}
+    acts[0], pres[0], *grads[0] = block_step(rows, packed[0], F32, 1)
     acts[0], next_up, next_down = lax.optimization_barrier((acts[0], next_up, next_down))
-    packed[1] = [(next_up, 1), (next_up, 2)]
-    packed[3] = [(next_down, 1), (next_down, 2)]
-    packed[2] = [(next_up, 0), (next_down, 0)]
+    packed[2] = quarters(next_up, 0, 2) + quarters(next_down, 0, 2)
+    packed[1] = quarters(next_up, 2 * step, 4)
+    packed[3] = quarters(next_down, 2 * step, 4)
+    acts[2], pres[2], up, down = block_step(rows, packed[2], BF16, 2)
+    up, down = turn(up, 1), turn(down, -1)
     for steps in (1, 3):
-        acts[steps], pres[steps], grads[steps] = block_step(own, other, packed[steps], BF16)
-        grads[steps] = turn(grads[steps], -steps)
-    acts[2], pres[2] = block_step(own, other, packed[2], None)
-    listed = [[held[steps] for steps in order] for held in (acts, pres, packed)]
-    arrived = swap(back_to_width(1, *listed, None))
-    grads[2] = block_grads(own, other, acts[2], pres[2], BF16)
-    arrived, grads[2] = lax.optimization_barrier((arrived, grads[2]))
-    grads[2] = turn(grads[2], -2)
-    result = back_to_width(0, *listed, arrived)
-    result, grads[1], grads[3] = lax.optimization_barrier((result, grads[1], grads[3]))
+        acts[steps], pres[steps], *grads[steps] = block_step(rows, packed[steps], BF16, 2)
+        grads[steps] = [turn(part, -steps) for part in grads[steps]]
+    acts[3], up, down = lax.optimization_barrier((acts[3], up, down))
+    grads[2] = [turn(up, 1), turn(down, -1)]
+    listed = [[held[steps] for steps in packed] for held in (acts, pres, packed)]
+    arrived = swap(back_to_width(1, *listed, []))
+    result = back_to_width(0, *listed, [arrived])
+    result, grads[1][0], grads[3][0] = lax.optimization_barrier((result, grads[1][0], grads[3][0]))
     returned = exchange(result, groups)
 
+    held = ()
+    for steps in (0,):
+        held = place_grads(spots[steps : steps + 1], grads[steps], n_y, held)
+    returned, *held = lax.optimization_barrier((returned, *held))
     hidden_grad, back = grad_rows(routes, cotangent, mixing, returned, experts, n_y)
     low, high = edges(back)
     frames_grad = conv_down(low, back, high, conv_kernel, hidden_grad)
     mixed = mix_out(routes, gates, hidden, returned, experts, n_y)
-
-    held = ()
-    for steps in order:
+    for steps in (1, 3, 2):
         held = place_grads(spots[steps : steps + 1], grads[steps], n_y, held)
     w_in_grad, w_out_grad = held
     return (mixed[None], frames_grad[None], w_in_grad, w_out_grad)

time: 224 us -> 207 us (0.924)
  the two profiles are of different devices: /device:TPU:11 before, /device:TPU:5 now
where the time goes in v3:
time: 207 us; the launch traced here: 206 us
  waiting for transfers between devices  83 us (40%)
  Pallas kernels  57.6 us (28%)
  starting transfers between devices  48.5 us (23%)
  local copies, waits for them, and re-layouts  15.6 us (8%)
    all_to_all x2, waiting for transfers between devices, exchange(): lax.all_to_all(grouped, ('y', 'exp'), split_axis=0, concat_axis=0, tiled=...  42 us
    ppermute x12, waiting for transfers between devices, turn(): lax.ppermute(block, 'y', [(i, (i + steps) % count) for i in range(count)])  30.4 us
    all_to_all x2, starting transfers between devices, exchange(): lax.all_to_all(grouped, ('y', 'exp'), split_axis=0, concat_axis=0, tiled=...  18.6 us
    pallas_call x4, Pallas kernels, block_step(): pl.pallas_call(body, out_shape=result, compiler_params=params(48), cost_e...  18.6 us
    ppermute x12, starting transfers between devices, turn(): lax.ppermute(block, 'y', [(i, (i + steps) % count) for i in range(count)])  16 us
    unnamed x50, local copies, waits for them, and re-layouts  13.1 us
    pallas_call x2, Pallas kernels, back_to_width(): pl.pallas_call(body, out_shape=shape_of((rows, 2 * width), BF16), compile...  12.2 us
    pallas_call x4, Pallas kernels, place_grads(): pl.pallas_call(body, grid_spec=pltpu.PrefetchScalarGridSpec(num_scalar_pr...  11.6 us
  transfers between devices with their start and end apart: 21, of which 13 were waited for; matrix products, arithmetic and copies ran while one was open for 1% of the time, Pallas kernels for 20%

profile of v3, /device:TPU:5, one launch (start us, length us, event | category | flops | bytes accessed | tf_op | source)
XLA Modules:
  0.0 205.6 jit_solution(5640173857979875440)
XLA Ops:
  9.6 3.1 %collective-permute-start = (bf16[16,1024]{1,0:T(8,128)(2,1)S(1)}, bf16[16,1024]{1,0:T(8,128)(2,1)S(1)}, u32[]{:S(2)}, u32[]{:S(2)}) collective-permute-start(bf16[16,1024]{1,0:T(8,128)(2,1)S(1)} %get-tuple-element.109), channel_id=1, source_target_pairs={{0,16},{16,32},{32,48},{48,64},{64,80},{80,96},{96,112},{1,17},{17... | collective-permute-start | bytes 98312 | tf_op jit(solution)/shard_map/ppermute | solution.py:468
  14.9 2.1 %down_slots.1._ = bf16[512,2048]{1,0:T(8,128)(2,1)} custom-call(s32[128,2]{1,0:T(8,128)S(1)} %bitcast.20, f32[128,2]{1,0:T(8,128)S(1)} %bitcast.26, bf16[128,1024]{1,0:T(8,128)(2,1)S(1)} %bitcast.24), custom_call_target="tpu_custom_call" | custom-call | flops 1 | bytes 1 | tf_op jit(solution)/shard_map/down_slots/pallas_call | solution.py:74
  17.0 2.7 %collective-permute-done.low_ref = bf16[16,1024]{1,0:T(8,128)(2,1)S(1)} collective-permute-done((bf16[16,1024]{1,0:T(8,128)(2,1)S(1)}, bf16[16,1024]{1,0:T(8,128)(2,1)S(1)}, u32[]{:S(2)}, u32[]{:S(2)}) %collective-permute-start) | collective-permute-done | bytes 32800 | tf_op jit(solution)/shard_map/ppermute | solution.py:468
  19.7 2.7 %collective-permute-done.1.high_ref = bf16[16,1024]{1,0:T(8,128)(2,1)S(1)} collective-permute-done((bf16[16,1024]{1,0:T(8,128)(2,1)S(1)}, bf16[16,1024]{1,0:T(8,128)(2,1)S(1)}, u32[]{:S(2)}, u32[]{:S(2)}) %collective-permute-start.1) | collective-permute-done | bytes 32800 | tf_op jit(solution)/shard_map/ppermute | solution.py:469
  22.4 4.7 %conv_up.1 = (f32[128,1024]{1,0:T(8,128)S(1)}, bf16[128,1024]{1,0:T(8,128)(2,1)S(1)}, bf16[512,2048]{1,0:T(8,128)(2,1)}) custom-call(bf16[16,1024]{1,0:T(8,128)(2,1)S(1)} %collective-permute-done.low_ref, bf16[128,1024]{1,0:T(8,128)(2,1)S(1)} %bitcast.28, bf16[16,1024]{1,0:T(8,128)(2,1)S(1)} %collective-permute-done.1.high_ref, ...), custom_call_target="tpu_custom_call", output_to_operand_aliasing={{2}: (5, {})} | custom-call | flops 1 | bytes 1 | tf_op jit(solution)/shard_map/conv_up/pallas_call | solution.py:131
  28.6 10.8 %all-to-all-start = ((bf16[64,8,2048]{2,1,0:T(8,128)(2,1)}), bf16[64,8,2048]{2,1,0:T(8,128)(2,1)}, u32[]{:S(2)}, u32[]{:S(2)}) async-start(bf16[64,8,2048]{2,1,0:T(8,128)(2,1)} %bitcast.6), calls=%async_computation | async-start | bytes 4194304 | tf_op jit(solution)/shard_map/all_to_all | solution.py:484
  44.1 24.1 %all-to-all-done = bf16[64,8,2048]{2,1,0:T(8,128)(2,1)} async-done(((bf16[64,8,2048]{2,1,0:T(8,128)(2,1)}), bf16[64,8,2048]{2,1,0:T(8,128)(2,1)}, u32[]{:S(2)}, u32[]{:S(2)}) %all-to-all-start) | async-done | bytes 2097184 | tf_op jit(solution)/shard_map/all_to_all | solution.py:484
  70.6 2.1 %collective-permute-done.4.refs_1_ = bf16[256,2048]{1,0:T(8,128)(2,1)S(1)} collective-permute-done((bf16[256,2048]{1,0:T(8,128)(2,1)S(1)}, bf16[256,2048]{1,0:T(8,128)(2,1)S(1)}, u32[]{:S(2)}, u32[]{:S(2)}) %collective-permute-start.4) | collective-permute-done | bytes 1048608 | tf_op jit(solution)/shard_map/ppermute | solution.py:479
  74.3 5.5 %block_step.4 = (bf16[1024,256]{1,0:T(8,128)(2,1)S(1)}, bf16[1024,256]{1,0:T(8,128)(2,1)S(1)}, f32[1024,512]{1,0:T(8,128)}) custom-call(bf16[512,2048]{1,0:T(8,128)(2,1)} %bitcast.7.refs_0_, bf16[256,2048]{1,0:T(8,128)(2,1)S(1)} %collective-permute-done.4.refs_1_, bf16[256,2048]{1,0:T(8,128)(2,1)S(1)} %collective-permute-done.5.refs_2_, ...), custom_call_target="tpu_custom_call" | custom-call | flops 1 | bytes 1 | tf_op jit(solution)/shard_map/block_step/pallas_call | solution.py:300
  79.8 18.7 %collective-permute-done.6.refs_3_.refs_9_ = bf16[1536,512]{1,0:T(8,128)(2,1)S(1)} collective-permute-done((bf16[1536,512]{1,0:T(8,128)(2,1)}, bf16[1536,512]{1,0:T(8,128)(2,1)S(1)}, u32[]{:S(2)}, u32[]{:S(2)}) %collective-permute-start.6) | collective-permute-done | bytes 1572896 | tf_op jit(solution)/shard_map/ppermute | solution.py:475
  99.7 4.6 %block_step.5 = (bf16[1024,256]{1,0:T(8,128)(2,1)S(1)}, bf16[1024,256]{1,0:T(8,128)(2,1)S(1)}, bf16[512,512]{1,0:T(8,128)(2,1)S(1)}, bf16[512,512]{1,0:T(8,128)(2,1)S(1)}) custom-call(bf16[512,2048]{1,0:T(8,128)(2,1)} %bitcast.7.refs_0_, bf16[256,2048]{1,0:T(8,128)(2,1)S(1)} %collective-permute-done.4.refs_1_, ...), custom_call_target="tpu_custom_call" | custom-call | flops 1 | bytes 1 | tf_op jit(solution)/shard_map/block_step/pallas_call | solution.py:300
  104.4 2.7 %collective-permute-start.9 = (bf16[512,512]{1,0:T(8,128)(2,1)S(1)}, bf16[512,512]{1,0:T(8,128)(2,1)S(1)}, u32[]{:S(2)}, u32[]{:S(2)}) collective-permute-start(bf16[512,512]{1,0:T(8,128)(2,1)S(1)} %get-tuple-element.74), channel_id=1, source_target_pairs={{0,96},{32,0},{64,32},{96,64},{1,97},{33,1},{65,33},{97,65},{2,98}... | collective-permute-start | bytes 1572872 | tf_op jit(solution)/shard_map/ppermute | solution.py:475
  107.1 4.2 %block_step.6 = (bf16[1024,256]{1,0:T(8,128)(2,1)S(1)}, bf16[1024,256]{1,0:T(8,128)(2,1)S(1)}, bf16[512,512]{1,0:T(8,128)(2,1)S(1)}, bf16[512,512]{1,0:T(8,128)(2,1)S(1)}) custom-call(bf16[512,2048]{1,0:T(8,128)(2,1)} %bitcast.7.refs_0_, bf16[256,2048]{1,0:T(8,128)(2,1)S(1)} %collective-permute-done.4.refs_1_, ...), custom_call_target="tpu_custom_call" | custom-call | flops 1 | bytes 1 | tf_op jit(solution)/shard_map/block_step/pallas_call | solution.py:300
  112.2 4.2 %block_step.7 = (bf16[1024,256]{1,0:T(8,128)(2,1)S(1)}, bf16[1024,256]{1,0:T(8,128)(2,1)S(1)}, bf16[512,512]{1,0:T(8,128)(2,1)S(1)}, bf16[512,512]{1,0:T(8,128)(2,1)S(1)}) custom-call(bf16[512,2048]{1,0:T(8,128)(2,1)} %bitcast.7.refs_0_, bf16[256,2048]{1,0:T(8,128)(2,1)S(1)} %collective-permute-done.4.refs_1_, ...), custom_call_target="tpu_custom_call" | custom-call | flops 1 | bytes 1 | tf_op jit(solution)/shard_map/block_step/pallas_call | solution.py:300
  116.4 2.4 %collective-permute-done.8 = bf16[512,512]{1,0:T(8,128)(2,1)S(1)} collective-permute-done((bf16[512,512]{1,0:T(8,128)(2,1)S(1)}, bf16[512,512]{1,0:T(8,128)(2,1)S(1)}, u32[]{:S(2)}, u32[]{:S(2)}) %collective-permute-start.8) | collective-permute-done | bytes 524320 | tf_op jit(solution)/shard_map/ppermute | solution.py:475
  118.7 5.9 %back_to_width.2 = bf16[512,2048]{1,0:T(8,128)(2,1)} custom-call(bf16[1024,256]{1,0:T(8,128)(2,1)S(1)} %get-tuple-element.67.refs_0_, bf16[1024,256]{1,0:T(8,128)(2,1)S(1)} %get-tuple-element.70.refs_1_, bf16[1024,256]{1,0:T(8,128)(2,1)S(1)} %get-tuple-element.71.refs_2_, bf16[1024,256]{1,0:T(8,128)(2,1)S(1)} %get-tuple-element.75.refs_3_, ...), custom_call_target="tpu_custom_call" | custom-call | flops 1 | bytes 1 | tf_op jit(solution)/shard_map/back_to_width/pallas_call | solution.py:339
  126.0 2.5 %collective-permute-start.11 = (bf16[512,512]{1,0:T(8,128)(2,1)S(1)}, bf16[512,512]{1,0:T(8,128)(2,1)S(1)}, u32[]{:S(2)}, u32[]{:S(2)}) collective-permute-start(bf16[512,512]{1,0:T(8,128)(2,1)S(1)} %get-tuple-element.80), channel_id=1, source_target_pairs={{0,96},{32,0},{64,32},{96,64},{1,97},{33,1},{65,33},{97,65},{2,98}... | collective-permute-start | bytes 1572872 | tf_op jit(solution)/shard_map/ppermute | solution.py:475
  131.3 6.3 %back_to_width.3 = bf16[512,2048]{1,0:T(8,128)(2,1)} custom-call(bf16[1024,256]{1,0:T(8,128)(2,1)S(1)} %get-tuple-element.67.refs_0_, bf16[1024,256]{1,0:T(8,128)(2,1)S(1)} %get-tuple-element.70.refs_1_, bf16[1024,256]{1,0:T(8,128)(2,1)S(1)} %get-tuple-element.71.refs_2_, bf16[1024,256]{1,0:T(8,128)(2,1)S(1)} %get-tuple-element.75.refs_3_, ...), custom_call_target="tpu_custom_call" | custom-call | flops 1 | bytes 1 | tf_op jit(solution)/shard_map/back_to_width/pallas_call | solution.py:339
  137.6 2.2 %collective-permute-done.11.refs_0_ = bf16[512,512]{1,0:T(8,128)(2,1)S(1)} collective-permute-done((bf16[512,512]{1,0:T(8,128)(2,1)S(1)}, bf16[512,512]{1,0:T(8,128)(2,1)S(1)}, u32[]{:S(2)}, u32[]{:S(2)}) %collective-permute-start.11) | collective-permute-done | bytes 524320 | tf_op jit(solution)/shard_map/ppermute | solution.py:475
  139.8 3.1 %collective-permute-done.12.refs_0_ = bf16[512,512]{1,0:T(8,128)(2,1)S(1)} collective-permute-done((bf16[512,512]{1,0:T(8,128)(2,1)S(1)}, bf16[512,512]{1,0:T(8,128)(2,1)S(1)}, u32[]{:S(2)}, u32[]{:S(2)}) %collective-permute-start.12) | collective-permute-done | bytes 524320 | tf_op jit(solution)/shard_map/ppermute | solution.py:475
  142.9 7.8 %all-to-all-start.1 = ((bf16[64,8,2048]{2,1,0:T(8,128)(2,1)}), bf16[64,8,2048]{2,1,0:T(8,128)(2,1)S(1)}, u32[]{:S(2)}, u32[]{:S(2)}) async-start(bf16[64,8,2048]{2,1,0:T(8,128)(2,1)} %bitcast.29), calls=%async_computation.1 | async-start | bytes 4194304 | tf_op jit(solution)/shard_map/all_to_all | solution.py:484
  150.7 2.7 %collective-permute-start.18 = (bf16[512,512]{1,0:T(8,128)(2,1)}, bf16[512,512]{1,0:T(8,128)(2,1)}, u32[]{:S(2)}, u32[]{:S(2)}) collective-permute-start(bf16[512,512]{1,0:T(8,128)(2,1)} %copy-done.18), channel_id=1, source_target_pairs={{0,96},{32,0},{64,32},{96,64},{1,97},{33,1},{65,33},{97,65},{2,98}... | collective-permute-start | bytes 1572872 | tf_op jit(solution)/shard_map/ppermute | solution.py:475
  153.4 2.7 %collective-permute-start.16 = (bf16[512,512]{1,0:T(8,128)(2,1)}, bf16[512,512]{1,0:T(8,128)(2,1)}, u32[]{:S(2)}, u32[]{:S(2)}) collective-permute-start(bf16[512,512]{1,0:T(8,128)(2,1)} %copy-done.23), channel_id=1, source_target_pairs={{0,96},{32,0},{64,32},{96,64},{1,97},{33,1},{65,33},{97,65},{2,98}... | collective-permute-start | bytes 1572872 | tf_op jit(solution)/shard_map/ppermute | solution.py:475
  158.4 2.1 %place_grads.4 = (f32[4,1024,256]{2,1,0:T(8,128)}, f32[4,256,1024]{2,1,0:T(8,128)}) custom-call(s32[1]{0:T(128)} %get-tuple-element.113.spot_ref, f32[1024,512]{1,0:T(8,128)S(1)} %copy-done.5), custom_call_target="tpu_custom_call" | custom-call | flops 1 | bytes 1 | tf_op jit(solution)/shard_map/place_grads/pallas_call | solution.py:441
  160.5 17.9 %all-to-all-done.1 = bf16[64,8,2048]{2,1,0:T(8,128)(2,1)S(1)} async-done(((bf16[64,8,2048]{2,1,0:T(8,128)(2,1)}), bf16[64,8,2048]{2,1,0:T(8,128)(2,1)S(1)}, u32[]{:S(2)}, u32[]{:S(2)}) %all-to-all-start.1) | async-done | bytes 2097184 | tf_op jit(solution)/shard_map/all_to_all | solution.py:484
  180.1 4.2 %collective-permute-start.13 = (bf16[16,1024]{1,0:T(8,128)(2,1)S(1)}, bf16[16,1024]{1,0:T(8,128)(2,1)S(1)}, u32[]{:S(2)}, u32[]{:S(2)}) collective-permute-start(bf16[16,1024]{1,0:T(8,128)(2,1)S(1)} %get-tuple-element.107), channel_id=1, source_target_pairs={{0,16},{16,32},{32,48},{48,64},{64,80},{80,96},{96,112},{1,17},{17... | collective-permute-start | bytes 98312 | tf_op jit(solution)/shard_map/ppermute | solution.py:468
  184.3 2.4 %collective-permute-done.18.refs_1_ = bf16[512,512]{1,0:T(8,128)(2,1)} collective-permute-done((bf16[512,512]{1,0:T(8,128)(2,1)}, bf16[512,512]{1,0:T(8,128)(2,1)}, u32[]{:S(2)}, u32[]{:S(2)}) %collective-permute-start.18) | collective-permute-done | bytes 524320 | tf_op jit(solution)/shard_map/ppermute | solution.py:475
  186.7 2.8 %collective-permute-start.14 = (bf16[16,1024]{1,0:T(8,128)(2,1)S(1)}, bf16[16,1024]{1,0:T(8,128)(2,1)S(1)}, u32[]{:S(2)}, u32[]{:S(2)}) collective-permute-start(bf16[16,1024]{1,0:T(8,128)(2,1)S(1)} %get-tuple-element.106), channel_id=1, source_target_pairs={{16,0},{32,16},{48,32},{64,48},{80,64},{96,80},{112,96},{17,1},{33... | collective-permute-start | bytes 98312 | tf_op jit(solution)/shard_map/ppermute | solution.py:469
  191.0 3.1 %place_grads.5 = (f32[4,1024,256]{2,1,0:T(8,128)}, f32[4,256,1024]{2,1,0:T(8,128)}) custom-call(s32[1]{0:T(128)} %get-tuple-element.110.spot_ref, bf16[512,512]{1,0:T(8,128)(2,1)S(1)} %collective-permute-done.11.refs_0_, bf16[512,512]{1,0:T(8,128)(2,1)} %collective-permute-done.18.refs_1_, ...), custom_call_target="tpu_custom_call", output_to_operand_aliasing={{0}: (3, {}), {1}: (4, {})} | custom-call | flops 1 | bytes 1 | tf_op jit(solution)/shard_map/place_grads/pallas_call | solution.py:441
  194.1 3.1 %place_grads.6 = (f32[4,1024,256]{2,1,0:T(8,128)}, f32[4,256,1024]{2,1,0:T(8,128)}) custom-call(s32[1]{0:T(128)} %get-tuple-element.111.spot_ref, bf16[512,512]{1,0:T(8,128)(2,1)S(1)} %collective-permute-done.12.refs_0_, bf16[512,512]{1,0:T(8,128)(2,1)} %collective-permute-done.17.refs_1_, ...), custom_call_target="tpu_custom_call", output_to_operand_aliasing={{0}: (3, {}), {1}: (4, {})} | custom-call | flops 1 | bytes 1 | tf_op jit(solution)/shard_map/place_grads/pallas_call | solution.py:441
  198.9 3.3 %place_grads.7 = (f32[4,1024,256]{2,1,0:T(8,128)}, f32[4,256,1024]{2,1,0:T(8,128)}) custom-call(s32[1]{0:T(128)} %get-tuple-element.112.spot_ref, bf16[512,512]{1,0:T(8,128)(2,1)} %collective-permute-done.15.refs_0_, bf16[512,512]{1,0:T(8,128)(2,1)} %collective-permute-done.16.refs_1_, ...), custom_call_target="tpu_custom_call", output_to_operand_aliasing={{0}: (3, {}), {1}: (4, {})} | custom-call | flops 1 | bytes 1 | tf_op jit(solution)/shard_map/place_grads/pallas_call | solution.py:441
  202.2 3.5 %conv_down.1 = bf16[128,1024]{1,0:T(8,128)(2,1)} custom-call(bf16[16,1024]{1,0:T(8,128)(2,1)S(1)} %collective-permute-done.13.low_ref, bf16[128,1024]{1,0:T(8,128)(2,1)S(1)} %get-tuple-element.88.back_ref, bf16[16,1024]{1,0:T(8,128)(2,1)S(1)} %collective-permute-done.14.high_ref, f32[31,1024]{1,0:T(8,128)S(1)} %copy-done.11, ...), custom_call_target="tpu_custom_call" | custom-call | flops 1 | bytes 1 | tf_op jit(solution)/shard_map/conv_down/pallas_call | solution.py:417
  (82 shorter events, 34.7 us)
Async XLA Ops:
  3.8 10.8 %copy-start.20 = (s32[1,128,2]{1,2,0:T(2,128)S(1)}, s32[1,128,2]{1,2,0:T(2,128)}, u32[]{:S(2)}) copy-start(s32[1,128,2]{1,2,0:T(2,128)} %param.9) | copy-start | bytes 3076
  3.8 10.9 %copy-start.21 = (f32[1,128,2]{1,2,0:T(2,128)S(1)}, f32[1,128,2]{1,2,0:T(2,128)}, u32[]{:S(2)}) copy-start(f32[1,128,2]{1,2,0:T(2,128)} %param.10) | copy-start | bytes 3076
  3.8 11.0 %copy-start.9 = (bf16[1,128,1024]{2,1,0:T(8,128)(2,1)S(1)}, bf16[1,128,1024]{2,1,0:T(8,128)(2,1)}, u32[]{:S(2)}) copy-start(bf16[1,128,1024]{2,1,0:T(8,128)(2,1)} %param.13) | copy-start | bytes 786436
  6.9 15.5 %copy-start.10 = (f32[31,1024]{1,0:T(8,128)S(1)}, f32[31,1024]{1,0:T(8,128)}, u32[]{:S(2)}) copy-start(f32[31,1024]{1,0:T(8,128)} %kernel_ref.3) | copy-start | bytes 380932
  6.9 21.7 %collective-permute-start.2 = (bf16[512,512]{1,0:T(8,128)(2,1)}, bf16[512,512]{1,0:T(8,128)(2,1)S(1)}, u32[]{:S(2)}, u32[]{:S(2)}) collective-permute-start(bf16[512,512]{1,0:T(8,128)(2,1)} %get-tuple-element.56), channel_id=1, source_target_pairs={{0,32},{32,64},{64,96},{96,0},{1,33},{33,65},{65,97},{97,1},{2,34}... | collective-permute-start | bytes 1572872 | tf_op jit(solution)/shard_map/ppermute | solution.py:475
  8.2 20.4 %collective-permute-start.3 = (bf16[512,512]{1,0:T(8,128)(2,1)}, bf16[512,512]{1,0:T(8,128)(2,1)S(1)}, u32[]{:S(2)}, u32[]{:S(2)}) collective-permute-start(bf16[512,512]{1,0:T(8,128)(2,1)} %get-tuple-element.57), channel_id=1, source_target_pairs={{0,96},{32,0},{64,32},{96,64},{1,97},{33,1},{65,33},{97,65},{2,98}... | collective-permute-start | bytes 1572872 | tf_op jit(solution)/shard_map/ppermute | solution.py:475
  9.6 10.1 %collective-permute-start = (bf16[16,1024]{1,0:T(8,128)(2,1)S(1)}, bf16[16,1024]{1,0:T(8,128)(2,1)S(1)}, u32[]{:S(2)}, u32[]{:S(2)}) collective-permute-start(bf16[16,1024]{1,0:T(8,128)(2,1)S(1)} %get-tuple-element.109), channel_id=1, source_target_pairs={{0,16},{16,32},{32,48},{48,64},{64,80},{80,96},{96,112},{1,17},{17... | collective-permute-start | bytes 98312 | tf_op jit(solution)/shard_map/ppermute | solution.py:468
  12.7 9.7 %collective-permute-start.1 = (bf16[16,1024]{1,0:T(8,128)(2,1)S(1)}, bf16[16,1024]{1,0:T(8,128)(2,1)S(1)}, u32[]{:S(2)}, u32[]{:S(2)}) collective-permute-start(bf16[16,1024]{1,0:T(8,128)(2,1)S(1)} %get-tuple-element.108), channel_id=1, source_target_pairs={{16,0},{32,16},{48,32},{64,48},{80,64},{96,80},{112,96},{17,1},{33... | collective-permute-start | bytes 98312 | tf_op jit(solution)/shard_map/ppermute | solution.py:469
  28.6 39.6 %all-to-all-start = ((bf16[64,8,2048]{2,1,0:T(8,128)(2,1)}), bf16[64,8,2048]{2,1,0:T(8,128)(2,1)}, u32[]{:S(2)}, u32[]{:S(2)}) async-start(bf16[64,8,2048]{2,1,0:T(8,128)(2,1)} %bitcast.6), calls=%async_computation | async-start | bytes 4194304 | tf_op jit(solution)/shard_map/all_to_all | solution.py:484
  41.4 57.1 %collective-permute-start.6 = (bf16[1536,512]{1,0:T(8,128)(2,1)}, bf16[1536,512]{1,0:T(8,128)(2,1)S(1)}, u32[]{:S(2)}, u32[]{:S(2)}) collective-permute-start(bf16[1536,512]{1,0:T(8,128)(2,1)} %get-tuple-element.65), channel_id=1, source_target_pairs={{0,32},{32,64},{64,96},{96,0},{1,33},{33,65},{65,97},{97,1},{2,34}... | collective-permute-start | bytes 4718600 | tf_op jit(solution)/shard_map/ppermute | solution.py:475
  42.6 55.9 %collective-permute-start.7 = (bf16[1536,512]{1,0:T(8,128)(2,1)}, bf16[1536,512]{1,0:T(8,128)(2,1)S(1)}, u32[]{:S(2)}, u32[]{:S(2)}) collective-permute-start(bf16[1536,512]{1,0:T(8,128)(2,1)} %copy-done.8), channel_id=1, source_target_pairs={{0,96},{32,0},{64,32},{96,64},{1,97},{33,1},{65,33},{97,65},{2,98}... | collective-permute-start | bytes 4718600 | tf_op jit(solution)/shard_map/ppermute | solution.py:475
  68.2 6.1 %copy-start.4 = (bf16[1024,512]{1,0:T(8,128)(2,1)S(1)}, bf16[1024,512]{1,0:T(8,128)(2,1)}, u32[]{:S(2)}) copy-start(bf16[1024,512]{1,0:T(8,128)(2,1)} %copy-done.3) | copy-start | bytes 3145732
  70.0 2.7 %collective-permute-start.4 = (bf16[256,2048]{1,0:T(8,128)(2,1)S(1)}, bf16[256,2048]{1,0:T(8,128)(2,1)S(1)}, u32[]{:S(2)}, u32[]{:S(2)}) collective-permute-start(bf16[256,2048]{1,0:T(8,128)(2,1)S(1)} %get-tuple-element.105), channel_id=1, source_target_pairs={{0,16},{16,0},{1,17},{17,1},{2,18},{18,2},{3,19},{19,3},{4,20},{20... | collective-permute-start | bytes 3145736 | tf_op jit(solution)/shard_map/ppermute | solution.py:479
  70.5 3.8 %collective-permute-start.5 = (bf16[256,2048]{1,0:T(8,128)(2,1)S(1)}, bf16[256,2048]{1,0:T(8,128)(2,1)S(1)}, u32[]{:S(2)}, u32[]{:S(2)}) collective-permute-start(bf16[256,2048]{1,0:T(8,128)(2,1)S(1)} %get-tuple-element.104), channel_id=1, source_target_pairs={{0,16},{16,0},{1,17},{17,1},{2,18},{18,2},{3,19},{19,3},{4,20},{20... | collective-permute-start | bytes 3145736 | tf_op jit(solution)/shard_map/ppermute | solution.py:479
  98.5 8.6 %copy-start = (bf16[1536,512]{1,0:T(8,128)(2,1)}, bf16[1536,512]{1,0:T(8,128)(2,1)S(1)}, u32[]{:S(2)}) copy-start(bf16[1536,512]{1,0:T(8,128)(2,1)S(1)} %collective-permute-done.6.refs_3_.refs_9_) | copy-start | bytes 4718596
  104.3 14.4 %collective-permute-start.8 = (bf16[512,512]{1,0:T(8,128)(2,1)S(1)}, bf16[512,512]{1,0:T(8,128)(2,1)S(1)}, u32[]{:S(2)}, u32[]{:S(2)}) collective-permute-start(bf16[512,512]{1,0:T(8,128)(2,1)S(1)} %get-tuple-element.73), channel_id=1, source_target_pairs={{0,32},{32,64},{64,96},{96,0},{1,33},{33,65},{65,97},{97,1},{2,34}... | collective-permute-start | bytes 1572872 | tf_op jit(solution)/shard_map/ppermute | solution.py:475
  104.4 7.7 %copy-start.2 = (bf16[1536,512]{1,0:T(8,128)(2,1)S(1)}, bf16[1536,512]{1,0:T(8,128)(2,1)}, u32[]{:S(2)}) copy-start(bf16[1536,512]{1,0:T(8,128)(2,1)} %copy-done.1) | copy-start | bytes 4718596
  104.4 14.3 %collective-permute-start.9 = (bf16[512,512]{1,0:T(8,128)(2,1)S(1)}, bf16[512,512]{1,0:T(8,128)(2,1)S(1)}, u32[]{:S(2)}, u32[]{:S(2)}) collective-permute-start(bf16[512,512]{1,0:T(8,128)(2,1)S(1)} %get-tuple-element.74), channel_id=1, source_target_pairs={{0,96},{32,0},{64,32},{96,64},{1,97},{33,1},{65,33},{97,65},{2,98}... | collective-permute-start | bytes 1572872 | tf_op jit(solution)/shard_map/ppermute | solution.py:475
  116.4 8.3 %copy-start.17 = (bf16[512,512]{1,0:T(8,128)(2,1)}, bf16[512,512]{1,0:T(8,128)(2,1)S(1)}, u32[]{:S(2)}) copy-start(bf16[512,512]{1,0:T(8,128)(2,1)S(1)} %get-tuple-element.93) | copy-start | bytes 1572868
  118.7 5.9 %copy-start.22 = (bf16[512,512]{1,0:T(8,128)(2,1)}, bf16[512,512]{1,0:T(8,128)(2,1)S(1)}, u32[]{:S(2)}) copy-start(bf16[512,512]{1,0:T(8,128)(2,1)S(1)} %collective-permute-done.8) | copy-start | bytes 1572868
  118.7 5.9 %copy-start.23 = (bf16[512,512]{1,0:T(8,128)(2,1)}, bf16[512,512]{1,0:T(8,128)(2,1)S(1)}, u32[]{:S(2)}) copy-start(bf16[512,512]{1,0:T(8,128)(2,1)S(1)} %collective-permute-done.9) | copy-start | bytes 1572868
  124.7 5.3 %collective-permute-start.10 = (bf16[512,2048]{1,0:T(8,128)(2,1)}, bf16[512,2048]{1,0:T(8,128)(2,1)S(1)}, u32[]{:S(2)}, u32[]{:S(2)}) collective-permute-start(bf16[512,2048]{1,0:T(8,128)(2,1)} %back_to_width.2), channel_id=1, source_target_pairs={{0,16},{16,0},{1,17},{17,1},{2,18},{18,2},{3,19},{19,3},{4,20},{20... | collective-permute-start | bytes 6291464 | tf_op jit(solution)/shard_map/ppermute | solution.py:479
  126.0 13.8 %collective-permute-start.11 = (bf16[512,512]{1,0:T(8,128)(2,1)S(1)}, bf16[512,512]{1,0:T(8,128)(2,1)S(1)}, u32[]{:S(2)}, u32[]{:S(2)}) collective-permute-start(bf16[512,512]{1,0:T(8,128)(2,1)S(1)} %get-tuple-element.80), channel_id=1, source_target_pairs={{0,96},{32,0},{64,32},{96,64},{1,97},{33,1},{65,33},{97,65},{2,98}... | collective-permute-start | bytes 1572872 | tf_op jit(solution)/shard_map/ppermute | solution.py:475
  128.5 14.4 %collective-permute-start.12 = (bf16[512,512]{1,0:T(8,128)(2,1)S(1)}, bf16[512,512]{1,0:T(8,128)(2,1)S(1)}, u32[]{:S(2)}, u32[]{:S(2)}) collective-permute-start(bf16[512,512]{1,0:T(8,128)(2,1)S(1)} %get-tuple-element.81), channel_id=1, source_target_pairs={{0,32},{32,64},{64,96},{96,0},{1,33},{33,65},{65,97},{97,1},{2,34}... | collective-permute-start | bytes 1572872 | tf_op jit(solution)/shard_map/ppermute | solution.py:475
  142.9 35.5 %all-to-all-start.1 = ((bf16[64,8,2048]{2,1,0:T(8,128)(2,1)}), bf16[64,8,2048]{2,1,0:T(8,128)(2,1)S(1)}, u32[]{:S(2)}, u32[]{:S(2)}) async-start(bf16[64,8,2048]{2,1,0:T(8,128)(2,1)} %bitcast.29), calls=%async_computation.1 | async-start | bytes 4194304 | tf_op jit(solution)/shard_map/all_to_all | solution.py:484
  150.7 36.0 %collective-permute-start.18 = (bf16[512,512]{1,0:T(8,128)(2,1)}, bf16[512,512]{1,0:T(8,128)(2,1)}, u32[]{:S(2)}, u32[]{:S(2)}) collective-permute-start(bf16[512,512]{1,0:T(8,128)(2,1)} %copy-done.18), channel_id=1, source_target_pairs={{0,96},{32,0},{64,32},{96,64},{1,97},{33,1},{65,33},{97,65},{2,98}... | collective-permute-start | bytes 1572872 | tf_op jit(solution)/shard_map/ppermute | solution.py:475
  153.4 40.7 %collective-permute-start.17 = (bf16[512,512]{1,0:T(8,128)(2,1)}, bf16[512,512]{1,0:T(8,128)(2,1)}, u32[]{:S(2)}, u32[]{:S(2)}) collective-permute-start(bf16[512,512]{1,0:T(8,128)(2,1)} %copy-done.17), channel_id=1, source_target_pairs={{0,32},{32,64},{64,96},{96,0},{1,33},{33,65},{65,97},{97,1},{2,34}... | collective-permute-start | bytes 1572872 | tf_op jit(solution)/shard_map/ppermute | solution.py:475
  153.4 45.5 %collective-permute-start.15 = (bf16[512,512]{1,0:T(8,128)(2,1)}, bf16[512,512]{1,0:T(8,128)(2,1)}, u32[]{:S(2)}, u32[]{:S(2)}) collective-permute-start(bf16[512,512]{1,0:T(8,128)(2,1)} %copy-done.22), channel_id=1, source_target_pairs={{0,32},{32,64},{64,96},{96,0},{1,33},{33,65},{65,97},{97,1},{2,34}... | collective-permute-start | bytes 1572872 | tf_op jit(solution)/shard_map/ppermute | solution.py:475
  153.4 45.4 %collective-permute-start.16 = (bf16[512,512]{1,0:T(8,128)(2,1)}, bf16[512,512]{1,0:T(8,128)(2,1)}, u32[]{:S(2)}, u32[]{:S(2)}) collective-permute-start(bf16[512,512]{1,0:T(8,128)(2,1)} %copy-done.23), channel_id=1, source_target_pairs={{0,96},{32,0},{64,32},{96,64},{1,97},{33,1},{65,33},{97,65},{2,98}... | collective-permute-start | bytes 1572872 | tf_op jit(solution)/shard_map/ppermute | solution.py:475
  179.4 10.2 %copy-start.16 = (bf16[128,1024]{1,0:T(8,128)(2,1)S(1)}, bf16[128,1024]{1,0:T(8,128)(2,1)}, u32[]{:S(2)}) copy-start(bf16[128,1024]{1,0:T(8,128)(2,1)} %copy-done.15) | copy-start | bytes 786436
  180.1 22.0 %collective-permute-start.13 = (bf16[16,1024]{1,0:T(8,128)(2,1)S(1)}, bf16[16,1024]{1,0:T(8,128)(2,1)S(1)}, u32[]{:S(2)}, u32[]{:S(2)}) collective-permute-start(bf16[16,1024]{1,0:T(8,128)(2,1)S(1)} %get-tuple-element.107), channel_id=1, source_target_pairs={{0,16},{16,32},{32,48},{48,64},{64,80},{80,96},{96,112},{1,17},{17... | collective-permute-start | bytes 98312 | tf_op jit(solution)/shard_map/ppermute | solution.py:468
  186.7 15.4 %collective-permute-start.14 = (bf16[16,1024]{1,0:T(8,128)(2,1)S(1)}, bf16[16,1024]{1,0:T(8,128)(2,1)S(1)}, u32[]{:S(2)}, u32[]{:S(2)}) collective-permute-start(bf16[16,1024]{1,0:T(8,128)(2,1)S(1)} %get-tuple-element.106), channel_id=1, source_target_pairs={{16,0},{32,16},{48,32},{64,48},{80,64},{96,80},{112,96},{17,1},{33... | collective-permute-start | bytes 98312 | tf_op jit(solution)/shard_map/ppermute | solution.py:469
  (13 other events, 21.9 us)

commit v4 on v3

--- a/solution.py
+++ b/solution.py
@@ -165,68 +165,40 @@
     _, width, hidden = w_in.shape
     pieces = width // hidden
     half = width // 2
-
-    def body(spots_ref, in_ref, out_ref, own_ref, first_up, first_down, next_up, next_down, sems):
+    rows = (width, half, half, width, width)
+
+    def body(spots_ref, in_ref, out_ref, own_ref, far_up, far_down, near_up, near_down, sems):
         copies = []
 
         def move(source, target):
             copies.append(pltpu.make_async_copy(source, target, sems.at[len(copies)]))
 
-        def pack(steps, low, high, ref, offset):
+        def pack(steps, low, high, ref):
             spot = spots_ref[steps]
-            move(
-                in_ref.at[spot, pl.ds(low, high - low)],
-                ref.at[pl.ds(offset, high - low), :hidden],
-            )
+            move(in_ref.at[spot, pl.ds(low, high - low)], ref.at[:, :hidden])
             for start in range(low, high, hidden):
                 move(
                     out_ref.at[spot, :, pl.ds(start, hidden)],
-                    ref.at[pl.ds(offset + start - low, hidden), hidden:],
+                    ref.at[pl.ds(start - low, hidden), hidden:],
                 )
 
-        pack(2, 0, half, first_up, 0)
-        pack(2, half, width, first_down, 0)
-        pack(1, 0, width, next_up, half)
-        pack(3, 0, width, next_down, half)
-        pack(0, 0, width, own_ref, 0)
+        pack(2, 0, half, far_up)
+        pack(2, half, width, far_down)
+        pack(1, 0, width, near_up)
+        pack(3, 0, width, near_down)
+        pack(0, 0, width, own_ref)
         copy_all(copies)
 
-    rows = (width, half, half, width + half, width + half)
     return pl.pallas_call(
         body,
         in_specs=[pl.BlockSpec(memory_space=pltpu.SMEM)] + [pl.BlockSpec(memory_space=pl.ANY)] * 2,
         out_specs=[pl.BlockSpec(memory_space=pl.ANY)] * len(rows),
         out_shape=[shape_of((count, 2 * hidden), BF16) for count in rows],
-        scratch_shapes=[pltpu.SemaphoreType.DMA((4 * (1 + pieces) + 1,))],
+        scratch_shapes=[pltpu.SemaphoreType.DMA((4 * pieces + 5,))],
         compiler_params=params(16),
         cost_estimate=COST,
         name="pack_weights",
     )(spots, w_in, w_out)
-
-
-def fill_first(parts, wholes):
-    count = parts[0].shape[0]
-
-    def body(*refs):
-        sems = refs[-1]
-        copy_all(
-            [
-                pltpu.make_async_copy(refs[i], refs[4 + i].at[:count], sems.at[i])
-                for i in range(2)
-            ]
-        )
-
-    return pl.pallas_call(
-        body,
-        in_specs=[pl.BlockSpec(memory_space=pl.ANY)] * 4,
-        out_specs=[pl.BlockSpec(memory_space=pl.ANY)] * 2,
-        out_shape=[shape_of(whole.shape, BF16) for whole in wholes],
-        input_output_aliases={2: 0, 3: 1},
-        scratch_shapes=[pltpu.SemaphoreType.DMA((2,))],
-        compiler_params=params(16),
-        cost_estimate=COST,
-        name="fill_first",
-    )(*parts, *wholes)
 
 
 def listed_refs(quarters, refs, arrays):
@@ -461,6 +433,56 @@
     )(spot, *parts, *held)
 
 
+def picked(index, values):
+    result = values[-1]
+    for spot, value in enumerate(values[:-1]):
+        result = jnp.where(index == spot, value, result)
+    return result
+
+
+def place_halves(spots, chosen, parts, count, held):
+    hidden = parts[0][0].shape[1] // 2
+    half = 2 * hidden
+    amount = len(parts)
+    steps, sides = zip(*chosen)
+
+    def body(spots_ref, *refs):
+        in_ref, out_ref = refs[-2:]
+        for index in range(amount):
+
+            @pl.when(pl.program_id(0) == index)
+            def _():
+                in_ref[0] = refs[index][:, :hidden].astype(F32)
+                for piece in range(0, half, hidden):
+                    rows = slice(piece, piece + hidden)
+                    out_ref[0, :, rows] = refs[index][rows, hidden:].astype(F32)
+
+    return pl.pallas_call(
+        body,
+        grid_spec=pltpu.PrefetchScalarGridSpec(
+            num_scalar_prefetch=1,
+            grid=(amount,),
+            in_specs=[
+                pl.BlockSpec((half, 2 * hidden), lambda i, spots, side=side: (side, 0))
+                for _, side in parts
+            ]
+            + [pl.BlockSpec(memory_space=pl.ANY)] * 2,
+            out_specs=(
+                pl.BlockSpec((1, half, hidden), lambda i, spots: (spots[picked(i, steps)], picked(i, sides), 0)),
+                pl.BlockSpec((1, hidden, half), lambda i, spots: (spots[picked(i, steps)], 0, picked(i, sides))),
+            ),
+        ),
+        out_shape=(
+            shape_of((count, 2 * half, hidden), F32),
+            shape_of((count, hidden, 2 * half), F32),
+        ),
+        input_output_aliases={1 + amount: 0, 2 + amount: 1},
+        compiler_params=params(32),
+        cost_estimate=COST,
+        name="place_halves",
+    )(spots, *[part for part, _ in parts], *held)
+
+
 def edges(block):
     count = lax.axis_size("y") * lax.axis_size("core")
     forward = [(i, i + 1) for i in range(count - 1)]
@@ -495,15 +517,18 @@
     spots = (y + jnp.arange(n_y, dtype=jnp.int32)) % n_y
 
     low, high = edges(frames)
-    own_block, first_up, first_down, next_up, next_down = pack_weights(spots, w_in, w_out)
-    first_up, first_down = turn(first_up, 1), turn(first_down, -1)
+    own_block, far_up, far_down, near_up, near_down = pack_weights(spots, w_in, w_out)
+    far_up, far_down = turn(far_up, 1), turn(far_down, -1)
+    near_up, near_down = turn(near_up, 1), turn(near_down, -1)
 
     send = down_slots(routes, gates, cotangent, experts, n_y)
     mixing, hidden, send = conv_up(low, frames, high, conv_kernel, routes, send, experts, n_y)
-    send, first_up, first_down = lax.optimization_barrier((send, first_up, first_down))
+    send, far_up, far_down, near_up, near_down = lax.optimization_barrier(
+        (send, far_up, far_down, near_up, near_down)
+    )
     own = exchange(send, groups)
-    next_up, next_down = fill_first((first_up, first_down), (next_up, next_down))
-    next_up, next_down = turn(next_up, 1), turn(next_down, -1)
+    far_up, far_down = turn(far_up, 1), turn(far_down, -1)
+    own, far_up, far_down = lax.optimization_barrier((own, far_up, far_down))
     middle = own.shape[0] // 2
     rows = [own, swap(own[:middle]), swap(own[middle:])]
 
@@ -514,34 +539,40 @@
 
     acts, pres, grads, packed = {}, {}, {}, {0: quarters(own_block, 0, 4)}
     acts[0], pres[0], *grads[0] = block_step(rows, packed[0], F32, 1)
-    acts[0], next_up, next_down = lax.optimization_barrier((acts[0], next_up, next_down))
-    packed[2] = quarters(next_up, 0, 2) + quarters(next_down, 0, 2)
-    packed[1] = quarters(next_up, 2 * step, 4)
-    packed[3] = quarters(next_down, 2 * step, 4)
+    packed[2] = quarters(far_up, 0, 2) + quarters(far_down, 0, 2)
     acts[2], pres[2], up, down = block_step(rows, packed[2], BF16, 2)
     up, down = turn(up, 1), turn(down, -1)
+    acts[2], near_up, near_down = lax.optimization_barrier((acts[2], near_up, near_down))
+    packed[1], packed[3] = quarters(near_up, 0, 4), quarters(near_down, 0, 4)
     for steps in (1, 3):
         acts[steps], pres[steps], *grads[steps] = block_step(rows, packed[steps], BF16, 2)
-        grads[steps] = [turn(part, -steps) for part in grads[steps]]
+        grads[steps][0] = turn(grads[steps][0], -steps)
     acts[3], up, down = lax.optimization_barrier((acts[3], up, down))
-    grads[2] = [turn(up, 1), turn(down, -1)]
+    late_up = jnp.concatenate([grads[3][1], up])
+    late_down = jnp.concatenate([grads[1][1], down])
     listed = [[held[steps] for steps in packed] for held in (acts, pres, packed)]
     arrived = swap(back_to_width(1, *listed, []))
     result = back_to_width(0, *listed, [arrived])
-    result, grads[1][0], grads[3][0] = lax.optimization_barrier((result, grads[1][0], grads[3][0]))
+    result, grads[1][0], grads[3][0], late_up, late_down = lax.optimization_barrier(
+        (result, grads[1][0], grads[3][0], late_up, late_down)
+    )
+    late_up, late_down = turn(late_up, 1), turn(late_down, -1)
     returned = exchange(result, groups)
 
-    held = ()
-    for steps in (0,):
-        held = place_grads(spots[steps : steps + 1], grads[steps], n_y, held)
+    held = place_grads(spots, grads[0], n_y, ())
+
+    held = place_halves(spots, ((1, 0), (3, 0)), [(grads[1][0], 0), (grads[3][0], 0)], n_y, held)
     returned, *held = lax.optimization_barrier((returned, *held))
     hidden_grad, back = grad_rows(routes, cotangent, mixing, returned, experts, n_y)
     low, high = edges(back)
     frames_grad = conv_down(low, back, high, conv_kernel, hidden_grad)
     mixed = mix_out(routes, gates, hidden, returned, experts, n_y)
-    for steps in (1, 3, 2):
-        held = place_grads(spots[steps : steps + 1], grads[steps], n_y, held)
-    w_in_grad, w_out_grad = held
+    frames_grad, mixed, late_up, late_down = lax.optimization_barrier(
+        (frames_grad, mixed, late_up, late_down)
+    )
+    w_in_grad, w_out_grad = place_halves(
+        spots, ((1, 1), (3, 1), (2, 0), (2, 1)), [(late_down, 0), (late_up, 0), (late_up, 1), (late_down, 1)], n_y, held
+    )
     return (mixed[None], frames_grad[None], w_in_grad, w_out_grad)
 
 

time: 207 us -> 220 us (1.063)
  waiting for transfers between devices: 83 us -> 98.7 us
  Pallas kernels: 57.6 us -> 53 us
    ppermute x2, waiting for transfers between devices: 2.71 us -> 38.3 us  [edges(): high = lax.ppermute(block[:EDGE], ('y', 'core'), backward)]
    all_to_all x2, waiting for transfers between devices: 42 us -> 18.6 us  [exchange(): lax.all_to_all(grouped, ('y', 'exp'), split_axis=0, concat_axis=0, tiled=...]
    pallas_call x4 -> x1, Pallas kernels: 11.6 us -> 2.01 us  [place_grads(): pl.pallas_call(body, grid_spec=pltpu.PrefetchScalarGridSpec(num_scalar_pr...]
    ppermute x12, waiting for transfers between devices: 30.4 us -> 37.1 us  [turn(): lax.ppermute(block, 'y', [(i, (i + steps) % count) for i in range(count)])]
    pallas_call x1 -> x2, Pallas kernels: 0.82 us -> 6.22 us  [place_halves(): pl.pallas_call(body, grid_spec=pltpu.PrefetchScalarGridSpec(num_scalar_pr...]
    ppermute x2, starting transfers between devices: 7.21 us -> 4.01 us  [edges(): low = lax.ppermute(block[-EDGE:], ('y', 'core'), forward)]
    ppermute x2, waiting for transfers between devices: 2.71 us -> 0.01 us  [edges(): low = lax.ppermute(block[-EDGE:], ('y', 'core'), forward)]
    ppermute x2, starting transfers between devices: 4.72 us -> 7.31 us  [edges(): high = lax.ppermute(block[:EDGE], ('y', 'core'), backward)]
  transfers between devices with their start and end apart: 21 -> 21, of which waited for: 13 -> 9; matrix products, arithmetic and copies ran while one was open for 1% -> 1% of each run, Pallas kernels for 20% -> 17%
where the time goes in v4:
time: 220 us; the launch traced here: 219 us
  waiting for transfers between devices  98.7 us (45%)
  Pallas kernels  53 us (24%)
  starting transfers between devices  47.6 us (22%)
  local copies, waits for them, and re-layouts  17.1 us (8%)
    ppermute x2, waiting for transfers between devices, edges(): high = lax.ppermute(block[:EDGE], ('y', 'core'), backward)  38.3 us
    ppermute x12, waiting for transfers between devices, turn(): lax.ppermute(block, 'y', [(i, (i + steps) % count) for i in range(count)])  37.1 us
    all_to_all x2, starting transfers between devices, exchange(): lax.all_to_all(grouped, ('y', 'exp'), split_axis=0, concat_axis=0, tiled=...  18.9 us
    all_to_all x2, waiting for transfers between devices, exchange(): lax.all_to_all(grouped, ('y', 'exp'), split_axis=0, concat_axis=0, tiled=...  18.6 us
    pallas_call x4, Pallas kernels, block_step(): pl.pallas_call(body, out_shape=result, compiler_params=params(48), cost_e...  17.5 us
    ppermute x12, starting transfers between devices, turn(): lax.ppermute(block, 'y', [(i, (i + steps) % count) for i in range(count)])  15.3 us
    unnamed x56, local copies, waits for them, and re-layouts  13.8 us
    pallas_call x2, Pallas kernels, back_to_width(): pl.pallas_call(body, out_shape=shape_of((rows, 2 * width), BF16), compile...  11.8 us
  transfers between devices with their start and end apart: 21, of which 9 were waited for; matrix products, arithmetic and copies ran while one was open for 1% of the time, Pallas kernels for 17%

profile of v4, /device:TPU:5, one launch (start us, length us, event | category | flops | bytes accessed | tf_op | source)
XLA Modules:
  0.0 218.8 jit_solution(9533509663698920277)
XLA Ops:
  0.7 1.6 copy-done.8
  2.2 1.6 copy-done.9
  3.8 2.4 %pack_weights.1 = (bf16[1024,512]{1,0:T(8,128)(2,1)S(1)}, bf16[512,512]{1,0:T(8,128)(2,1)}, bf16[512,512]{1,0:T(8,128)(2,1)}, bf16[1024,512]{1,0:T(8,128)(2,1)}, bf16[1024,512]{1,0:T(8,128)(2,1)}) custom-call(s32[4]{0:T(128)S(1)} %and_select_fusion.spots_ref.spot_ref, bf16[4,1024,256]{2,1,0:T(8,128)(2,1)S(1)} %copy-done.8, bf16[4,256,1024]{2,1,0:T(8,128)(2,1)S(1)} %copy-done.9), custom_call_target="tpu_custom_call" | custom-call | flops 1 | bytes 1 | tf_op jit(solution)/shard_map/pack_weights/pallas_call | solution.py:192
  7.6 1.5 collective-permute-start.5
  9.1 2.7 %collective-permute-start.3 = (bf16[512,512]{1,0:T(8,128)(2,1)}, bf16[512,512]{1,0:T(8,128)(2,1)}, u32[]{:S(2)}, u32[]{:S(2)}) collective-permute-start(bf16[512,512]{1,0:T(8,128)(2,1)} %get-tuple-element.64), channel_id=1, source_target_pairs={{0,96},{32,0},{64,32},{96,64},{1,97},{33,1},{65,33},{97,65},{2,98}... | collective-permute-start | bytes 1572872 | tf_op jit(solution)/shard_map/ppermute | solution.py:497
  13.2 3.6 %collective-permute-start.1 = (bf16[16,1024]{1,0:T(8,128)(2,1)S(1)}, bf16[16,1024]{1,0:T(8,128)(2,1)S(1)}, u32[]{:S(2)}, u32[]{:S(2)}) collective-permute-start(bf16[16,1024]{1,0:T(8,128)(2,1)S(1)} %get-tuple-element.122), channel_id=1, source_target_pairs={{16,0},{32,16},{48,32},{64,48},{80,64},{96,80},{112,96},{17,1},{33... | collective-permute-start | bytes 98312 | tf_op jit(solution)/shard_map/ppermute | solution.py:491
  16.8 27.6 %collective-permute-done.1.high_ref = bf16[16,1024]{1,0:T(8,128)(2,1)S(1)} collective-permute-done((bf16[16,1024]{1,0:T(8,128)(2,1)S(1)}, bf16[16,1024]{1,0:T(8,128)(2,1)S(1)}, u32[]{:S(2)}, u32[]{:S(2)}) %collective-permute-start.1) | collective-permute-done | bytes 32800 | tf_op jit(solution)/shard_map/ppermute | solution.py:491
  45.0 1.9 collective-permute-start
  47.2 2.1 down_slots.1._
  49.3 5.4 %conv_up.1 = (f32[128,1024]{1,0:T(8,128)S(1)}, bf16[128,1024]{1,0:T(8,128)(2,1)S(1)}, bf16[512,2048]{1,0:T(8,128)(2,1)}) custom-call(bf16[16,1024]{1,0:T(8,128)(2,1)} %collective-permute-done.low_ref, bf16[128,1024]{1,0:T(8,128)(2,1)S(1)} %bitcast.24, bf16[16,1024]{1,0:T(8,128)(2,1)S(1)} %copy-done.23, ...), custom_call_target="tpu_custom_call", output_to_operand_aliasing={{2}: (5, {})} | custom-call | flops 1 | bytes 1 | tf_op jit(solution)/shard_map/conv_up/pallas_call | solution.py:131
  56.3 10.8 %all-to-all-start = ((bf16[64,8,2048]{2,1,0:T(8,128)(2,1)}), bf16[64,8,2048]{2,1,0:T(8,128)(2,1)}, u32[]{:S(2)}, u32[]{:S(2)}) async-start(bf16[64,8,2048]{2,1,0:T(8,128)(2,1)} %bitcast.6), calls=%async_computation | async-start | bytes 4194304 | tf_op jit(solution)/shard_map/all_to_all | solution.py:506
  69.9 33.9 %collective-permute-done.6.refs_3_.refs_9_ = bf16[512,512]{1,0:T(8,128)(2,1)S(1)} collective-permute-done((bf16[512,512]{1,0:T(8,128)(2,1)}, bf16[512,512]{1,0:T(8,128)(2,1)S(1)}, u32[]{:S(2)}, u32[]{:S(2)}) %collective-permute-start.6) | collective-permute-done | bytes 524320 | tf_op jit(solution)/shard_map/ppermute | solution.py:497
  105.4 1.9 fusion.1
  108.4 2.2 %collective-permute-done.9.refs_2_ = bf16[256,2048]{1,0:T(8,128)(2,1)S(1)} collective-permute-done((bf16[256,2048]{1,0:T(8,128)(2,1)S(1)}, bf16[256,2048]{1,0:T(8,128)(2,1)S(1)}, u32[]{:S(2)}, u32[]{:S(2)}) %collective-permute-start.9) | collective-permute-done | bytes 1048608 | tf_op jit(solution)/shard_map/ppermute | solution.py:501
  112.1 4.0 %block_step.5 = (bf16[1024,256]{1,0:T(8,128)(2,1)S(1)}, bf16[1024,256]{1,0:T(8,128)(2,1)S(1)}, bf16[512,512]{1,0:T(8,128)(2,1)S(1)}, bf16[512,512]{1,0:T(8,128)(2,1)S(1)}) custom-call(bf16[512,2048]{1,0:T(8,128)(2,1)} %bitcast.7.refs_0_, bf16[256,2048]{1,0:T(8,128)(2,1)S(1)} %collective-permute-done.8.refs_1_, ...), custom_call_target="tpu_custom_call" | custom-call | flops 1 | bytes 1 | tf_op jit(solution)/shard_map/block_step/pallas_call | solution.py:272
  116.2 2.7 %collective-permute-start.11 = (bf16[512,512]{1,0:T(8,128)(2,1)S(1)}, bf16[512,512]{1,0:T(8,128)(2,1)S(1)}, u32[]{:S(2)}, u32[]{:S(2)}) collective-permute-start(bf16[512,512]{1,0:T(8,128)(2,1)S(1)} %get-tuple-element.84), channel_id=1, source_target_pairs={{0,96},{32,0},{64,32},{96,64},{1,97},{33,1},{65,33},{97,65},{2,98}... | collective-permute-start | bytes 1572872 | tf_op jit(solution)/shard_map/ppermute | solution.py:497
  118.9 4.0 %block_step.6 = (bf16[1024,256]{1,0:T(8,128)(2,1)S(1)}, bf16[1024,256]{1,0:T(8,128)(2,1)S(1)}, bf16[512,512]{1,0:T(8,128)(2,1)S(1)}, bf16[512,512]{1,0:T(8,128)(2,1)S(1)}) custom-call(bf16[512,2048]{1,0:T(8,128)(2,1)} %bitcast.7.refs_0_, bf16[256,2048]{1,0:T(8,128)(2,1)S(1)} %collective-permute-done.8.refs_1_, ...), custom_call_target="tpu_custom_call" | custom-call | flops 1 | bytes 1 | tf_op jit(solution)/shard_map/block_step/pallas_call | solution.py:272
  123.0 4.0 %block_step.7 = (bf16[1024,256]{1,0:T(8,128)(2,1)S(1)}, bf16[1024,256]{1,0:T(8,128)(2,1)S(1)}, bf16[512,512]{1,0:T(8,128)(2,1)S(1)}, bf16[512,512]{1,0:T(8,128)(2,1)S(1)}) custom-call(bf16[512,2048]{1,0:T(8,128)(2,1)} %bitcast.7.refs_0_, bf16[256,2048]{1,0:T(8,128)(2,1)S(1)} %collective-permute-done.8.refs_1_, ...), custom_call_target="tpu_custom_call" | custom-call | flops 1 | bytes 1 | tf_op jit(solution)/shard_map/block_step/pallas_call | solution.py:272
  127.0 5.4 %block_step.4 = (bf16[1024,256]{1,0:T(8,128)(2,1)S(1)}, bf16[1024,256]{1,0:T(8,128)(2,1)S(1)}, f32[1024,512]{1,0:T(8,128)}) custom-call(bf16[512,2048]{1,0:T(8,128)(2,1)} %bitcast.7.refs_0_, bf16[256,2048]{1,0:T(8,128)(2,1)S(1)} %collective-permute-done.8.refs_1_, bf16[256,2048]{1,0:T(8,128)(2,1)S(1)} %collective-permute-done.9.refs_2_, ...), custom_call_target="tpu_custom_call" | custom-call | flops 1 | bytes 1 | tf_op jit(solution)/shard_map/block_step/pallas_call | solution.py:272
  132.4 5.5 %back_to_width.2 = bf16[512,2048]{1,0:T(8,128)(2,1)} custom-call(bf16[1024,256]{1,0:T(8,128)(2,1)S(1)} %get-tuple-element.72.refs_0_, bf16[1024,256]{1,0:T(8,128)(2,1)S(1)} %get-tuple-element.78.refs_1_, bf16[1024,256]{1,0:T(8,128)(2,1)S(1)} %get-tuple-element.80.refs_2_, bf16[1024,256]{1,0:T(8,128)(2,1)S(1)} %get-tuple-element.85.refs_3_, ...), custom_call_target="tpu_custom_call" | custom-call | flops 1 | bytes 1 | tf_op jit(solution)/shard_map/back_to_width/pallas_call | solution.py:311
  144.1 6.2 %back_to_width.3 = bf16[512,2048]{1,0:T(8,128)(2,1)} custom-call(bf16[1024,256]{1,0:T(8,128)(2,1)S(1)} %get-tuple-element.72.refs_0_, bf16[1024,256]{1,0:T(8,128)(2,1)S(1)} %get-tuple-element.78.refs_1_, bf16[1024,256]{1,0:T(8,128)(2,1)S(1)} %get-tuple-element.80.refs_2_, bf16[1024,256]{1,0:T(8,128)(2,1)S(1)} %get-tuple-element.85.refs_3_, ...), custom_call_target="tpu_custom_call" | custom-call | flops 1 | bytes 1 | tf_op jit(solution)/shard_map/back_to_width/pallas_call | solution.py:311
  150.4 2.0 collective-permute-done.13.refs_0_
  155.2 8.1 %all-to-all-start.1 = ((bf16[64,8,2048]{2,1,0:T(8,128)(2,1)}), bf16[64,8,2048]{2,1,0:T(8,128)(2,1)S(1)}, u32[]{:S(2)}, u32[]{:S(2)}) async-start(bf16[64,8,2048]{2,1,0:T(8,128)(2,1)} %bitcast.25), calls=%async_computation.1 | async-start | bytes 4194304 | tf_op jit(solution)/shard_map/all_to_all | solution.py:506
  166.1 1.6 copy-done.7
  167.7 2.0 place_grads.1
  170.7 2.0 place_halves.2
  172.7 18.6 %all-to-all-done.1 = bf16[64,8,2048]{2,1,0:T(8,128)(2,1)S(1)} async-done(((bf16[64,8,2048]{2,1,0:T(8,128)(2,1)}), bf16[64,8,2048]{2,1,0:T(8,128)(2,1)S(1)}, u32[]{:S(2)}, u32[]{:S(2)}) %all-to-all-start.1) | async-done | bytes 2097184 | tf_op jit(solution)/shard_map/all_to_all | solution.py:506
  193.1 3.8 %collective-permute-start.16 = (bf16[16,1024]{1,0:T(8,128)(2,1)S(1)}, bf16[16,1024]{1,0:T(8,128)(2,1)S(1)}, u32[]{:S(2)}, u32[]{:S(2)}) collective-permute-start(bf16[16,1024]{1,0:T(8,128)(2,1)S(1)} %get-tuple-element.120), channel_id=1, source_target_pairs={{16,0},{32,16},{48,32},{64,48},{80,64},{96,80},{112,96},{17,1},{33... | collective-permute-start | bytes 98312 | tf_op jit(solution)/shard_map/ppermute | solution.py:491
  196.8 2.1 collective-permute-start.15
  200.4 10.7 %collective-permute-done.16.high_ref = bf16[16,1024]{1,0:T(8,128)(2,1)S(1)} collective-permute-done((bf16[16,1024]{1,0:T(8,128)(2,1)S(1)}, bf16[16,1024]{1,0:T(8,128)(2,1)S(1)}, u32[]{:S(2)}, u32[]{:S(2)}) %collective-permute-start.16) | collective-permute-done | bytes 32800 | tf_op jit(solution)/shard_map/ppermute | solution.py:491
  211.1 3.4 %conv_down.1 = bf16[128,1024]{1,0:T(8,128)(2,1)} custom-call(bf16[16,1024]{1,0:T(8,128)(2,1)S(1)} %collective-permute-done.15.low_ref, bf16[128,1024]{1,0:T(8,128)(2,1)S(1)} %get-tuple-element.105.back_ref, bf16[16,1024]{1,0:T(8,128)(2,1)S(1)} %collective-permute-done.16.high_ref, f32[31,1024]{1,0:T(8,128)S(1)} %copy-done.16, ...), custom_call_target="tpu_custom_call" | custom-call | flops 1 | bytes 1 | tf_op jit(solution)/shard_map/conv_down/pallas_call | solution.py:389
  214.6 4.2 %place_halves.3 = (f32[4,1024,256]{2,1,0:T(8,128)}, f32[4,256,1024]{2,1,0:T(8,128)}) custom-call(s32[4]{0:T(128)S(1)} %and_select_fusion.spots_ref.spot_ref, bf16[1024,512]{1,0:T(8,128)(2,1)} %collective-permute-done.18.refs_0_.refs_3_, bf16[1024,512]{1,0:T(8,128)(2,1)S(1)} %collective-permute-done.17.refs_1_.refs_2_, ...), custom_call_target="tpu_custom_call", output_to_operand_aliasing={{0}: (5, {}), {1}: (6, {})} | custom-call | flops 1 | bytes 1 | tf_op jit(solution)/shard_map/place_halves/pallas_call | solution.py:460
  (86 shorter events, 28.4 us)
Async XLA Ops:
  3.8 43.1 %copy-start.25 = (s32[1,128,2]{1,2,0:T(2,128)S(1)}, s32[1,128,2]{1,2,0:T(2,128)}, u32[]{:S(2)}) copy-start(s32[1,128,2]{1,2,0:T(2,128)} %param.9) | copy-start | bytes 3076
  3.8 43.2 %copy-start.26 = (f32[1,128,2]{1,2,0:T(2,128)S(1)}, f32[1,128,2]{1,2,0:T(2,128)}, u32[]{:S(2)}) copy-start(f32[1,128,2]{1,2,0:T(2,128)} %param.10) | copy-start | bytes 3076
  3.8 43.3 %copy-start.10 = (bf16[1,128,1024]{2,1,0:T(8,128)(2,1)S(1)}, bf16[1,128,1024]{2,1,0:T(8,128)(2,1)}, u32[]{:S(2)}) copy-start(bf16[1,128,1024]{2,1,0:T(8,128)(2,1)} %param.13) | copy-start | bytes 786436
  6.2 120.8 %copy-start = (bf16[1024,512]{1,0:T(8,128)(2,1)}, bf16[1024,512]{1,0:T(8,128)(2,1)S(1)}, u32[]{:S(2)}) copy-start(bf16[1024,512]{1,0:T(8,128)(2,1)S(1)} %get-tuple-element.71.refs_3_.refs_8_) | copy-start | bytes 3145732
  6.3 50.0 %collective-permute-start.4 = (bf16[1024,512]{1,0:T(8,128)(2,1)}, bf16[1024,512]{1,0:T(8,128)(2,1)S(1)}, u32[]{:S(2)}, u32[]{:S(2)}) collective-permute-start(bf16[1024,512]{1,0:T(8,128)(2,1)} %get-tuple-element.65), channel_id=1, source_target_pairs={{0,32},{32,64},{64,96},{96,0},{1,33},{33,65},{65,97},{97,1},{2,34}... | collective-permute-start | bytes 3145736 | tf_op jit(solution)/shard_map/ppermute | solution.py:497
  7.6 48.7 %collective-permute-start.5 = (bf16[1024,512]{1,0:T(8,128)(2,1)}, bf16[1024,512]{1,0:T(8,128)(2,1)S(1)}, u32[]{:S(2)}, u32[]{:S(2)}) collective-permute-start(bf16[1024,512]{1,0:T(8,128)(2,1)} %get-tuple-element.66), channel_id=1, source_target_pairs={{0,96},{32,0},{64,32},{96,64},{1,97},{33,1},{65,33},{97,65},{2,98}... | collective-permute-start | bytes 3145736 | tf_op jit(solution)/shard_map/ppermute | solution.py:497
  9.1 47.1 %collective-permute-start.2 = (bf16[512,512]{1,0:T(8,128)(2,1)}, bf16[512,512]{1,0:T(8,128)(2,1)}, u32[]{:S(2)}, u32[]{:S(2)}) collective-permute-start(bf16[512,512]{1,0:T(8,128)(2,1)} %get-tuple-element.63), channel_id=1, source_target_pairs={{0,32},{32,64},{64,96},{96,0},{1,33},{33,65},{65,97},{97,1},{2,34}... | collective-permute-start | bytes 1572872 | tf_op jit(solution)/shard_map/ppermute | solution.py:497
  9.1 47.1 %collective-permute-start.3 = (bf16[512,512]{1,0:T(8,128)(2,1)}, bf16[512,512]{1,0:T(8,128)(2,1)}, u32[]{:S(2)}, u32[]{:S(2)}) collective-permute-start(bf16[512,512]{1,0:T(8,128)(2,1)} %get-tuple-element.64), channel_id=1, source_target_pairs={{0,96},{32,0},{64,32},{96,64},{1,97},{33,1},{65,33},{97,65},{2,98}... | collective-permute-start | bytes 1572872 | tf_op jit(solution)/shard_map/ppermute | solution.py:497
  13.2 31.1 %collective-permute-start.1 = (bf16[16,1024]{1,0:T(8,128)(2,1)S(1)}, bf16[16,1024]{1,0:T(8,128)(2,1)S(1)}, u32[]{:S(2)}, u32[]{:S(2)}) collective-permute-start(bf16[16,1024]{1,0:T(8,128)(2,1)S(1)} %get-tuple-element.122), channel_id=1, source_target_pairs={{16,0},{32,16},{48,32},{64,48},{80,64},{96,80},{112,96},{17,1},{33... | collective-permute-start | bytes 98312 | tf_op jit(solution)/shard_map/ppermute | solution.py:491
  45.0 4.3 %collective-permute-start = (bf16[16,1024]{1,0:T(8,128)(2,1)}, bf16[16,1024]{1,0:T(8,128)(2,1)}, u32[]{:S(2)}, u32[]{:S(2)}) collective-permute-start(bf16[16,1024]{1,0:T(8,128)(2,1)} %get-tuple-element.123), channel_id=1, source_target_pairs={{0,16},{16,32},{32,48},{48,64},{64,80},{80,96},{96,112},{1,17},{17... | collective-permute-start | bytes 98312 | tf_op jit(solution)/shard_map/ppermute | solution.py:490
  47.1 2.2 copy-start.15
  56.3 62.6 %copy-start.1 = (bf16[1024,512]{1,0:T(8,128)(2,1)}, bf16[1024,512]{1,0:T(8,128)(2,1)S(1)}, u32[]{:S(2)}) copy-start(bf16[1024,512]{1,0:T(8,128)(2,1)S(1)} %collective-permute-done.4.refs_3_.refs_11_) | copy-start | bytes 3145732
  56.3 66.7 %copy-start.2 = (bf16[1024,512]{1,0:T(8,128)(2,1)}, bf16[1024,512]{1,0:T(8,128)(2,1)S(1)}, u32[]{:S(2)}) copy-start(bf16[1024,512]{1,0:T(8,128)(2,1)S(1)} %collective-permute-done.5.refs_3_.refs_12_) | copy-start | bytes 3145732
  56.3 49.1 %all-to-all-start = ((bf16[64,8,2048]{2,1,0:T(8,128)(2,1)}), bf16[64,8,2048]{2,1,0:T(8,128)(2,1)}, u32[]{:S(2)}, u32[]{:S(2)}) async-start(bf16[64,8,2048]{2,1,0:T(8,128)(2,1)} %bitcast.6), calls=%async_computation | async-start | bytes 4194304 | tf_op jit(solution)/shard_map/all_to_all | solution.py:506
  67.1 36.7 %collective-permute-start.6 = (bf16[512,512]{1,0:T(8,128)(2,1)}, bf16[512,512]{1,0:T(8,128)(2,1)S(1)}, u32[]{:S(2)}, u32[]{:S(2)}) collective-permute-start(bf16[512,512]{1,0:T(8,128)(2,1)} %collective-permute-done.2), channel_id=1, source_target_pairs={{0,32},{32,64},{64,96},{96,0},{1,33},{33,65},{65,97},{97,1},{2,34}... | collective-permute-start | bytes 1572872 | tf_op jit(solution)/shard_map/ppermute | solution.py:497
  68.4 36.2 %collective-permute-start.7 = (bf16[512,512]{1,0:T(8,128)(2,1)}, bf16[512,512]{1,0:T(8,128)(2,1)S(1)}, u32[]{:S(2)}, u32[]{:S(2)}) collective-permute-start(bf16[512,512]{1,0:T(8,128)(2,1)} %collective-permute-done.3), channel_id=1, source_target_pairs={{0,96},{32,0},{64,32},{96,64},{1,97},{33,1},{65,33},{97,65},{2,98}... | collective-permute-start | bytes 1572872 | tf_op jit(solution)/shard_map/ppermute | solution.py:497
  105.4 6.7 %copy-start.4 = (bf16[512,512]{1,0:T(8,128)(2,1)S(1)}, bf16[512,512]{1,0:T(8,128)(2,1)}, u32[]{:S(2)}) copy-start(bf16[512,512]{1,0:T(8,128)(2,1)} %copy-done.3) | copy-start | bytes 1572868
  105.4 6.7 %copy-start.6 = (bf16[512,512]{1,0:T(8,128)(2,1)S(1)}, bf16[512,512]{1,0:T(8,128)(2,1)}, u32[]{:S(2)}) copy-start(bf16[512,512]{1,0:T(8,128)(2,1)} %copy-done.5) | copy-start | bytes 1572868
  107.3 3.3 %collective-permute-start.9 = (bf16[256,2048]{1,0:T(8,128)(2,1)S(1)}, bf16[256,2048]{1,0:T(8,128)(2,1)S(1)}, u32[]{:S(2)}, u32[]{:S(2)}) collective-permute-start(bf16[256,2048]{1,0:T(8,128)(2,1)S(1)} %get-tuple-element.118), channel_id=1, source_target_pairs={{0,16},{16,0},{1,17},{17,1},{2,18},{18,2},{3,19},{19,3},{4,20},{20... | collective-permute-start | bytes 3145736 | tf_op jit(solution)/shard_map/ppermute | solution.py:501
  108.3 3.8 %collective-permute-start.8 = (bf16[256,2048]{1,0:T(8,128)(2,1)S(1)}, bf16[256,2048]{1,0:T(8,128)(2,1)S(1)}, u32[]{:S(2)}, u32[]{:S(2)}) collective-permute-start(bf16[256,2048]{1,0:T(8,128)(2,1)S(1)} %get-tuple-element.119), channel_id=1, source_target_pairs={{0,16},{16,0},{1,17},{17,1},{2,18},{18,2},{3,19},{19,3},{4,20},{20... | collective-permute-start | bytes 3145736 | tf_op jit(solution)/shard_map/ppermute | solution.py:501
  116.1 16.2 %collective-permute-start.10 = (bf16[512,512]{1,0:T(8,128)(2,1)S(1)}, bf16[512,512]{1,0:T(8,128)(2,1)S(1)}, u32[]{:S(2)}, u32[]{:S(2)}) collective-permute-start(bf16[512,512]{1,0:T(8,128)(2,1)S(1)} %get-tuple-element.83), channel_id=1, source_target_pairs={{0,32},{32,64},{64,96},{96,0},{1,33},{33,65},{65,97},{97,1},{2,34}... | collective-permute-start | bytes 1572872 | tf_op jit(solution)/shard_map/ppermute | solution.py:497
  116.2 16.1 %collective-permute-start.11 = (bf16[512,512]{1,0:T(8,128)(2,1)S(1)}, bf16[512,512]{1,0:T(8,128)(2,1)S(1)}, u32[]{:S(2)}, u32[]{:S(2)}) collective-permute-start(bf16[512,512]{1,0:T(8,128)(2,1)S(1)} %get-tuple-element.84), channel_id=1, source_target_pairs={{0,96},{32,0},{64,32},{96,64},{1,97},{33,1},{65,33},{97,65},{2,98}... | collective-permute-start | bytes 1572872 | tf_op jit(solution)/shard_map/ppermute | solution.py:497
  137.9 4.9 %collective-permute-start.12 = (bf16[512,2048]{1,0:T(8,128)(2,1)}, bf16[512,2048]{1,0:T(8,128)(2,1)S(1)}, u32[]{:S(2)}, u32[]{:S(2)}) collective-permute-start(bf16[512,2048]{1,0:T(8,128)(2,1)} %back_to_width.2), channel_id=1, source_target_pairs={{0,16},{16,0},{1,17},{17,1},{2,18},{18,2},{3,19},{19,3},{4,20},{20... | collective-permute-start | bytes 6291464 | tf_op jit(solution)/shard_map/ppermute | solution.py:501
  138.8 13.6 %collective-permute-start.13 = (bf16[512,512]{1,0:T(8,128)(2,1)S(1)}, bf16[512,512]{1,0:T(8,128)(2,1)S(1)}, u32[]{:S(2)}, u32[]{:S(2)}) collective-permute-start(bf16[512,512]{1,0:T(8,128)(2,1)S(1)} %get-tuple-element.90), channel_id=1, source_target_pairs={{0,96},{32,0},{64,32},{96,64},{1,97},{33,1},{65,33},{97,65},{2,98}... | collective-permute-start | bytes 1572872 | tf_op jit(solution)/shard_map/ppermute | solution.py:497
  140.0 14.4 %collective-permute-start.14 = (bf16[512,512]{1,0:T(8,128)(2,1)S(1)}, bf16[512,512]{1,0:T(8,128)(2,1)S(1)}, u32[]{:S(2)}, u32[]{:S(2)}) collective-permute-start(bf16[512,512]{1,0:T(8,128)(2,1)S(1)} %get-tuple-element.91), channel_id=1, source_target_pairs={{0,32},{32,64},{64,96},{96,0},{1,33},{33,65},{65,97},{97,1},{2,34}... | collective-permute-start | bytes 1572872 | tf_op jit(solution)/shard_map/ppermute | solution.py:497
  155.2 36.1 %all-to-all-start.1 = ((bf16[64,8,2048]{2,1,0:T(8,128)(2,1)}), bf16[64,8,2048]{2,1,0:T(8,128)(2,1)S(1)}, u32[]{:S(2)}, u32[]{:S(2)}) async-start(bf16[64,8,2048]{2,1,0:T(8,128)(2,1)} %bitcast.25), calls=%async_computation.1 | async-start | bytes 4194304 | tf_op jit(solution)/shard_map/all_to_all | solution.py:506
  163.3 51.3 %collective-permute-start.17 = (bf16[1024,512]{1,0:T(8,128)(2,1)}, bf16[1024,512]{1,0:T(8,128)(2,1)S(1)}, u32[]{:S(2)}, u32[]{:S(2)}) collective-permute-start(bf16[1024,512]{1,0:T(8,128)(2,1)} %get-tuple-element.108), channel_id=1, source_target_pairs={{0,32},{32,64},{64,96},{96,0},{1,33},{33,65},{65,97},{97,1},{2,34}... | collective-permute-start | bytes 3145736 | tf_op jit(solution)/shard_map/ppermute | solution.py:497
  164.6 50.0 %collective-permute-start.18 = (bf16[1024,512]{1,0:T(8,128)(2,1)}, bf16[1024,512]{1,0:T(8,128)(2,1)}, u32[]{:S(2)}, u32[]{:S(2)}) collective-permute-start(bf16[1024,512]{1,0:T(8,128)(2,1)} %get-tuple-element.109), channel_id=1, source_target_pairs={{0,96},{32,0},{64,32},{96,64},{1,97},{33,1},{65,33},{97,65},{2,98}... | collective-permute-start | bytes 3145736 | tf_op jit(solution)/shard_map/ppermute | solution.py:497
  192.3 6.6 %copy-start.21 = (bf16[128,1024]{1,0:T(8,128)(2,1)S(1)}, bf16[128,1024]{1,0:T(8,128)(2,1)}, u32[]{:S(2)}) copy-start(bf16[128,1024]{1,0:T(8,128)(2,1)} %copy-done.20) | copy-start | bytes 786436
  193.1 18.1 %copy-start.16 = (f32[31,1024]{1,0:T(8,128)S(1)}, f32[31,1024]{1,0:T(8,128)}, u32[]{:S(2)}) copy-start(f32[31,1024]{1,0:T(8,128)} %kernel_ref.3) | copy-start | bytes 380932
  193.1 18.0 %collective-permute-start.16 = (bf16[16,1024]{1,0:T(8,128)(2,1)S(1)}, bf16[16,1024]{1,0:T(8,128)(2,1)S(1)}, u32[]{:S(2)}, u32[]{:S(2)}) collective-permute-start(bf16[16,1024]{1,0:T(8,128)(2,1)S(1)} %get-tuple-element.120), channel_id=1, source_target_pairs={{16,0},{32,16},{48,32},{64,48},{80,64},{96,80},{112,96},{17,1},{33... | collective-permute-start | bytes 98312 | tf_op jit(solution)/shard_map/ppermute | solution.py:491
  196.8 14.3 %collective-permute-start.15 = (bf16[16,1024]{1,0:T(8,128)(2,1)S(1)}, bf16[16,1024]{1,0:T(8,128)(2,1)S(1)}, u32[]{:S(2)}, u32[]{:S(2)}) collective-permute-start(bf16[16,1024]{1,0:T(8,128)(2,1)S(1)} %get-tuple-element.121), channel_id=1, source_target_pairs={{0,16},{16,32},{32,48},{48,64},{64,80},{80,96},{96,112},{1,17},{17... | collective-permute-start | bytes 98312 | tf_op jit(solution)/shard_map/ppermute | solution.py:490
  (16 other events, 19.9 us)
